TPU v7x, 512 devices: a whole 4x8x8 slice. The times are simulated.
512 devices in a mesh: blk: 32 (over x_hi, z, core), pair: 16 (over y, x_lo).
Axes of the slice: x: 4 (x_hi: 2, x_lo: 2; x = x_hi * 2 + x_lo), y: 8, z: 8, core: 2. Of those that a mesh axis runs over, the one named last changes fastest.
Arguments:
- first_feat: bfloat16 [32, 30720, 128], P('pair', 'blk'), parts along dimension 0, may hold values from -8 to 8
- second_feat: bfloat16 [32, 30720, 128], P('pair', 'blk'), parts along dimension 0, may hold values from -8 to 8
- conv_weight: float32 [4, 4, 3, 3], replicated, may hold values from -1 to 1
- conv_bias: float32 [4], replicated, may hold values from -0.5 to 0.5
Outputs:
- refined: float32 [32, 4, 64, 480], P('pair', None, 'blk'), parts along dimension 0
There are 16 independent parts, one for each index of `pair`. A program takes and returns all parts, laid end to end along the dimension named above; an argument that names none is the same for every part. Nothing has to cross between parts.
All inputs are finite; a program needn't handle non-finite values.
Results may differ from a plain program's by a relative error of at most 0.0003.
Values may be sent and summed in bfloat16 or wider, within the bound.
No kernel may reach another device: no remote copies, remote signals or barrier semaphores. Data moves between devices by JAX's collectives and lax.ppermute only.
A program may use at most 128 MiB of HBM per device.

v0:
```python
import math

import jax
import jax.numpy as jnp
from jax import lax
from jax.sharding import PartitionSpec as P

W = 480


def padded(x, sides, width):
    for axis, dim in sides:
        size, length = (lax.axis_size(axis), x.shape[dim])
        up = [(i, (i + 1) % size) for i in range(size - 1)]
        down = [(j, i) for i, j in up]
        last = lax.slice_in_dim(x, length - width, length, axis=dim)
        initial = lax.slice_in_dim(x, 0, width, axis=dim)
        before = lax.ppermute(last, axis, up)
        after = lax.ppermute(initial, axis, down)
        x = jnp.concatenate([before, x, after], axis=dim)
    return x


def coordinates(position, height):
    row_index = (position // W).astype(jnp.float32)
    col_index = (position % W).astype(jnp.float32)
    return ((2.0 * col_index + 1.0) / W - 1.0, (2.0 * row_index + 1.0) / height - 1.0)


def piece_count(length):
    count = 1
    while length % count != 0 or length // count > 1024:
        count += 1
    return count


def block_scores(query_rows, key_rows, inverse_root):
    products = lax.dot_general(
        query_rows, key_rows, (((1,), (1,)), ((), ())), preferred_element_type=jnp.float32
    )
    return products * inverse_root


def absorb(status, scores, values_x, values_y, axis):
    running_max, running_sum, moment_x, moment_y = status
    block_max = jnp.max(scores, axis=axis)
    updated = jnp.maximum(running_max, block_max)
    retain = jnp.exp(running_max - updated)
    weights = jnp.exp(scores - jnp.expand_dims(updated, axis))
    spread_x = jnp.expand_dims(values_x, 1 - axis)
    spread_y = jnp.expand_dims(values_y, 1 - axis)
    return (
        updated,
        running_sum * retain + jnp.sum(weights, axis=axis),
        moment_x * retain + jnp.sum(weights * spread_x, axis=axis),
        moment_y * retain + jnp.sum(weights * spread_y, axis=axis),
    )


def empty_status(length):
    zeros = jnp.zeros((length,), jnp.float32)
    return (jnp.full((length,), -jnp.inf, jnp.float32), zeros, zeros, zeros)


def keep_if(flag, updated, previous):
    return tuple((jnp.where(flag, fresh, older) for fresh, older in zip(updated, previous)))


def join_parts(statuses):
    return tuple((jnp.concatenate([status[member] for status in statuses]) for member in range(4)))


def stack_frames(statuses):
    return tuple((jnp.stack([status[member] for status in statuses]) for member in range(4)))


def on_device(first_feat, second_feat, conv_weight, conv_bias):
    frame_count, local_pixels, channels = first_feat.shape
    cycle_size = lax.axis_size("blk")
    position = lax.axis_index("blk")
    rows_here = local_pixels // W
    height = rows_here * cycle_size
    inverse_root = 1.0 / math.sqrt(channels)
    pieces = piece_count(local_pixels)
    span = local_pixels // pieces
    tile_start = position * local_pixels
    own_x, own_y = coordinates(tile_start + jnp.arange(local_pixels, dtype=jnp.int32), height)
    neighbours = (0, -1, 1)
    present = {-1: position > 0, 1: position < cycle_size - 1}

    def key_coords(neighbour, key_piece):
        begin = tile_start + neighbour * local_pixels + key_piece * span
        return coordinates(begin + jnp.arange(span, dtype=jnp.int32), height)

    def key_block(band, neighbour, key_piece):
        begin = (neighbour + 1) * local_pixels + key_piece * span
        return band[begin : begin + span]

    def match_rows(queries, band):
        status = empty_status(span)
        for neighbour in neighbours:
            key_x, key_y = key_coords(neighbour, 0)
            scores = block_scores(queries, key_block(band, neighbour, 0), inverse_root)
            updated = absorb(status, scores, key_x, key_y, 1)
            status = updated if neighbour == 0 else keep_if(present[neighbour], updated, status)
        results = [status]
        return join_parts(results)

    stacked = jnp.stack([first_feat, second_feat])
    band = padded(stacked, (("blk", 2),), local_pixels)
    forward_list = []
    backward_list = []
    for frame in range(frame_count):
        forward_list.append(match_rows(first_feat[frame], band[1, frame]))
        backward_list.append(match_rows(second_feat[frame], band[0, frame]))
    forward = stack_frames(forward_list)
    backward = stack_frames(backward_list)
    back_sum, back_x, back_y = (backward[1], backward[2], backward[3])
    flow = jnp.stack(
        [
            forward[2] / forward[1] - own_x,
            forward[3] / forward[1] - own_y,
            back_x / back_sum - own_x,
            back_y / back_sum - own_y,
        ],
        axis=1,
    )
    flow = flow.reshape(frame_count, 4, rows_here, W)
    extended = padded(flow, (("blk", 2),), 1)
    extended = jnp.pad(extended, ((0, 0), (0, 0), (0, 0), (1, 1)))
    mixture = jnp.zeros_like(flow)
    for row_tap in range(3):
        for col_tap in range(3):
            window = extended[:, :, row_tap : row_tap + rows_here, col_tap : col_tap + W]
            mixture = mixture + jnp.einsum(
                "oi,firc->forc",
                conv_weight[:, :, row_tap, col_tap],
                window,
                precision=lax.Precision.HIGHEST,
            )
    return flow + mixture + conv_bias[None, :, None, None]


def solution(mesh):
    placed = (P("pair", "blk", None), P("pair", "blk", None), P(), P())
    return jax.shard_map(
        on_device,
        mesh=mesh,
        in_specs=placed,
        out_specs=P("pair", None, "blk", None),
        check_vma=False,
    )
```

profile of v0, /device:TPU:38, one launch (start us, length us, event | category | flops | bytes accessed | tf_op | source)
XLA Modules:
  0.0 93.9 jit_solution(3406794874186186657)
XLA Ops:
  0.0 2.3 %pad_maximum_fusion = bf16[2,2,960,128]{3,2,1,0:T(8,128)(2,1)} fusion(bf16[1,2,960,128]{3,2,1,0:T(8,128)(2,1)} %bitcast.202, bf16[1,2,960,128]{3,2,1,0:T(8,128)(2,1)} %bitcast.199), kind=kLoop, calls=%fused_computation.71 | loop fusion | flops 491520 | bytes 1966080 | tf_op jit(solution)/shard_map/stack | solution.py:109
  2.3 11.2 %collective-permute-start.1 = (bf16[2,2,960,128]{3,2,1,0:T(8,128)(2,1)}, bf16[2,2,960,128]{3,2,1,0:T(8,128)(2,1)S(1)}, u32[]{:S(2)}, u32[]{:S(2)}) collective-permute-start(bf16[2,2,960,128]{3,2,1,0:T(8,128)(2,1)} %pad_maximum_fusion), channel_id=1, source_target_pairs={{16,0},{32,16},{48,32},{64,48},{80,64},{96,80},{112,96},{128,112},... | collective-permute-start | bytes 2949128 | tf_op jit(solution)/shard_map/ppermute | solution.py:19
  13.6 1.9 %collective-permute-start = (bf16[2,2,960,128]{3,2,1,0:T(8,128)(2,1)}, bf16[2,2,960,128]{3,2,1,0:T(8,128)(2,1)S(1)}, u32[]{:S(2)}, u32[]{:S(2)}) collective-permute-start(bf16[2,2,960,128]{3,2,1,0:T(8,128)(2,1)} %pad_maximum_fusion), channel_id=1, source_target_pairs={{0,16},{16,32},{32,48},{48,64},{64,80},{80,96},{96,112},{112,128},... | collective-permute-start | bytes 2949128 | tf_op jit(solution)/shard_map/ppermute | solution.py:18
  15.5 3.7 %multiply_reduce_fusion.29 = (f32[960]{0:T(1024)S(1)}, f32[960,960]{0,1:T(8,128)}) fusion(bf16[1,2,960,128]{3,2,1,0:T(8,128)(2,1)} %bitcast.200, bf16[2,960,128]{2,1,0:T(8,128)(2,1)} %param.5), kind=kOutput, calls=%fused_computation.41 | convolution fusion | flops 237771840 | bytes 4181760 | tf_op jit(solution)/shard_map/dot_general | solution.py:38
  19.2 2.7 %multiply_reduce_fusion.32 = (f32[960]{0:T(1024)S(1)}, f32[960,960]{0,1:T(8,128)}) fusion(bf16[1,2,960,128]{3,2,1,0:T(8,128)(2,1)S(1)} %bitcast.203, bf16[2,960,128]{2,1,0:T(8,128)(2,1)S(1)} %copy-done), kind=kOutput, calls=%fused_computation.44 | convolution fusion | flops 237771840 | bytes 4181760 | tf_op jit(solution)/shard_map/dot_general | solution.py:38
  21.9 2.6 %multiply_reduce_fusion.35 = (f32[960]{0:T(1024)S(1)}, f32[960,960]{0,1:T(8,128)}) fusion(bf16[1,2,960,128]{3,2,1,0:T(8,128)(2,1)S(1)} %bitcast.204, bf16[2,960,128]{2,1,0:T(8,128)(2,1)S(1)} %copy-done), kind=kOutput, calls=%fused_computation.47 | convolution fusion | flops 237771840 | bytes 4181760 | tf_op jit(solution)/shard_map/dot_general | solution.py:38
  24.4 2.6 %multiply_reduce_fusion.26 = (f32[960]{0:T(1024)S(1)}, f32[960,960]{0,1:T(8,128)}) fusion(bf16[1,2,960,128]{3,2,1,0:T(8,128)(2,1)S(1)} %bitcast.201, bf16[2,960,128]{2,1,0:T(8,128)(2,1)S(1)} %copy-done.1), kind=kOutput, calls=%fused_computation.38 | convolution fusion | flops 237771840 | bytes 4181760 | tf_op jit(solution)/shard_map/dot_general | solution.py:38
  27.0 8.7 %multiply_reduce_fusion.8 = (f32[960]{0:T(1024)S(1)}, f32[960]{0:T(1024)S(1)}, f32[960]{0:T(1024)S(1)}, f32[960]{0:T(1024)S(1)}, f32[960]{0:T(1024)S(1)}, /*inde...) fusion(f32[960,960]{0,1:T(8,128)} %get-tuple-element.103, ...), kind=kLoop, calls=%fused_computation.10 | loop fusion | flops 25793280 | bytes 14814720 | tf_op jit(solution)/shard_map/reduce_sum | solution.py:55
  35.8 0.1 reduce_max.133
  35.8 0.1 reduce_max.139
  35.9 0.1 reduce_max.145
  36.0 0.1 reduce_max.151
  36.1 0.1 reduce_sum.397
  36.2 0.1 reduce_sum.403
  36.2 0.1 reduce_sum.409
  36.3 0.1 reduce_sum.421
  36.4 0.1 reduce_sum.415
  36.5 0.1 reduce_sum.427
  36.6 0.1 reduce_sum.433
  36.6 0.1 reduce_sum.439
  36.7 0.1 reduce_sum.445
  36.8 0.1 reduce_sum.457
  36.9 0.1 reduce_sum.451
  36.9 0.1 reduce_sum.463
  37.2 2.7 %multiply_reduce_fusion.34 = (f32[960]{0:T(1024)S(1)}, f32[960,960]{0,1:T(8,128)}) fusion(bf16[2,960,128]{2,1,0:T(8,128)(2,1)S(1)} %copy-done, bf16[2,2,960,128]{3,2,1,0:T(8,128)(2,1)S(1)} %collective-permute-done), kind=kOutput, calls=%fused_computation.46 | convolution fusion | flops 237771840 | bytes 4181760 | tf_op jit(solution)/shard_map/dot_general | solution.py:38
  39.8 0.1 reduce_max.135
  39.9 2.6 %multiply_reduce_fusion.33 = (f32[960]{0:T(1024)S(1)}, f32[960,960]{0,1:T(8,128)}) fusion(bf16[2,960,128]{2,1,0:T(8,128)(2,1)S(1)} %copy-done, bf16[2,2,960,128]{3,2,1,0:T(8,128)(2,1)S(1)} %collective-permute-done.1), kind=kOutput, calls=%fused_computation.45 | convolution fusion | flops 237771840 | bytes 4181760 | tf_op jit(solution)/shard_map/dot_general | solution.py:38
  42.5 0.1 reduce_max.137
  42.5 2.6 %multiply_reduce_fusion.31 = (f32[960]{0:T(1024)S(1)}, f32[960,960]{0,1:T(8,128)}) fusion(bf16[2,960,128]{2,1,0:T(8,128)(2,1)S(1)} %copy-done, bf16[2,2,960,128]{3,2,1,0:T(8,128)(2,1)S(1)} %collective-permute-done), kind=kOutput, calls=%fused_computation.43 | convolution fusion | flops 237771840 | bytes 4181760 | tf_op jit(solution)/shard_map/dot_general | solution.py:38
  45.1 0.1 reduce_max.141
  45.2 2.6 %multiply_reduce_fusion.30 = (f32[960]{0:T(1024)S(1)}, f32[960,960]{0,1:T(8,128)}) fusion(bf16[2,960,128]{2,1,0:T(8,128)(2,1)S(1)} %copy-done, bf16[2,2,960,128]{3,2,1,0:T(8,128)(2,1)S(1)} %collective-permute-done.1), kind=kOutput, calls=%fused_computation.42 | convolution fusion | flops 237771840 | bytes 4181760 | tf_op jit(solution)/shard_map/dot_general | solution.py:38
  47.8 0.1 reduce_max.143
  47.9 2.6 %multiply_reduce_fusion.28 = (f32[960]{0:T(1024)S(1)}, f32[960,960]{0,1:T(8,128)}) fusion(bf16[2,960,128]{2,1,0:T(8,128)(2,1)S(1)} %copy-done.1, bf16[2,2,960,128]{3,2,1,0:T(8,128)(2,1)S(1)} %collective-permute-done), kind=kOutput, calls=%fused_computation.40 | convolution fusion | flops 237771840 | bytes 4181760 | tf_op jit(solution)/shard_map/dot_general | solution.py:38
  50.5 0.1 reduce_max.147
  50.6 2.6 %multiply_reduce_fusion.27 = (f32[960]{0:T(1024)S(1)}, f32[960,960]{0,1:T(8,128)}) fusion(bf16[2,960,128]{2,1,0:T(8,128)(2,1)S(1)} %copy-done.1, bf16[2,2,960,128]{3,2,1,0:T(8,128)(2,1)S(1)} %collective-permute-done.1), kind=kOutput, calls=%fused_computation.39 | convolution fusion | flops 237771840 | bytes 4181760 | tf_op jit(solution)/shard_map/dot_general | solution.py:38
  53.2 0.1 reduce_max.149
  53.3 2.7 %multiply_reduce_fusion.25 = (f32[960]{0:T(1024)S(1)}, f32[960,960]{0,1:T(8,128)}) fusion(bf16[2,960,128]{2,1,0:T(8,128)(2,1)S(1)} %copy-done.1, bf16[2,2,960,128]{3,2,1,0:T(8,128)(2,1)S(1)} %collective-permute-done), kind=kOutput, calls=%fused_computation.37 | convolution fusion | flops 237771840 | bytes 4181760 | tf_op jit(solution)/shard_map/dot_general | solution.py:38
  56.0 0.1 reduce_max.153
  56.1 2.6 %multiply_reduce_fusion.24 = (f32[960]{0:T(1024)S(1)}, f32[960,960]{0,1:T(8,128)}) fusion(bf16[2,960,128]{2,1,0:T(8,128)(2,1)S(1)} %copy-done.1, bf16[2,2,960,128]{3,2,1,0:T(8,128)(2,1)S(1)} %collective-permute-done.1), kind=kOutput, calls=%fused_computation.36 | convolution fusion | flops 237771840 | bytes 4181760 | tf_op jit(solution)/shard_map/dot_general | solution.py:38
  58.6 0.1 reduce_max.155
  58.7 9.7 %multiply_reduce_fusion.7 = (f32[960]{0:T(1024)S(1)}, f32[960]{0:T(1024)S(1)}, f32[960]{0:T(1024)S(1)}, f32[960]{0:T(1024)S(1)}, f32[960]{0:T(1024)S(1)}, /*inde...) fusion(f32[960,960]{0,1:T(8,128)} %get-tuple-element.105, ...), kind=kLoop, calls=%fused_computation.8 | loop fusion | flops 25793280 | bytes 14814720 | tf_op jit(solution)/shard_map/reduce_sum | solution.py:55
  68.4 0.1 reduce_sum.399
  68.4 0.1 reduce_sum.405
  68.5 9.6 %multiply_reduce_fusion.6 = (f32[960]{0:T(1024)S(1)}, f32[960]{0:T(1024)S(1)}, f32[960]{0:T(1024)S(1)}, f32[960]{0:T(1024)S(1)}, f32[960]{0:T(1024)S(1)}, /*inde...) fusion(f32[960,960]{0,1:T(8,128)} %get-tuple-element.101, ...), kind=kLoop, calls=%fused_computation.6 | loop fusion | flops 25793280 | bytes 14814720 | tf_op jit(solution)/shard_map/reduce_sum | solution.py:55
  78.2 0.1 reduce_sum.401
  78.2 0.1 reduce_sum.407
  78.3 0.1 reduce_sum.411
  78.4 0.1 reduce_sum.423
  78.5 0.1 reduce_sum.413
  78.8 0.1 reduce_sum.419
  80.4 1.9 %collective-permute-start.2 = (f32[2,4,1,480]{3,1,2,0:T(4,128)S(1)}, f32[2,4,1,480]{3,1,2,0:T(4,128)S(1)}, u32[]{:S(2)}, u32[]{:S(2)}) collective-permute-start(f32[2,4,1,480]{3,1,2,0:T(4,128)S(1)} %get-tuple-element.84), channel_id=1, source_target_pairs={{0,16},{16,32},{32,48},{48,64},{64,80},{80,96},{96,112},{112,128},... | collective-permute-start | bytes 46088 | tf_op jit(solution)/shard_map/ppermute | solution.py:18
  82.3 7.3 %collective-permute-start.3 = (f32[2,4,1,480]{3,1,2,0:T(4,128)S(1)}, f32[2,4,1,480]{3,1,2,0:T(4,128)S(1)}, u32[]{:S(2)}, u32[]{:S(2)}) collective-permute-start(f32[2,4,1,480]{3,1,2,0:T(4,128)S(1)} %get-tuple-element.85), channel_id=1, source_target_pairs={{16,0},{32,16},{48,32},{64,48},{80,64},{96,80},{112,96},{128,112},... | collective-permute-start | bytes 46088 | tf_op jit(solution)/shard_map/ppermute | solution.py:19
  89.6 1.4 %collective-permute-done.3 = f32[2,4,1,480]{3,1,2,0:T(4,128)S(1)} collective-permute-done((f32[2,4,1,480]{3,1,2,0:T(4,128)S(1)}, f32[2,4,1,480]{3,1,2,0:T(4,128)S(1)}, u32[]{:S(2)}, u32[]{:S(2)}) %collective-permute-start.3) | collective-permute-done | bytes 15392 | tf_op jit(solution)/shard_map/ppermute | solution.py:19
  91.0 0.2 select_maximum_fusion
  91.2 0.3 fusion.72
  91.4 0.2 fusion.53
  91.6 0.2 convolution_add_fusion.6
  91.8 0.3 convolution_add_fusion.5
  92.1 0.2 convolution_add_fusion.4
  92.3 0.2 convolution_add_fusion.3
  92.5 0.3 convolution_add_fusion.2
  92.8 0.2 convolution_add_fusion.1
  93.0 0.2 fusion.15
  93.2 0.6 copy.21
  (50 shorter events, 1.9 us)
Async XLA Ops:
  0.0 19.2 %copy-start.1 = (bf16[2,960,128]{2,1,0:T(8,128)(2,1)S(1)}, bf16[2,960,128]{2,1,0:T(8,128)(2,1)}, u32[]{:S(2)}) copy-start(bf16[2,960,128]{2,1,0:T(8,128)(2,1)} %param.5) | copy-start | bytes 1474564
  0.0 19.2 %copy-start = (bf16[2,960,128]{2,1,0:T(8,128)(2,1)S(1)}, bf16[2,960,128]{2,1,0:T(8,128)(2,1)}, u32[]{:S(2)}) copy-start(bf16[2,960,128]{2,1,0:T(8,128)(2,1)} %param.4) | copy-start | bytes 1474564
  2.3 37.6 %collective-permute-start.1 = (bf16[2,2,960,128]{3,2,1,0:T(8,128)(2,1)}, bf16[2,2,960,128]{3,2,1,0:T(8,128)(2,1)S(1)}, u32[]{:S(2)}, u32[]{:S(2)}) collective-permute-start(bf16[2,2,960,128]{3,2,1,0:T(8,128)(2,1)} %pad_maximum_fusion), channel_id=1, source_target_pairs={{16,0},{32,16},{48,32},{64,48},{80,64},{96,80},{112,96},{128,112},... | collective-permute-start | bytes 2949128 | tf_op jit(solution)/shard_map/ppermute | solution.py:19
  13.6 23.6 %collective-permute-start = (bf16[2,2,960,128]{3,2,1,0:T(8,128)(2,1)}, bf16[2,2,960,128]{3,2,1,0:T(8,128)(2,1)S(1)}, u32[]{:S(2)}, u32[]{:S(2)}) collective-permute-start(bf16[2,2,960,128]{3,2,1,0:T(8,128)(2,1)} %pad_maximum_fusion), channel_id=1, source_target_pairs={{0,16},{16,32},{32,48},{48,64},{64,80},{80,96},{96,112},{112,128},... | collective-permute-start | bytes 2949128 | tf_op jit(solution)/shard_map/ppermute | solution.py:18
  68.5 22.6 %copy-start.2 = (f32[4,4,3,3]{1,0,3,2:T(4,128)S(1)}, f32[4,4,3,3]{1,0,3,2:T(4,128)}, u32[]{:S(2)}) copy-start(f32[4,4,3,3]{1,0,3,2:T(4,128)} %param.6) | copy-start | bytes 1732
  68.5 24.5 %copy-start.3 = (f32[4]{0:T(128)S(1)}, f32[4]{0:T(128)}, u32[]{:S(2)}) copy-start(f32[4]{0:T(128)} %param.7) | copy-start | bytes 52
  80.4 9.2 %collective-permute-start.2 = (f32[2,4,1,480]{3,1,2,0:T(4,128)S(1)}, f32[2,4,1,480]{3,1,2,0:T(4,128)S(1)}, u32[]{:S(2)}, u32[]{:S(2)}) collective-permute-start(f32[2,4,1,480]{3,1,2,0:T(4,128)S(1)} %get-tuple-element.84), channel_id=1, source_target_pairs={{0,16},{16,32},{32,48},{48,64},{64,80},{80,96},{96,112},{112,128},... | collective-permute-start | bytes 46088 | tf_op jit(solution)/shard_map/ppermute | solution.py:18
  82.3 8.7 %collective-permute-start.3 = (f32[2,4,1,480]{3,1,2,0:T(4,128)S(1)}, f32[2,4,1,480]{3,1,2,0:T(4,128)S(1)}, u32[]{:S(2)}, u32[]{:S(2)}) collective-permute-start(f32[2,4,1,480]{3,1,2,0:T(4,128)S(1)} %get-tuple-element.85), channel_id=1, source_target_pairs={{16,0},{32,16},{48,32},{64,48},{80,64},{96,80},{112,96},{128,112},... | collective-permute-start | bytes 46088 | tf_op jit(solution)/shard_map/ppermute | solution.py:19
where the time goes:
time: 94.1 us; the launch traced here: 93.9 us
  matrix products  34.4 us (37%)
  other arithmetic  31.1 us (33%)
  starting transfers between devices  22.3 us (24%)
  local copies, waits for them, and re-layouts  4.42 us (5%)
  waiting for transfers between devices  1.42 us (2%)
    dot_general x12, matrix products, block_scores(): lax.dot_general(query_rows, key_rows, (((1,), (1,)), ((), ())), preferred...  32.4 us
    reduce_sum x3, other arithmetic, absorb(): jnp.sum(weights * spread_x, axis=axis)  28 us
    ppermute x2, starting transfers between devices, padded(): after = lax.ppermute(initial, axis, down)  18.5 us
    ppermute x2, starting transfers between devices, padded(): before = lax.ppermute(last, axis, up)  3.84 us
    another operation x1, other arithmetic, on_device(): stacked = jnp.stack([first_feat, second_feat])  2.33 us
    dot_general x9, matrix products, on_device(): jnp.einsum('oi,firc->forc', conv_weight[:, :, row_tap, col_tap], window,...  2 us
  transfers between devices with their start and end apart: 4, of which 1 were waited for; matrix products, arithmetic and copies ran while one was open for 26% of the time, Pallas kernels for 0%

commit v1 on v0

v1 whole, which is shorter than its diff:
```python
import functools
import math

import jax
import jax.numpy as jnp
from jax import lax
from jax.experimental import pallas as pl
from jax.experimental.pallas import tpu as pltpu
from jax.sharding import PartitionSpec as P


W = 480
TILE = 960
CH = 128
FR = 2
MID = 240.0
SCALE = math.log2(math.e) / math.sqrt(CH)
LOW = 2.0**-60
HIGH = 2.0**100
CHUNKS = ((0, 256), (256, 256), (512, 256), (768, 192))
NT = (((1,), (1,)), ((), ()))
NN = (((1,), (0,)), ((), ()))


def dot(a, b, dims):
    return lax.dot_general(a, b, dims, preferred_element_type=jnp.float32)


def side():
    pos = lax.axis_index("blk")
    even = pos % 2 == 0
    present = jnp.where(even, pos > 0, pos < lax.axis_size("blk") - 1)
    return even, present


def moments():
    lane = lax.broadcasted_iota(jnp.int32, (8, TILE), 1)
    row = lax.broadcasted_iota(jnp.int32, (8, TILE), 0)
    second = (lane >= W).astype(jnp.int32)
    col = lane - W * second - int(MID)
    value = jnp.where(row == 0, 1, jnp.where(row == 1, col, jnp.where(row == 2, second, 0)))
    return value.astype(jnp.float32).astype(jnp.bfloat16)


def split_into(dst, feat):
    scaled = feat.astype(jnp.float32) * SCALE
    hi = scaled.astype(jnp.bfloat16)
    dst[:, :CH] = hi
    dst[:, CH:] = (scaled - hi.astype(jnp.float32)).astype(jnp.bfloat16)


def twice_into(dst, feat):
    dst[:, :CH] = feat
    dst[:, CH:] = feat


def sums(lhs, rhs, mom, down, across=False):
    total = None
    for n0, w in CHUNKS:
        weight = jnp.exp2(dot(lhs[...], rhs[n0 : n0 + w, :], NT)).astype(jnp.bfloat16)
        down(n0, w, dot(mom, weight, NN))
        if across:
            part = dot(mom[:, n0 : n0 + w], weight, NT)
            total = part if total is None else total + part
    return total


def own_kernel(first, second, fwd, bwd, fs, ss):
    mom = moments()

    def frame(f, _):
        split_into(fs, first[f])
        twice_into(ss, second[f])

        def down(n0, w, part):
            fwd[f, :, n0 : n0 + w] = part

        bwd[f] = sums(ss, fs, mom, down, across=True)
        return 0

    lax.fori_loop(0, FR, frame, 0)


def shift_y(part, offset):
    row = lax.broadcasted_iota(jnp.int32, part.shape, 0)
    return part + jnp.where(row == 2, offset * part[0:1, :], 0.0)


def chip_kernel(first, second, first_p, second_p, fwd0, bwd0, fwd, bwd, fs, ss, fp, sp):
    mom = moments()
    even, _ = side()
    offset = jnp.where(even, 2.0, -2.0)

    def frame(f, _):
        split_into(fs, first[f])
        twice_into(ss, second[f])
        split_into(fp, first_p[f])
        twice_into(sp, second_p[f])

        def down_f(n0, w, part):
            fwd[f, :, n0 : n0 + w] = fwd0[f, :, n0 : n0 + w] + shift_y(part, offset)

        def down_b(n0, w, part):
            bwd[f, :, n0 : n0 + w] = bwd0[f, :, n0 : n0 + w] + shift_y(part, offset)

        sums(sp, fs, mom, down_f)
        sums(fp, ss, mom, down_b)
        return 0

    lax.fori_loop(0, FR, frame, 0)


def merge(a, b):
    top = jnp.maximum(a[0], b[0])
    ka, kb = jnp.exp2(a[0] - top), jnp.exp2(b[0] - top)
    return (top,) + tuple(u * ka + v * kb for u, v in zip(a[1:], b[1:]))


def finish(total, mom_x, mom_y, row, height):
    col = lax.broadcasted_iota(jnp.int32, total.shape, 1).astype(jnp.float32) - MID
    return (mom_x / total - col) * (2.0 / W), (mom_y / total - row) * (2.0 / height)


def halves(x):
    return x[:, :W], x[:, W:]


def far_kernel(height, first, second, first_p, second_p, second_o, fwd0, bwd0,
               msg, loc, fs, so, fwd, col, bwd, feats, tops):
    mom = moments()
    even, present = side()
    here = jnp.where(present, 1.0, 0.0)
    far = jnp.where(even, -2.0, 2.0)
    near = -far

    def frame(f, _):
        split_into(fs, first[f])
        twice_into(so, second_o[f])

        def down(n0, w, part):
            fwd[f, :, n0 : n0 + w] = fwd0[f, :, n0 : n0 + w] + here * shift_y(part, far)

        col[f] = here * sums(so, fs, mom, down, across=True)
        bwd[f] = bwd0[f]
        return 0

    lax.fori_loop(0, FR, frame, 0)
    tops[...] = jnp.zeros_like(tops)

    def inside(x):
        return jnp.all((x >= LOW) & (x <= HIGH))

    good = inside(fwd[:, 0:1, :]) & inside(bwd[:, 0:1, :])
    good &= inside(col[:, 0:1, :]) | jnp.logical_not(present)

    @pl.when(jnp.logical_not(good))
    def _():
        index = lax.broadcasted_iota(jnp.int32, (TILE, 1), 0)
        second_row = (index >= W).astype(jnp.float32)
        column = index.astype(jnp.float32) - W * second_row - MID

        def frame(f, _):
            for k, src in enumerate((second, second_p, second_o, first, first_p)):
                feats[k] = src[f]

            def job(dst, slot, query, begin, count):
                for n0 in range(0, TILE, CH):
                    w = min(CH, TILE - n0)
                    rows = query[f, n0 : n0 + w, :]

                    def step(k, old):
                        scores = dot(feats[k], rows, NT) * SCALE
                        rel = k - begin
                        offset = jnp.where(rel == 0, 0.0, jnp.where(rel == 1, near, far))
                        use = jnp.where((rel < 2) | present, 1.0, 0.0)
                        top = jnp.max(scores, axis=0, keepdims=True)
                        weight = jnp.exp2(scores - top) * use
                        total = jnp.sum(weight, axis=0, keepdims=True)
                        fresh = (
                            jnp.where(use > 0, top, -1e30),
                            total,
                            jnp.sum(weight * column, axis=0, keepdims=True),
                            jnp.sum(weight * second_row, axis=0, keepdims=True) + offset * total,
                        )
                        return merge(old, fresh)

                    zero = jnp.zeros((1, w), jnp.float32)
                    status = (jnp.full((1, w), -1e30, jnp.float32), zero, zero, zero)
                    status = lax.fori_loop(begin, begin + count, step, status)
                    tops[f, slot : slot + 1, n0 : n0 + w] = status[0]
                    for k in range(3):
                        dst[f, k : k + 1, n0 : n0 + w] = status[1 + k]

            job(fwd, 0, first, 0, 3)
            job(bwd, 1, second, 3, 2)
            job(col, 2, second_o, 3, 1)
            return 0

        lax.fori_loop(0, FR, frame, 0)

    def pack(f, _):
        g_o = jnp.concatenate([tops[f, 2:3, :], col[f, 0:3, :]], axis=0)
        g_i = jnp.concatenate([tops[f, 1:2, :], bwd[f, 0:3, :]], axis=0)
        o0, o1 = halves(g_o)
        i0, i1 = halves(g_i)
        flows = []
        for row, stat in enumerate(halves(fwd[f, 0:3, :])):
            fx, fy = finish(stat[0:1], stat[1:2], stat[2:3], float(row), height)
            flows.append(jnp.concatenate([fx, fy], axis=0))
        blank = jnp.zeros((2, W), jnp.float32)
        msg[f, 0:4, :] = o0
        msg[f, 4:8, :] = o1
        msg[f, 8:12, :] = jnp.where(even, i0, i1)
        msg[f, 12:14, :] = jnp.where(even, flows[0], flows[1])
        msg[f, 14:16, :] = blank
        loc[f, 0:4, :] = i0
        loc[f, 4:8, :] = i1
        loc[f, 8:10, :] = flows[0]
        loc[f, 10:12, :] = flows[1]
        return 0

    lax.fori_loop(0, FR, pack, 0)


def flow_kernel(height, loc, sent, got, rows, edge):
    even, present = side()
    far = jnp.where(even, -2.0, 2.0)

    def stat(x, offset, keep=None):
        top, total, mx, my = x[0:1], x[1:2], x[2:3], x[3:4]
        if keep is not None:
            top = jnp.where(keep, top, -1e30)
        return top, total, mx, my + offset * total

    for f in range(FR):
        maps = []
        for r in range(2):
            _, total, mx, my = merge(
                stat(loc[f, 4 * r : 4 * r + 4, :], 0.0),
                stat(got[f, 4 * r : 4 * r + 4, :], far, present),
            )
            bx, by = finish(total, mx, my, float(r), height)
            maps.append(jnp.concatenate([loc[f, 8 + 2 * r : 10 + 2 * r, :], bx, by], axis=0))
        mine = jnp.where(even, sent[f, 4:8, :], sent[f, 0:4, :])
        _, total, mx, my = merge(stat(got[f, 8:12, :], 0.0, present), stat(mine, -far))
        total = jnp.where(present, total, 1.0)
        bx, by = finish(total, mx, my, jnp.where(even, 1.0, 0.0), height)
        halo = jnp.concatenate([got[f, 12:14, :], bx, by], axis=0)
        halo = jnp.where(present, halo, 0.0)
        edge[f] = jnp.where(even, maps[1], maps[0])
        rows[f, 0:4, :] = jnp.where(even, halo, 0.0)
        rows[f, 4:8, :] = maps[0]
        rows[f, 8:12, :] = maps[1]
        rows[f, 12:16, :] = jnp.where(even, 0.0, halo)


def refine_kernel(rows, edge, taps, bias, out):
    even, _ = side()
    none = jnp.zeros((16, 1), jnp.float32)
    for f in range(FR):
        mine = rows[f]
        other = edge[f]
        full = jnp.concatenate(
            [jnp.where(even, mine[0:4], other), mine[4:12], jnp.where(even, other, mine[12:16])], axis=0
        )
        left = jnp.concatenate([none, full[:, : W - 1]], axis=1)
        right = jnp.concatenate([full[:, 1:], none], axis=1)
        patches = jnp.concatenate([left, full, right], axis=0)
        mixed = lax.dot_general(
            taps[...], patches, NN, precision=lax.Precision.HIGHEST, preferred_element_type=jnp.float32
        )
        mixed = mixed + bias[...] + full[4:12]
        for o in range(4):
            out[f, o, 0:1, :] = mixed[o : o + 1]
            out[f, o, 1:2, :] = mixed[4 + o : 5 + o]


def call(kernel, shapes, scratch, limit, flops, *args):
    spec = pl.BlockSpec(memory_space=pltpu.VMEM)
    single = not isinstance(shapes, tuple)
    return pl.pallas_call(
        kernel,
        out_shape=shapes,
        in_specs=[spec] * len(args),
        out_specs=spec if single else (spec,) * len(shapes),
        scratch_shapes=scratch,
        compiler_params=pltpu.CompilerParams(vmem_limit_bytes=limit << 20),
        cost_estimate=pl.CostEstimate(flops=flops, bytes_accessed=flops // 1000, transcendentals=0),
    )(*args)


def device_program(first, second, conv_weight, conv_bias):
    size = lax.axis_size("blk")
    height = 2 * size
    f32 = functools.partial(jax.ShapeDtypeStruct, dtype=jnp.float32)
    wide = pltpu.VMEM((TILE, 2 * CH), jnp.bfloat16)
    chip = [(i, i ^ 1) for i in range(size)]
    far = [(i, i - 1 if i % 2 == 0 else i + 1) for i in range(1, size - 1)]

    second_o = lax.ppermute(second, "blk", far)
    second_p = lax.ppermute(second, "blk", chip)
    first_p = lax.ppermute(first, "blk", chip)
    stats = f32((FR, 8, TILE))
    fwd, bwd = call(own_kernel, (stats, stats), [wide] * 2, 16, 10**9, first, second)
    fwd, bwd = call(chip_kernel, (stats, stats), [wide] * 4, 16, 2 * 10**9,
                    first, second, first_p, second_p, fwd, bwd)
    kept = pltpu.VMEM((FR, 8, TILE), jnp.float32)
    msg, loc = call(functools.partial(far_kernel, height), (f32((FR, 16, W)),) * 2,
                    [wide] * 2 + [kept] * 3 + [pltpu.VMEM((5, TILE, CH), jnp.bfloat16), kept], 24, 10**9,
                    first, second, first_p, second_p, second_o, fwd, bwd)
    got = lax.ppermute(msg, "blk", far)
    rows, edge = call(functools.partial(flow_kernel, height), (f32((FR, 16, W)), f32((FR, 4, W))), [], 4, 10**6,
                      loc, msg, got)
    other = lax.ppermute(edge, "blk", chip)
    taps = conv_weight.transpose(0, 3, 2, 1)
    taps = jnp.stack([jnp.pad(taps, ((0, 0), (0, 0), (r, 1 - r), (0, 0))) for r in range(2)])
    taps = taps.reshape(8, 48)
    bias = jnp.concatenate([conv_bias, conv_bias]).reshape(8, 1)
    return call(refine_kernel, f32((FR, 4, 2, W)), [], 4, 10**6, rows, other, taps, bias)


def solution(mesh):
    placed = (P("pair", "blk", None), P("pair", "blk", None), P(), P())
    return jax.shard_map(
        device_program,
        mesh=mesh,
        in_specs=placed,
        out_specs=P("pair", None, "blk", None),
        check_vma=False,
    )
```

time: 94.1 us -> 90.1 us (0.957)
  Pallas kernels: 0 us -> 59.2 us
  matrix products: 34.4 us -> 0 us
  other arithmetic: 31.1 us -> 0.09 us
  waiting for transfers between devices: 1.42 us -> 8.13 us
  starting transfers between devices: 22.3 us -> 19.6 us
  local copies, waits for them, and re-layouts: 4.42 us -> 2.3 us
    pallas_call x0 -> x5, Pallas kernels: none -> 59.2 us  [call(): pl.pallas_call(kernel, out_shape=shapes, in_specs=[spec] * len(args), out...]
    dot_general x21 -> x0, matrix products: 34.4 us -> none  [the longest x12 32.4 us: block_scores(): lax.dot_general(query_rows, key_rows, (((1,), (1,)), ((), ())), preferred...]
    reduce_sum x3 -> x0, other arithmetic: 28 us -> none  [absorb(): jnp.sum(weights * spread_x, axis=axis)]
    ppermute x4 -> x5, waiting for transfers between devices: 1.42 us -> 8.13 us  [the longest x1 7.25 us: device_program(): got = lax.ppermute(msg, 'blk', far)]
    reduce_sum x36 -> x0, local copies, waits for them, and re-layouts: 2.82 us -> none  [the longest x12 0.94 us: absorb(): jnp.sum(weights * spread_x, axis=axis)]
    ppermute x4 -> x5, starting transfers between devices: 22.3 us -> 19.6 us  [the longest x1 11.4 us: device_program(): second_o = lax.ppermute(second, 'blk', far)]
    another operation x11 -> x1, other arithmetic: 2.69 us -> 0.02 us  [device_program(): jnp.stack([jnp.pad(taps, ((0, 0), (0, 0), (r, 1 - r), (0, 0))) for r in r...]
    unnamed x8 -> x12, local copies, waits for them, and re-layouts: 0.01 us -> 2.08 us
  transfers between devices with their start and end apart: 4 -> 5, of which waited for: 1 -> 2; matrix products, arithmetic and copies ran while one was open for 26% -> 0% of each run, Pallas kernels for 0% -> 12%
where the time goes in v1:
time: 90.1 us; the launch traced here: 89.5 us
  Pallas kernels  59.2 us (66%)
  starting transfers between devices  19.6 us (22%)
  waiting for transfers between devices  8.13 us (9%)
  local copies, waits for them, and re-layouts  2.3 us (3%)
    pallas_call x5, Pallas kernels, call(): pl.pallas_call(kernel, out_shape=shapes, in_specs=[spec] * len(args), out...  59.2 us
    ppermute x1, starting transfers between devices, device_program(): second_o = lax.ppermute(second, 'blk', far)  11.4 us
    ppermute x1, waiting for transfers between devices, device_program(): got = lax.ppermute(msg, 'blk', far)  7.25 us
    ppermute x1, starting transfers between devices, device_program(): second_p = lax.ppermute(second, 'blk', chip)  2.41 us
    unnamed x12, local copies, waits for them, and re-layouts  2.08 us
    ppermute x1, starting transfers between devices, device_program(): got = lax.ppermute(msg, 'blk', far)  1.92 us
    ppermute x1, starting transfers between devices, device_program(): other = lax.ppermute(edge, 'blk', chip)  1.92 us
    ppermute x1, starting transfers between devices, device_program(): first_p = lax.ppermute(first, 'blk', chip)  1.91 us
  transfers between devices with their start and end apart: 5, of which 2 were waited for; matrix products, arithmetic and copies ran while one was open for 0% of the time, Pallas kernels for 12%

profile of v1, /device:TPU:38, one launch (start us, length us, event | category | flops | bytes accessed | tf_op | source)
XLA Modules:
  0.0 89.5 jit_solution(14355323421767066830)
XLA Ops:
  0.0 1.9 %collective-permute-start = (bf16[2,960,128]{2,1,0:T(8,128)(2,1)}, bf16[2,960,128]{2,1,0:T(8,128)(2,1)S(1)}, u32[]{:S(2)}, u32[]{:S(2)}) collective-permute-start(bf16[2,960,128]{2,1,0:T(8,128)(2,1)} %first.5), channel_id=1, source_target_pairs={{0,16},{16,0},{32,48},{48,32},{64,80},{80,64},{96,112},{112,96},{1... | collective-permute-start | bytes 1474568 | tf_op jit(solution)/shard_map/ppermute | solution.py:302
  1.9 2.4 %collective-permute-start.1 = (bf16[2,960,128]{2,1,0:T(8,128)(2,1)}, bf16[2,960,128]{2,1,0:T(8,128)(2,1)S(1)}, u32[]{:S(2)}, u32[]{:S(2)}) collective-permute-start(bf16[2,960,128]{2,1,0:T(8,128)(2,1)} %second.5), channel_id=1, source_target_pairs={{0,16},{16,0},{32,48},{48,32},{64,80},{80,64},{96,112},{112,96},{1... | collective-permute-start | bytes 1474568 | tf_op jit(solution)/shard_map/ppermute | solution.py:301
  4.3 11.4 %collective-permute-start.2 = (bf16[2,960,128]{2,1,0:T(8,128)(2,1)}, bf16[2,960,128]{2,1,0:T(8,128)(2,1)S(1)}, u32[]{:S(2)}, u32[]{:S(2)}) collective-permute-start(bf16[2,960,128]{2,1,0:T(8,128)(2,1)} %second.5), channel_id=1, source_target_pairs={{16,32},{32,16},{48,64},{64,48},{80,96},{96,80},{112,128},{128,112... | collective-permute-start | bytes 1474568 | tf_op jit(solution)/shard_map/ppermute | solution.py:300
  15.8 0.0 copy-start
  15.8 1.0 %copy-done = bf16[2,960,128]{2,1,0:T(8,128)(2,1)S(1)} copy-done((bf16[2,960,128]{2,1,0:T(8,128)(2,1)S(1)}, bf16[2,960,128]{2,1,0:T(8,128)(2,1)}, u32[]{:S(2)}) %copy-start) | copy-done | bytes 491544
  16.8 0.0 copy-start.2
  16.8 1.0 %copy-done.2 = bf16[2,960,128]{2,1,0:T(8,128)(2,1)S(1)} copy-done((bf16[2,960,128]{2,1,0:T(8,128)(2,1)S(1)}, bf16[2,960,128]{2,1,0:T(8,128)(2,1)}, u32[]{:S(2)}) %copy-start.2) | copy-done | bytes 491544
  17.8 0.0 copy-start.4
  17.8 4.8 %shard_map.46 = (f32[2,8,960]{2,1,0:T(8,128)S(1)}, f32[2,8,960]{2,1,0:T(8,128)S(1)}) custom-call(bf16[2,960,128]{2,1,0:T(8,128)(2,1)S(1)} %copy-done, bf16[2,960,128]{2,1,0:T(8,128)(2,1)S(1)} %copy-done.2), custom_call_target="tpu_custom_call" | custom-call | flops 1000000000 | bytes 1000000 | tf_op jit(solution)/shard_map/pallas_call | solution.py:281
  22.6 0.0 copy-done.4
  22.7 0.0 collective-permute-done.first_p
  22.7 0.0 collective-permute-done.1.second_p
  22.7 0.0 copy-start.1
  22.7 0.0 copy-start.3
  22.7 6.3 %shard_map.47 = (f32[2,8,960]{2,1,0:T(8,128)S(1)}, f32[2,8,960]{2,1,0:T(8,128)S(1)}) custom-call(bf16[2,960,128]{2,1,0:T(8,128)(2,1)S(1)} %copy-done, bf16[2,960,128]{2,1,0:T(8,128)(2,1)S(1)} %copy-done.2, bf16[2,960,128]{2,1,0:T(8,128)(2,1)S(1)} %collective-permute-done.first_p, bf16[2,960,128]{2,1,0:T(8,128)(2,1)S(1)} %collective-permute-done.1.second_p, ...), custom_call_target="tpu_custom_call" | custom-call | flops 2000000000 | bytes 2000000 | tf_op jit(solution)/shard_map/pallas_call | solution.py:281
  29.0 0.0 collective-permute-done.2.second_o
  29.0 0.0 copy-done.1
  29.0 0.0 copy-done.3
  29.0 47.0 %shard_map.48 = (f32[2,16,480]{2,1,0:T(8,128)S(1)}, f32[2,16,480]{2,1,0:T(8,128)S(1)}) custom-call(bf16[2,960,128]{2,1,0:T(8,128)(2,1)S(1)} %copy-done.1, bf16[2,960,128]{2,1,0:T(8,128)(2,1)S(1)} %copy-done.3, bf16[2,960,128]{2,1,0:T(8,128)(2,1)S(1)} %collective-permute-done.first_p, bf16[2,960,128]{2,1,0:T(8,128)(2,1)S(1)} %collective-permute-done.1.second_p, ...), custom_call_target="tpu_custom_call" | custom-call | flops 1000000000 | bytes 1000000 | tf_op jit(solution)/shard_map/pallas_call | solution.py:281
  76.1 1.9 %collective-permute-start.3 = (f32[2,16,480]{2,1,0:T(8,128)S(1)}, f32[2,16,480]{2,1,0:T(8,128)S(1)}, u32[]{:S(2)}, u32[]{:S(2)}) collective-permute-start(f32[2,16,480]{2,1,0:T(8,128)S(1)} %get-tuple-element.18.sent), channel_id=1, source_target_pairs={{16,32},{32,16},{48,64},{64,48},{80,96},{96,80},{112,128},{128,112... | collective-permute-start | bytes 184328 | tf_op jit(solution)/shard_map/ppermute | solution.py:311
  78.0 7.2 %collective-permute-done.3.got = f32[2,16,480]{2,1,0:T(8,128)S(1)} collective-permute-done((f32[2,16,480]{2,1,0:T(8,128)S(1)}, f32[2,16,480]{2,1,0:T(8,128)S(1)}, u32[]{:S(2)}, u32[]{:S(2)}) %collective-permute-start.3) | collective-permute-done | bytes 61472 | tf_op jit(solution)/shard_map/ppermute | solution.py:311
  85.3 0.2 shard_map.49
  85.4 0.0 copy-start.5
  85.5 1.9 %collective-permute-start.4 = (f32[2,4,480]{2,1,0:T(4,128)S(1)}, f32[2,4,480]{2,1,0:T(4,128)S(1)}, u32[]{:S(2)}, u32[]{:S(2)}) collective-permute-start(f32[2,4,480]{2,1,0:T(4,128)S(1)} %get-tuple-element.20), channel_id=1, source_target_pairs={{0,16},{16,0},{32,48},{48,32},{64,80},{80,64},{96,112},{112,96},{1... | collective-permute-start | bytes 46088 | tf_op jit(solution)/shard_map/ppermute | solution.py:314
  87.4 0.0 copy-done.5
  87.4 0.1 maximum_bitcast_fusion
  87.5 0.1 reshape.6.taps
  87.6 0.1 copy.6.bias
  87.7 0.9 collective-permute-done.4.edge
  88.5 0.9 %shard_map.50 = f32[2,4,2,480]{3,2,1,0:T(2,128)} custom-call(f32[2,16,480]{2,1,0:T(8,128)S(1)} %get-tuple-element.19.rows, f32[2,4,480]{2,1,0:T(4,128)S(1)} %collective-permute-done.4.edge, f32[8,48]{1,0:T(8,128)S(1)} %reshape.6.taps, f32[8,1]{1,0:T(8,128)S(1)} %copy.6.bias), custom_call_target="tpu_custom_call" | custom-call | flops 1000000 | bytes 1000 | tf_op jit(solution)/shard_map/pallas_call | solution.py:281
  (3 shorter events, 0.1 us)
Async XLA Ops:
  0.0 22.7 %collective-permute-start = (bf16[2,960,128]{2,1,0:T(8,128)(2,1)}, bf16[2,960,128]{2,1,0:T(8,128)(2,1)S(1)}, u32[]{:S(2)}, u32[]{:S(2)}) collective-permute-start(bf16[2,960,128]{2,1,0:T(8,128)(2,1)} %first.5), channel_id=1, source_target_pairs={{0,16},{16,0},{32,48},{48,32},{64,80},{80,64},{96,112},{112,96},{1... | collective-permute-start | bytes 1474568 | tf_op jit(solution)/shard_map/ppermute | solution.py:302
  1.9 20.8 %collective-permute-start.1 = (bf16[2,960,128]{2,1,0:T(8,128)(2,1)}, bf16[2,960,128]{2,1,0:T(8,128)(2,1)S(1)}, u32[]{:S(2)}, u32[]{:S(2)}) collective-permute-start(bf16[2,960,128]{2,1,0:T(8,128)(2,1)} %second.5), channel_id=1, source_target_pairs={{0,16},{16,0},{32,48},{48,32},{64,80},{80,64},{96,112},{112,96},{1... | collective-permute-start | bytes 1474568 | tf_op jit(solution)/shard_map/ppermute | solution.py:301
  4.3 24.7 %collective-permute-start.2 = (bf16[2,960,128]{2,1,0:T(8,128)(2,1)}, bf16[2,960,128]{2,1,0:T(8,128)(2,1)S(1)}, u32[]{:S(2)}, u32[]{:S(2)}) collective-permute-start(bf16[2,960,128]{2,1,0:T(8,128)(2,1)} %second.5), channel_id=1, source_target_pairs={{16,32},{32,16},{48,64},{64,48},{80,96},{96,80},{112,128},{128,112... | collective-permute-start | bytes 1474568 | tf_op jit(solution)/shard_map/ppermute | solution.py:300
  15.8 1.0 %copy-start = (bf16[2,960,128]{2,1,0:T(8,128)(2,1)S(1)}, bf16[2,960,128]{2,1,0:T(8,128)(2,1)}, u32[]{:S(2)}) copy-start(bf16[2,960,128]{2,1,0:T(8,128)(2,1)} %first.5) | copy-start | bytes 1474564
  16.8 1.0 %copy-start.2 = (bf16[2,960,128]{2,1,0:T(8,128)(2,1)S(1)}, bf16[2,960,128]{2,1,0:T(8,128)(2,1)}, u32[]{:S(2)}) copy-start(bf16[2,960,128]{2,1,0:T(8,128)(2,1)} %second.5) | copy-start | bytes 1474564
  17.8 4.8 %copy-start.4 = (f32[4,4,3,3]{1,0,3,2:T(4,128)S(1)}, f32[4,4,3,3]{1,0,3,2:T(4,128)}, u32[]{:S(2)}) copy-start(f32[4,4,3,3]{1,0,3,2:T(4,128)} %param.6) | copy-start | bytes 1732
  22.7 6.3 %copy-start.1 = (bf16[2,960,128]{2,1,0:T(8,128)(2,1)S(1)}, bf16[2,960,128]{2,1,0:T(8,128)(2,1)}, u32[]{:S(2)}) copy-start(bf16[2,960,128]{2,1,0:T(8,128)(2,1)} %first.5) | copy-start | bytes 1474564
  22.7 6.3 %copy-start.3 = (bf16[2,960,128]{2,1,0:T(8,128)(2,1)S(1)}, bf16[2,960,128]{2,1,0:T(8,128)(2,1)}, u32[]{:S(2)}) copy-start(bf16[2,960,128]{2,1,0:T(8,128)(2,1)} %second.5) | copy-start | bytes 1474564
  76.1 9.2 %collective-permute-start.3 = (f32[2,16,480]{2,1,0:T(8,128)S(1)}, f32[2,16,480]{2,1,0:T(8,128)S(1)}, u32[]{:S(2)}, u32[]{:S(2)}) collective-permute-start(f32[2,16,480]{2,1,0:T(8,128)S(1)} %get-tuple-element.18.sent), channel_id=1, source_target_pairs={{16,32},{32,16},{48,64},{64,48},{80,96},{96,80},{112,128},{128,112... | collective-permute-start | bytes 184328 | tf_op jit(solution)/shard_map/ppermute | solution.py:311
  85.4 1.9 %copy-start.5 = (f32[4]{0:T(128)S(1)}, f32[4]{0:T(128)}, u32[]{:S(2)}) copy-start(f32[4]{0:T(128)} %param.7) | copy-start | bytes 52
  85.5 3.1 %collective-permute-start.4 = (f32[2,4,480]{2,1,0:T(4,128)S(1)}, f32[2,4,480]{2,1,0:T(4,128)S(1)}, u32[]{:S(2)}, u32[]{:S(2)}) collective-permute-start(f32[2,4,480]{2,1,0:T(4,128)S(1)} %get-tuple-element.20), channel_id=1, source_target_pairs={{0,16},{16,0},{32,48},{48,32},{64,80},{80,64},{96,112},{112,96},{1... | collective-permute-start | bytes 46088 | tf_op jit(solution)/shard_map/ppermute | solution.py:314

commit v2 on v1

--- a/solution.py
+++ b/solution.py
@@ -17,7 +17,6 @@
 SCALE = math.log2(math.e) / math.sqrt(CH)
 LOW = 2.0**-60
 HIGH = 2.0**100
-CHUNKS = ((0, 256), (256, 256), (512, 256), (768, 192))
 NT = (((1,), (1,)), ((), ()))
 NN = (((1,), (0,)), ((), ()))
 
@@ -42,43 +41,84 @@
     return value.astype(jnp.float32).astype(jnp.bfloat16)
 
 
-def split_into(dst, feat):
+def split_into(dst, f, feat):
     scaled = feat.astype(jnp.float32) * SCALE
     hi = scaled.astype(jnp.bfloat16)
-    dst[:, :CH] = hi
-    dst[:, CH:] = (scaled - hi.astype(jnp.float32)).astype(jnp.bfloat16)
-
-
-def twice_into(dst, feat):
-    dst[:, :CH] = feat
-    dst[:, CH:] = feat
-
-
-def sums(lhs, rhs, mom, down, across=False):
-    total = None
-    for n0, w in CHUNKS:
-        weight = jnp.exp2(dot(lhs[...], rhs[n0 : n0 + w, :], NT)).astype(jnp.bfloat16)
-        down(n0, w, dot(mom, weight, NN))
-        if across:
-            part = dot(mom[:, n0 : n0 + w], weight, NT)
-            total = part if total is None else total + part
-    return total
-
-
-def own_kernel(first, second, fwd, bwd, fs, ss):
+    dst[f, :, :CH] = hi
+    dst[f, :, CH:] = (scaled - hi.astype(jnp.float32)).astype(jnp.bfloat16)
+
+
+def twice_into(dst, f, feat):
+    dst[f, :, :CH] = feat
+    dst[f, :, CH:] = feat
+
+
+def down_sums(weight):
+    total = ramp = later = None
+    for r in range(2):
+        run = None
+        for g in range(r * W, (r + 1) * W, 8):
+            part = weight[g : g + 8]
+            run = part if run is None else run + part
+            ramp = run if ramp is None else ramp + run
+        total = run if total is None else total + run
+        later = run
+    sub = lax.broadcasted_iota(jnp.int32, total.shape, 0).astype(jnp.float32)
+    col = (W - MID + sub) * total - 8.0 * ramp
+    rows = [jnp.sum(v, axis=0, keepdims=True) for v in (total, col, later)]
+    return jnp.concatenate(rows + [jnp.zeros((5, total.shape[1]), jnp.float32)], axis=0)
+
+
+def sums(lhs, rhs, f, down, mom=None):
+    size = 256 if mom is None else 512
+    cuts = [(n0, min(size, TILE - n0)) for n0 in range(0, TILE, size)]
+
+    def scores(n0, w):
+        return dot(lhs[f], rhs[f, n0 : n0 + w, :], NT)
+
+    across = None
+    ahead = scores(*cuts[0])
+    for i, (n0, w) in enumerate(cuts):
+        weight = jnp.exp2(ahead)
+        if i + 1 < len(cuts):
+            ahead = scores(*cuts[i + 1])
+        down(n0, w, down_sums(weight))
+        if mom is not None:
+            part = dot(mom[:, n0 : n0 + w], weight.astype(jnp.bfloat16), NT)
+            across = part if across is None else across + part
+    return across
+
+
+def own_block(first, second, fwd, bwd, fs, ss, fbuf, sbuf, sems):
+    copies = []
+    for f in range(FR):
+        for k, (src, dst) in enumerate(((first, fbuf), (second, sbuf))):
+            copies.append(pltpu.make_async_copy(src.at[f], dst.at[f], sems.at[2 * f + k]))
+    for c in copies:
+        c.start()
     mom = moments()
+    for c in copies:
+        c.wait()
 
     def frame(f, _):
-        split_into(fs, first[f])
-        twice_into(ss, second[f])
+        split_into(fs, f, fbuf[f])
+        twice_into(ss, f, sbuf[f])
 
         def down(n0, w, part):
             fwd[f, :, n0 : n0 + w] = part
 
-        bwd[f] = sums(ss, fs, mom, down, across=True)
+        bwd[f] = sums(ss, fs, f, down, mom)
         return 0
 
     lax.fori_loop(0, FR, frame, 0)
+
+
+def even_kernel(*refs):
+    even, _ = side()
+
+    @pl.when(even)
+    def _():
+        own_block(*refs)
 
 
 def shift_y(part, offset):
@@ -86,25 +126,26 @@
     return part + jnp.where(row == 2, offset * part[0:1, :], 0.0)
 
 
-def chip_kernel(first, second, first_p, second_p, fwd0, bwd0, fwd, bwd, fs, ss, fp, sp):
-    mom = moments()
+def chip_kernel(first, second, first_p, second_p, fwd0, bwd0, fs0, ss0, fwd, bwd, fs, ss, fp, sp, fbuf, sbuf, sems):
     even, _ = side()
     offset = jnp.where(even, 2.0, -2.0)
 
+    @pl.when(jnp.logical_not(even))
+    def _():
+        own_block(first, second, fwd, bwd, fs, ss, fbuf, sbuf, sems)
+
     def frame(f, _):
-        split_into(fs, first[f])
-        twice_into(ss, second[f])
-        split_into(fp, first_p[f])
-        twice_into(sp, second_p[f])
+        split_into(fp, f, first_p[f])
+        twice_into(sp, f, second_p[f])
 
         def down_f(n0, w, part):
-            fwd[f, :, n0 : n0 + w] = fwd0[f, :, n0 : n0 + w] + shift_y(part, offset)
+            fwd[f, :, n0 : n0 + w] += shift_y(part, offset)
 
         def down_b(n0, w, part):
-            bwd[f, :, n0 : n0 + w] = bwd0[f, :, n0 : n0 + w] + shift_y(part, offset)
-
-        sums(sp, fs, mom, down_f)
-        sums(fp, ss, mom, down_b)
+            bwd[f, :, n0 : n0 + w] += shift_y(part, offset)
+
+        sums(sp, fs, f, down_f)
+        sums(fp, ss, f, down_b)
         return 0
 
     lax.fori_loop(0, FR, frame, 0)
@@ -125,8 +166,8 @@
     return x[:, :W], x[:, W:]
 
 
-def far_kernel(height, first, second, first_p, second_p, second_o, fwd0, bwd0,
-               msg, loc, fs, so, fwd, col, bwd, feats, tops):
+def far_kernel(height, first, second, first_p, second_p, second_o, fwd0, bwd0, fs,
+               msg, loc, so, fwd, col, bwd, feats, tops, sems):
     mom = moments()
     even, present = side()
     here = jnp.where(present, 1.0, 0.0)
@@ -134,13 +175,12 @@
     near = -far
 
     def frame(f, _):
-        split_into(fs, first[f])
-        twice_into(so, second_o[f])
+        twice_into(so, f, second_o[f])
 
         def down(n0, w, part):
             fwd[f, :, n0 : n0 + w] = fwd0[f, :, n0 : n0 + w] + here * shift_y(part, far)
 
-        col[f] = here * sums(so, fs, mom, down, across=True)
+        col[f] = here * sums(so, fs, f, down, mom)
         bwd[f] = bwd0[f]
         return 0
 
@@ -160,13 +200,18 @@
         column = index.astype(jnp.float32) - W * second_row - MID
 
         def frame(f, _):
+            copies = []
             for k, src in enumerate((second, second_p, second_o, first, first_p)):
-                feats[k] = src[f]
+                copies.append(pltpu.make_async_copy(src.at[f], feats.at[k], sems.at[k]))
+            for c in copies:
+                c.start()
+            for c in copies:
+                c.wait()
 
             def job(dst, slot, query, begin, count):
                 for n0 in range(0, TILE, CH):
                     w = min(CH, TILE - n0)
-                    rows = query[f, n0 : n0 + w, :]
+                    rows = feats[query, n0 : n0 + w, :]
 
                     def step(k, old):
                         scores = dot(feats[k], rows, NT) * SCALE
@@ -191,9 +236,9 @@
                     for k in range(3):
                         dst[f, k : k + 1, n0 : n0 + w] = status[1 + k]
 
-            job(fwd, 0, first, 0, 3)
-            job(bwd, 1, second, 3, 2)
-            job(col, 2, second_o, 3, 1)
+            job(fwd, 0, 3, 0, 3)
+            job(bwd, 1, 0, 3, 2)
+            job(col, 2, 2, 3, 1)
             return 0
 
         lax.fori_loop(0, FR, frame, 0)
@@ -275,15 +320,18 @@
             out[f, o, 1:2, :] = mixed[4 + o : 5 + o]
 
 
-def call(kernel, shapes, scratch, limit, flops, *args):
+def call(kernel, shapes, scratch, limit, flops, *args, hbm=(), far=(), alias={}):
     spec = pl.BlockSpec(memory_space=pltpu.VMEM)
+    anywhere = pl.BlockSpec(memory_space=pl.ANY)
+    home = pl.BlockSpec(memory_space=pltpu.HBM)
     single = not isinstance(shapes, tuple)
     return pl.pallas_call(
         kernel,
         out_shape=shapes,
-        in_specs=[spec] * len(args),
+        in_specs=[home if i in hbm else anywhere if i in far else spec for i in range(len(args))],
         out_specs=spec if single else (spec,) * len(shapes),
         scratch_shapes=scratch,
+        input_output_aliases=alias,
         compiler_params=pltpu.CompilerParams(vmem_limit_bytes=limit << 20),
         cost_estimate=pl.CostEstimate(flops=flops, bytes_accessed=flops // 1000, transcendentals=0),
     )(*args)
@@ -293,21 +341,26 @@
     size = lax.axis_size("blk")
     height = 2 * size
     f32 = functools.partial(jax.ShapeDtypeStruct, dtype=jnp.float32)
-    wide = pltpu.VMEM((TILE, 2 * CH), jnp.bfloat16)
+    wide = pltpu.VMEM((FR, TILE, 2 * CH), jnp.bfloat16)
+    plain = pltpu.VMEM((FR, TILE, CH), jnp.bfloat16)
+    kept = pltpu.VMEM((FR, 8, TILE), jnp.float32)
     chip = [(i, i ^ 1) for i in range(size)]
     far = [(i, i - 1 if i % 2 == 0 else i + 1) for i in range(1, size - 1)]
 
-    second_o = lax.ppermute(second, "blk", far)
     second_p = lax.ppermute(second, "blk", chip)
     first_p = lax.ppermute(first, "blk", chip)
+    second_o = lax.ppermute(second, "blk", far)
     stats = f32((FR, 8, TILE))
-    fwd, bwd = call(own_kernel, (stats, stats), [wide] * 2, 16, 10**9, first, second)
-    fwd, bwd = call(chip_kernel, (stats, stats), [wide] * 4, 16, 2 * 10**9,
-                    first, second, first_p, second_p, fwd, bwd)
-    kept = pltpu.VMEM((FR, 8, TILE), jnp.float32)
-    msg, loc = call(functools.partial(far_kernel, height), (f32((FR, 16, W)),) * 2,
-                    [wide] * 2 + [kept] * 3 + [pltpu.VMEM((5, TILE, CH), jnp.bfloat16), kept], 24, 10**9,
-                    first, second, first_p, second_p, second_o, fwd, bwd)
+    doubled = jax.ShapeDtypeStruct((FR, TILE, 2 * CH), jnp.bfloat16)
+    own_out = (stats, stats, doubled, doubled)
+    load = [plain, plain, pltpu.SemaphoreType.DMA((4,))]
+    fwd, bwd, fs, ss = call(even_kernel, own_out, load, 16, 10**9, first, second, hbm=(0, 1))
+    fwd, bwd, fs, ss = call(chip_kernel, own_out, [wide, wide] + load, 24, 2 * 10**9,
+                            first, second, first_p, second_p, fwd, bwd, fs, ss,
+                            hbm=(0, 1), alias={4: 0, 5: 1, 6: 2, 7: 3})
+    scratch = [wide] + [kept] * 3 + [pltpu.VMEM((5, TILE, CH), jnp.bfloat16), kept, pltpu.SemaphoreType.DMA((5,))]
+    msg, loc = call(functools.partial(far_kernel, height), (f32((FR, 16, W)),) * 2, scratch, 24, 10**9,
+                    first, second, first_p, second_p, second_o, fwd, bwd, fs, hbm=(0, 1), far=(2, 3))
     got = lax.ppermute(msg, "blk", far)
     rows, edge = call(functools.partial(flow_kernel, height), (f32((FR, 16, W)), f32((FR, 4, W))), [], 4, 10**6,
                       loc, msg, got)

time: 90.1 us -> 86.3 us (0.958)
  the two profiles are of different devices: /device:TPU:38 before, /device:TPU:55 now
where the time goes in v2:
time: 86.3 us; the launch traced here: 85.9 us
  Pallas kernels  55.3 us (64%)
  starting transfers between devices  22.8 us (26%)
  waiting for transfers between devices  4.18 us (5%)
  local copies, waits for them, and re-layouts  3.37 us (4%)
    pallas_call x5, Pallas kernels, call(): pl.pallas_call(kernel, out_shape=shapes, in_specs=[home if i in hbm else...  55.3 us
    ppermute x1, starting transfers between devices, device_program(): other = lax.ppermute(edge, 'blk', chip)  12 us
    ppermute x1, starting transfers between devices, device_program(): second_o = lax.ppermute(second, 'blk', far)  4.38 us
    ppermute x1, waiting for transfers between devices, device_program(): got = lax.ppermute(msg, 'blk', far)  3.63 us
    unnamed x12, local copies, waits for them, and re-layouts  3.17 us
    ppermute x1, starting transfers between devices, device_program(): first_p = lax.ppermute(first, 'blk', chip)  2.57 us
    ppermute x1, starting transfers between devices, device_program(): got = lax.ppermute(msg, 'blk', far)  1.92 us
    ppermute x1, starting transfers between devices, device_program(): second_p = lax.ppermute(second, 'blk', chip)  1.92 us
  transfers between devices with their start and end apart: 5, of which 2 were waited for; matrix products, arithmetic and copies ran while one was open for 0% of the time, Pallas kernels for 8%

profile of v2, /device:TPU:55, one launch (start us, length us, event | category | flops | bytes accessed | tf_op | source)
XLA Modules:
  0.0 85.9 jit_solution(1060847462919317433)
XLA Ops:
  0.0 2.6 %collective-permute-start = (bf16[2,960,128]{2,1,0:T(8,128)(2,1)}, bf16[2,960,128]{2,1,0:T(8,128)(2,1)S(1)}, u32[]{:S(2)}, u32[]{:S(2)}) collective-permute-start(bf16[2,960,128]{2,1,0:T(8,128)(2,1)} %first.3), channel_id=1, source_target_pairs={{0,16},{16,0},{32,48},{48,32},{64,80},{80,64},{96,112},{112,96},{1... | collective-permute-start | bytes 1474568 | tf_op jit(solution)/shard_map/ppermute | solution.py:351
  2.6 1.9 %collective-permute-start.1 = (bf16[2,960,128]{2,1,0:T(8,128)(2,1)}, bf16[2,960,128]{2,1,0:T(8,128)(2,1)S(1)}, u32[]{:S(2)}, u32[]{:S(2)}) collective-permute-start(bf16[2,960,128]{2,1,0:T(8,128)(2,1)} %second.3), channel_id=1, source_target_pairs={{0,16},{16,0},{32,48},{48,32},{64,80},{80,64},{96,112},{112,96},{1... | collective-permute-start | bytes 1474568 | tf_op jit(solution)/shard_map/ppermute | solution.py:350
  4.5 4.4 %collective-permute-start.2 = (bf16[2,960,128]{2,1,0:T(8,128)(2,1)}, bf16[2,960,128]{2,1,0:T(8,128)(2,1)S(1)}, u32[]{:S(2)}, u32[]{:S(2)}) collective-permute-start(bf16[2,960,128]{2,1,0:T(8,128)(2,1)} %second.3), channel_id=1, source_target_pairs={{16,32},{32,16},{48,64},{64,48},{80,96},{96,80},{112,128},{128,112... | collective-permute-start | bytes 1474568 | tf_op jit(solution)/shard_map/ppermute | solution.py:352
  8.9 0.0 copy-start
  8.9 1.0 %copy-done = bf16[2,960,128]{2,1,0:T(8,128)(2,1)S(1)} copy-done((bf16[2,960,128]{2,1,0:T(8,128)(2,1)S(1)}, bf16[2,960,128]{2,1,0:T(8,128)(2,1)}, u32[]{:S(2)}) %copy-start) | copy-done | bytes 491544
  9.9 0.0 copy-start.2
  9.9 1.0 %copy-done.2 = bf16[2,960,128]{2,1,0:T(8,128)(2,1)S(1)} copy-done((bf16[2,960,128]{2,1,0:T(8,128)(2,1)S(1)}, bf16[2,960,128]{2,1,0:T(8,128)(2,1)}, u32[]{:S(2)}) %copy-start.2) | copy-done | bytes 491544
  11.0 0.0 copy-start.4
  11.0 0.0 copy-start.1
  11.0 0.0 copy-start.3
  11.0 0.7 copy-done.4
  11.7 0.0 collective-permute-done.first_p
  11.7 0.0 collective-permute-done.1.second_p
  11.7 0.3 copy-done.1
  12.0 0.1 copy-done.3
  12.2 6.6 %shard_map.47 = (f32[2,8,960]{2,1,0:T(8,128)S(1)}, f32[2,8,960]{2,1,0:T(8,128)S(1)}, bf16[2,960,256]{2,1,0:T(8,128)(2,1)S(1)}, bf16[2,960,256]{2,1,0:T(8,128)(2,1)S(1)}) custom-call(bf16[2,960,128]{2,1,0:T(8,128)(2,1)S(1)} %copy-done.1, bf16[2,960,128]{2,1,0:T(8,128)(2,1)S(1)} %copy-done.3, ...), custom_call_target="tpu_custom_call", output_to_operand_aliasing={{0}: (4, {}), {1}: (5, {}), {2}: (6, {}), {3}: (7, {})} | custom-call | flops 2000000000 | bytes 2000000 | tf_op jit(solution)/shard_map/pallas_call | solution.py:328
  18.8 0.0 collective-permute-done.2.second_o
  18.8 47.6 %shard_map.48 = (f32[2,16,480]{2,1,0:T(8,128)S(1)}, f32[2,16,480]{2,1,0:T(8,128)S(1)}) custom-call(bf16[2,960,128]{2,1,0:T(8,128)(2,1)S(1)} %copy-done.1, bf16[2,960,128]{2,1,0:T(8,128)(2,1)S(1)} %copy-done.3, bf16[2,960,128]{2,1,0:T(8,128)(2,1)S(1)} %collective-permute-done.first_p, bf16[2,960,128]{2,1,0:T(8,128)(2,1)S(1)} %collective-permute-done.1.second_p, ...), custom_call_target="tpu_custom_call" | custom-call | flops 1000000000 | bytes 1000000 | tf_op jit(solution)/shard_map/pallas_call | solution.py:328
  66.4 1.9 %collective-permute-start.3 = (f32[2,16,480]{2,1,0:T(8,128)S(1)}, f32[2,16,480]{2,1,0:T(8,128)S(1)}, u32[]{:S(2)}, u32[]{:S(2)}) collective-permute-start(f32[2,16,480]{2,1,0:T(8,128)S(1)} %get-tuple-element.24.sent), channel_id=1, source_target_pairs={{16,32},{32,16},{48,64},{64,48},{80,96},{96,80},{112,128},{128,112... | collective-permute-start | bytes 184328 | tf_op jit(solution)/shard_map/ppermute | solution.py:364
  68.4 3.6 %collective-permute-done.3.got = f32[2,16,480]{2,1,0:T(8,128)S(1)} collective-permute-done((f32[2,16,480]{2,1,0:T(8,128)S(1)}, f32[2,16,480]{2,1,0:T(8,128)S(1)}, u32[]{:S(2)}, u32[]{:S(2)}) %collective-permute-start.3) | collective-permute-done | bytes 61472 | tf_op jit(solution)/shard_map/ppermute | solution.py:364
  72.0 0.2 shard_map.49
  72.2 0.0 copy-start.5
  72.2 12.0 %collective-permute-start.4 = (f32[2,4,480]{2,1,0:T(4,128)S(1)}, f32[2,4,480]{2,1,0:T(4,128)S(1)}, u32[]{:S(2)}, u32[]{:S(2)}) collective-permute-start(f32[2,4,480]{2,1,0:T(4,128)S(1)} %get-tuple-element.26), channel_id=1, source_target_pairs={{0,16},{16,0},{32,48},{48,32},{64,80},{80,64},{96,112},{112,96},{1... | collective-permute-start | bytes 46088 | tf_op jit(solution)/shard_map/ppermute | solution.py:367
  84.2 0.0 copy-done.5
  84.2 0.1 maximum_bitcast_fusion
  84.3 0.1 reshape.6.taps
  84.4 0.1 copy.10.bias
  84.5 0.5 collective-permute-done.4.edge
  85.0 0.9 %shard_map.50 = f32[2,4,2,480]{3,2,1,0:T(2,128)} custom-call(f32[2,16,480]{2,1,0:T(8,128)S(1)} %get-tuple-element.25.rows, f32[2,4,480]{2,1,0:T(4,128)S(1)} %collective-permute-done.4.edge, f32[8,48]{1,0:T(8,128)S(1)} %reshape.6.taps, f32[8,1]{1,0:T(8,128)S(1)} %copy.10.bias), custom_call_target="tpu_custom_call" | custom-call | flops 1000000 | bytes 1000 | tf_op jit(solution)/shard_map/pallas_call | solution.py:328
  (4 shorter events, 0.1 us)
Async XLA Ops:
  0.0 11.7 %collective-permute-start = (bf16[2,960,128]{2,1,0:T(8,128)(2,1)}, bf16[2,960,128]{2,1,0:T(8,128)(2,1)S(1)}, u32[]{:S(2)}, u32[]{:S(2)}) collective-permute-start(bf16[2,960,128]{2,1,0:T(8,128)(2,1)} %first.3), channel_id=1, source_target_pairs={{0,16},{16,0},{32,48},{48,32},{64,80},{80,64},{96,112},{112,96},{1... | collective-permute-start | bytes 1474568 | tf_op jit(solution)/shard_map/ppermute | solution.py:351
  2.6 9.1 %collective-permute-start.1 = (bf16[2,960,128]{2,1,0:T(8,128)(2,1)}, bf16[2,960,128]{2,1,0:T(8,128)(2,1)S(1)}, u32[]{:S(2)}, u32[]{:S(2)}) collective-permute-start(bf16[2,960,128]{2,1,0:T(8,128)(2,1)} %second.3), channel_id=1, source_target_pairs={{0,16},{16,0},{32,48},{48,32},{64,80},{80,64},{96,112},{112,96},{1... | collective-permute-start | bytes 1474568 | tf_op jit(solution)/shard_map/ppermute | solution.py:350
  4.5 14.3 %collective-permute-start.2 = (bf16[2,960,128]{2,1,0:T(8,128)(2,1)}, bf16[2,960,128]{2,1,0:T(8,128)(2,1)S(1)}, u32[]{:S(2)}, u32[]{:S(2)}) collective-permute-start(bf16[2,960,128]{2,1,0:T(8,128)(2,1)} %second.3), channel_id=1, source_target_pairs={{16,32},{32,16},{48,64},{64,48},{80,96},{96,80},{112,128},{128,112... | collective-permute-start | bytes 1474568 | tf_op jit(solution)/shard_map/ppermute | solution.py:352
  8.9 1.0 %copy-start = (bf16[2,960,128]{2,1,0:T(8,128)(2,1)S(1)}, bf16[2,960,128]{2,1,0:T(8,128)(2,1)}, u32[]{:S(2)}) copy-start(bf16[2,960,128]{2,1,0:T(8,128)(2,1)} %first.3) | copy-start | bytes 1474564
  9.9 1.0 %copy-start.2 = (bf16[2,960,128]{2,1,0:T(8,128)(2,1)S(1)}, bf16[2,960,128]{2,1,0:T(8,128)(2,1)}, u32[]{:S(2)}) copy-start(bf16[2,960,128]{2,1,0:T(8,128)(2,1)} %second.3) | copy-start | bytes 1474564
  11.0 0.7 copy-start.4
  11.0 1.0 %copy-start.1 = (bf16[2,960,128]{2,1,0:T(8,128)(2,1)S(1)}, bf16[2,960,128]{2,1,0:T(8,128)(2,1)}, u32[]{:S(2)}) copy-start(bf16[2,960,128]{2,1,0:T(8,128)(2,1)} %first.3) | copy-start | bytes 1474564
  11.0 1.2 %copy-start.3 = (bf16[2,960,128]{2,1,0:T(8,128)(2,1)S(1)}, bf16[2,960,128]{2,1,0:T(8,128)(2,1)}, u32[]{:S(2)}) copy-start(bf16[2,960,128]{2,1,0:T(8,128)(2,1)} %second.3) | copy-start | bytes 1474564
  66.4 5.6 %collective-permute-start.3 = (f32[2,16,480]{2,1,0:T(8,128)S(1)}, f32[2,16,480]{2,1,0:T(8,128)S(1)}, u32[]{:S(2)}, u32[]{:S(2)}) collective-permute-start(f32[2,16,480]{2,1,0:T(8,128)S(1)} %get-tuple-element.24.sent), channel_id=1, source_target_pairs={{16,32},{32,16},{48,64},{64,48},{80,96},{96,80},{112,128},{128,112... | collective-permute-start | bytes 184328 | tf_op jit(solution)/shard_map/ppermute | solution.py:364
  72.2 12.1 %copy-start.5 = (f32[4]{0:T(128)S(1)}, f32[4]{0:T(128)}, u32[]{:S(2)}) copy-start(f32[4]{0:T(128)} %param.7) | copy-start | bytes 52
  72.2 12.9 %collective-permute-start.4 = (f32[2,4,480]{2,1,0:T(4,128)S(1)}, f32[2,4,480]{2,1,0:T(4,128)S(1)}, u32[]{:S(2)}, u32[]{:S(2)}) collective-permute-start(f32[2,4,480]{2,1,0:T(4,128)S(1)} %get-tuple-element.26), channel_id=1, source_target_pairs={{0,16},{16,0},{32,48},{48,32},{64,80},{80,64},{96,112},{112,96},{1... | collective-permute-start | bytes 46088 | tf_op jit(solution)/shard_map/ppermute | solution.py:367

commit v3 on v2

v3 whole, which is shorter than its diff:
```python
import functools
import math

import jax
import jax.numpy as jnp
from jax import lax
from jax.experimental import pallas as pl
from jax.experimental.pallas import tpu as pltpu
from jax.sharding import PartitionSpec as P


W = 480
TILE = 960
CH = 128
FR = 2
MID = 240.0
SCALE = math.log2(math.e) / math.sqrt(CH)
LOW = 2.0**-60
HIGH = 2.0**100
NT = (((1,), (1,)), ((), ()))
NN = (((1,), (0,)), ((), ()))


def dot(a, b, dims):
    return lax.dot_general(a, b, dims, preferred_element_type=jnp.float32)


def side():
    pos = lax.axis_index("blk")
    even = pos % 2 == 0
    present = jnp.where(even, pos > 0, pos < lax.axis_size("blk") - 1)
    return even, present


def moments():
    lane = lax.broadcasted_iota(jnp.int32, (8, TILE), 1)
    row = lax.broadcasted_iota(jnp.int32, (8, TILE), 0)
    second = (lane >= W).astype(jnp.int32)
    col = lane - W * second - int(MID)
    value = jnp.where(row == 0, 1, jnp.where(row == 1, col, jnp.where(row == 2, second, 0)))
    return value.astype(jnp.float32).astype(jnp.bfloat16)


def split_into(dst, f, feat):
    scaled = feat.astype(jnp.float32) * SCALE
    hi = scaled.astype(jnp.bfloat16)
    dst[f, :, :CH] = hi
    dst[f, :, CH:] = (scaled - hi.astype(jnp.float32)).astype(jnp.bfloat16)


def twice_into(dst, f, feat):
    dst[f, :, :CH] = feat
    dst[f, :, CH:] = feat


def down_sums(weight):
    total = ramp = later = None
    for r in range(2):
        run = None
        for g in range(r * W, (r + 1) * W, 8):
            part = weight[g : g + 8]
            run = part if run is None else run + part
            ramp = run if ramp is None else ramp + run
        total = run if total is None else total + run
        later = run
    sub = lax.broadcasted_iota(jnp.int32, total.shape, 0).astype(jnp.float32)
    col = (W - MID + sub) * total - 8.0 * ramp
    rows = [jnp.sum(v, axis=0, keepdims=True) for v in (total, col, later)]
    return jnp.concatenate(rows + [jnp.zeros((5, total.shape[1]), jnp.float32)], axis=0)


def sums(lhs, rhs, f, down, mom=None):
    size = 256 if mom is None else 512
    cuts = [(n0, min(size, TILE - n0)) for n0 in range(0, TILE, size)]

    def scores(n0, w):
        return dot(lhs[f], rhs[f, n0 : n0 + w, :], NT)

    across = None
    ahead = scores(*cuts[0])
    for i, (n0, w) in enumerate(cuts):
        weight = jnp.exp2(ahead)
        if i + 1 < len(cuts):
            ahead = scores(*cuts[i + 1])
        down(n0, w, down_sums(weight))
        if mom is not None:
            part = dot(mom[:, n0 : n0 + w], weight.astype(jnp.bfloat16), NT)
            across = part if across is None else across + part
    return across


def merge(a, b):
    top = jnp.maximum(a[0], b[0])
    ka, kb = jnp.exp2(a[0] - top), jnp.exp2(b[0] - top)
    return (top,) + tuple(u * ka + v * kb for u, v in zip(a[1:], b[1:]))


def finish(total, mom_x, mom_y, row, height):
    col = lax.broadcasted_iota(jnp.int32, total.shape, 1).astype(jnp.float32) - MID
    return (mom_x / total - col) * (2.0 / W), (mom_y / total - row) * (2.0 / height)


def own_kernel(first, second, fwd, bwd, fs, ss, fbuf, sbuf, sems):
    copies = []
    for f in range(FR):
        for k, (src, dst) in enumerate(((first, fbuf), (second, sbuf))):
            copies.append(pltpu.make_async_copy(src.at[f], dst.at[f], sems.at[2 * f + k]))
    for c in copies:
        c.start()
    mom = moments()
    for c in copies:
        c.wait()

    def frame(f, _):
        split_into(fs, f, fbuf[f])
        twice_into(ss, f, sbuf[f])

        def down(n0, w, part):
            fwd[f, :, n0 : n0 + w] = part

        bwd[f] = sums(ss, fs, f, down, mom)
        return 0

    lax.fori_loop(0, FR, frame, 0)


def shift_y(part, offset):
    row = lax.broadcasted_iota(jnp.int32, part.shape, 0)
    return part + jnp.where(row == 2, offset * part[0:1, :], 0.0)


def inside(x):
    return jnp.all((x[:, 0:1, :] >= LOW) & (x[:, 0:1, :] <= HIGH))


def exact(sources, feats, found, sems, jobs, tiles, near, far):
    index = lax.broadcasted_iota(jnp.int32, (TILE, 1), 0)
    second_row = (index >= W).astype(jnp.float32)
    column = index.astype(jnp.float32) - W * second_row - MID

    def frame(f, _):
        copies = [pltpu.make_async_copy(src.at[f], feats.at[k], sems.at[k]) for k, src in sources.items()]
        for c in copies:
            c.start()
        for c in copies:
            c.wait()

        def job(j, _):
            query = jnp.where(j == 0, 3, jnp.where(j == 1, 0, jnp.where(j == 2, 2, 5)))
            begin = jnp.where((j == 1) | (j == 2), 3, 0)
            end = begin + jnp.where(j < 2, tiles, 1)
            for n0 in range(0, TILE, CH):
                w = min(CH, TILE - n0)
                rows = feats[query, n0 : n0 + w, :]

                def step(k, old):
                    scores = dot(feats[k], rows, NT) * SCALE
                    rel = k - begin
                    offset = jnp.where(rel == 0, 0.0, jnp.where(rel == 1, near, far))
                    top = jnp.max(scores, axis=0, keepdims=True)
                    weight = jnp.exp2(scores - top)
                    total = jnp.sum(weight, axis=0, keepdims=True)
                    mom_x = jnp.sum(weight * column, axis=0, keepdims=True)
                    mom_y = jnp.sum(weight * second_row, axis=0, keepdims=True) + offset * total
                    return merge(old, (top, total, mom_x, mom_y))

                zero = jnp.zeros((1, w), jnp.float32)
                status = (jnp.full((1, w), -1e30, jnp.float32), zero, zero, zero)
                status = lax.fori_loop(begin, end, step, status)
                found[f, j, 0:4, n0 : n0 + w] = jnp.concatenate(status, axis=0)
            return 0

        lax.fori_loop(0, jobs, job, 0)
        return 0

    lax.fori_loop(0, FR, frame, 0)


def plain(part):
    return jnp.concatenate([jnp.zeros_like(part[0:1]), part[0:3]], axis=0)


def chip_kernel(first, second, first_p, second_p, fwd0, bwd0, fs, ss, fwd, bwd, part, up, fp, sp, feats, found, sems):
    even, _ = side()
    near = jnp.where(even, 2.0, -2.0)

    def frame(f, _):
        split_into(fp, f, first_p[f])
        twice_into(sp, f, second_p[f])

        def down_f(n0, w, part):
            fwd[f, :, n0 : n0 + w] = fwd0[f, :, n0 : n0 + w] + shift_y(part, near)

        def down_b(n0, w, part):
            bwd[f, :, n0 : n0 + w] = bwd0[f, :, n0 : n0 + w] + shift_y(part, near)

        sums(sp, fs, f, down_f)
        sums(fp, ss, f, down_b)
        return 0

    lax.fori_loop(0, FR, frame, 0)

    @pl.when(jnp.logical_not(even))
    def _():
        for f in range(FR):
            found[f, 0, 0:4, :] = plain(fwd[f])
            found[f, 1, 0:4, :] = plain(bwd[f])

        @pl.when(jnp.logical_not(inside(fwd) & inside(bwd)))
        def _():
            exact({0: second, 1: second_p, 3: first, 4: first_p}, feats, found, sems, 2, 2, near, near)

        for f in range(FR):
            for j in range(2):
                stat = found[f, j, 0:4, :]
                part[f, 4 * j : 4 * j + 4, :] = stat
                up[f, 4 * j : 4 * j + 4, :] = stat[:, W:]


def far_second_kernel(second_o, fs, fwd0, fwd, col, so):
    even, present = side()

    @pl.when(even & present)
    def _():
        mom = moments()

        def frame(f, _):
            twice_into(so, f, second_o[f])

            def down(n0, w, part):
                fwd[f, :, n0 : n0 + w] = fwd0[f, :, n0 : n0 + w] + shift_y(part, -2.0)

            col[f] = sums(so, fs, f, down, mom)
            return 0

        lax.fori_loop(0, FR, frame, 0)

    @pl.when(even & jnp.logical_not(present))
    def _():
        fwd[...] = fwd0[...]
        col[...] = jnp.ones_like(col)


def far_first_kernel(height, first, second, first_p, second_p, second_o, first_o, ss, bwd0, fwd, col,
                     down, flows, fo, bwd, row, feats, found, sems):
    even, present = side()

    @pl.when(even)
    def _():
        @pl.when(present)
        def _():
            mom = moments()

            def frame(f, _):
                split_into(fo, f, first_o[f])

                def keep(n0, w, part):
                    bwd[f, :, n0 : n0 + w] = bwd0[f, :, n0 : n0 + w] + shift_y(part, -2.0)

                row[f] = sums(fo, ss, f, keep, mom)
                return 0

            lax.fori_loop(0, FR, frame, 0)

        @pl.when(jnp.logical_not(present))
        def _():
            bwd[...] = bwd0[...]
            row[...] = jnp.ones_like(row)

        for f in range(FR):
            for j, stat in enumerate((fwd, bwd, col, row)):
                found[f, j, 0:4, :] = plain(stat[f])

        @pl.when(jnp.logical_not(inside(fwd) & inside(bwd) & inside(col) & inside(row)))
        def _():
            sources = {0: second, 1: second_p, 2: second_o, 3: first, 4: first_p, 5: first_o}
            exact(sources, feats, found, sems, jnp.where(present, 4, 2), jnp.where(present, 3, 2), 2.0, -2.0)

        for f in range(FR):
            for r in range(2):
                maps = []
                for j in range(2):
                    stat = found[f, j, 0:4, :]
                    stat = stat[:, r * W : r * W + W]
                    maps.extend(finish(stat[1:2], stat[2:3], stat[3:4], float(r), height))
                maps = jnp.concatenate(maps, axis=0)
                flows[f, 4 * r : 4 * r + 4, :] = maps
                if r == 0:
                    down[f, 16:20, :] = maps
            for j in range(2):
                stat = found[f, 2 + j, 0:4, :]
                down[f, 8 * j : 8 * j + 4, :] = stat[:, :W]
                down[f, 8 * j + 4 : 8 * j + 8, :] = stat[:, W:]
            down[f, 20:24, :] = jnp.zeros((4, W), jnp.float32)


def flow_kernel(height, part, flows, sent, up, down, rows, edge):
    even, present = side()

    def stat(x, offset):
        return x[0:1], x[1:2], x[2:3], x[3:4] + offset * x[1:2]

    @pl.when(even)
    def _():
        for f in range(FR):
            halo = []
            for j, mine in ((0, sent[f, 12:16, :]), (1, sent[f, 4:8, :])):
                _, total, mx, my = merge(stat(up[f, 4 * j : 4 * j + 4, :], 0.0), stat(mine, 2.0))
                halo.extend(finish(total, mx, my, 1.0, height))
            rows[f, 0:4, :] = jnp.where(present, jnp.concatenate(halo, axis=0), 0.0)
            rows[f, 4:12, :] = flows[f]
            rows[f, 12:16, :] = jnp.zeros((4, W), jnp.float32)
            edge[f] = flows[f, 4:8, :]

    @pl.when(jnp.logical_not(even))
    def _():
        for f in range(FR):
            for r in range(2):
                maps = []
                for j in range(2):
                    mine = part[f, 4 * j : 4 * j + 4, :]
                    at = 8 * (1 - j) + 4 * r
                    top, total, mx, my = stat(down[f, at : at + 4, :], 2.0)
                    other = (jnp.where(present, top, -1e30), total, mx, my)
                    _, total, mx, my = merge(stat(mine[:, r * W : r * W + W], 0.0), other)
                    maps.extend(finish(total, mx, my, float(r), height))
                maps = jnp.concatenate(maps, axis=0)
                rows[f, 4 + 4 * r : 8 + 4 * r, :] = maps
                if r == 0:
                    edge[f] = maps
            rows[f, 0:4, :] = jnp.zeros((4, W), jnp.float32)
            rows[f, 12:16, :] = jnp.where(present, down[f, 16:20, :], 0.0)


def refine_kernel(rows, edge, taps, bias, out):
    even, _ = side()
    none = jnp.zeros((16, 1), jnp.float32)
    for f in range(FR):
        mine = rows[f]
        other = edge[f]
        full = jnp.concatenate(
            [jnp.where(even, mine[0:4], other), mine[4:12], jnp.where(even, other, mine[12:16])], axis=0
        )
        left = jnp.concatenate([none, full[:, : W - 1]], axis=1)
        right = jnp.concatenate([full[:, 1:], none], axis=1)
        patches = jnp.concatenate([left, full, right], axis=0)
        mixed = lax.dot_general(
            taps[...], patches, NN, precision=lax.Precision.HIGHEST, preferred_element_type=jnp.float32
        )
        mixed = mixed + bias[...] + full[4:12]
        for o in range(4):
            out[f, o, 0:1, :] = mixed[o : o + 1]
            out[f, o, 1:2, :] = mixed[4 + o : 5 + o]


def call(kernel, shapes, scratch, limit, flops, *args, hbm=(), far=(), alias={}):
    spec = pl.BlockSpec(memory_space=pltpu.VMEM)
    anywhere = pl.BlockSpec(memory_space=pl.ANY)
    home = pl.BlockSpec(memory_space=pltpu.HBM)
    single = not isinstance(shapes, tuple)
    return pl.pallas_call(
        kernel,
        out_shape=shapes,
        in_specs=[home if i in hbm else anywhere if i in far else spec for i in range(len(args))],
        out_specs=spec if single else (spec,) * len(shapes),
        scratch_shapes=scratch,
        input_output_aliases=alias,
        compiler_params=pltpu.CompilerParams(vmem_limit_bytes=limit << 20),
        cost_estimate=pl.CostEstimate(flops=flops, bytes_accessed=flops // 1000, transcendentals=0),
    )(*args)


def device_program(first, second, conv_weight, conv_bias):
    size = lax.axis_size("blk")
    height = 2 * size
    f32 = functools.partial(jax.ShapeDtypeStruct, dtype=jnp.float32)
    wide = pltpu.VMEM((FR, TILE, 2 * CH), jnp.bfloat16)
    narrow = pltpu.VMEM((FR, TILE, CH), jnp.bfloat16)
    kept = pltpu.VMEM((FR, 8, TILE), jnp.float32)
    spare = [pltpu.VMEM((6, TILE, CH), jnp.bfloat16), pltpu.VMEM((FR, 4, 8, TILE), jnp.float32)]
    spare.append(pltpu.SemaphoreType.DMA((6,)))
    chip = [(i, i ^ 1) for i in range(size)]
    upward = [(i, i + 1) for i in range(1, size - 1, 2)]
    downward = [(j, i) for i, j in upward]

    second_o = lax.ppermute(second, "blk", upward)
    first_o = lax.ppermute(first, "blk", upward)
    second_p = lax.ppermute(second, "blk", chip)
    first_p = lax.ppermute(first, "blk", chip)
    first, second = (pltpu.with_memory_space_constraint(x, pltpu.HBM) for x in (first, second))
    stats = f32((FR, 8, TILE))
    doubled = jax.ShapeDtypeStruct((FR, TILE, 2 * CH), jnp.bfloat16)
    fwd, bwd, fs, ss = call(own_kernel, (stats, stats, doubled, doubled),
                            [narrow, narrow, pltpu.SemaphoreType.DMA((4,))], 12, 10**9,
                            first, second, hbm=(0, 1))
    fwd, bwd, part, up = call(chip_kernel, (stats, stats, stats, f32((FR, 8, W))), [wide, wide] + spare, 20,
                              2 * 10**9, first, second, first_p, second_p, fwd, bwd, fs, ss, hbm=(0, 1))
    up = lax.ppermute(up, "blk", upward)
    fwd, col = call(far_second_kernel, (stats, stats), [wide], 12, 10**9, second_o, fs, fwd)
    sent, flows = call(functools.partial(far_first_kernel, height), (f32((FR, 24, W)), f32((FR, 8, W))),
                       [wide, kept, kept] + spare, 20, 10**9,
                       first, second, first_p, second_p, second_o, first_o, ss, bwd, fwd, col,
                       hbm=(0, 1), far=(2, 3, 4))
    down = lax.ppermute(sent, "blk", downward)
    rows, edge = call(functools.partial(flow_kernel, height), (f32((FR, 16, W)), f32((FR, 4, W))), [], 4, 10**6,
                      part, flows, sent, up, down)
    other = lax.ppermute(edge, "blk", chip)
    taps = conv_weight.transpose(0, 3, 2, 1)
    taps = jnp.stack([jnp.pad(taps, ((0, 0), (0, 0), (r, 1 - r), (0, 0))) for r in range(2)])
    taps = taps.reshape(8, 48)
    bias = jnp.concatenate([conv_bias, conv_bias]).reshape(8, 1)
    return call(refine_kernel, f32((FR, 4, 2, W)), [], 4, 10**6, rows, other, taps, bias)


def solution(mesh):
    placed = (P("pair", "blk", None), P("pair", "blk", None), P(), P())
    return jax.shard_map(
        device_program,
        mesh=mesh,
        in_specs=placed,
        out_specs=P("pair", None, "blk", None),
        check_vma=False,
    )
```

time: 86.3 us -> 104 us (1.21)
  the two profiles are of different devices: /device:TPU:55 before, /device:TPU:38 now
where the time goes in v3:
time: 104 us; the launch traced here: 103 us
  Pallas kernels  72.1 us (69%)
  waiting for transfers between devices  19.3 us (19%)
  starting transfers between devices  11.5 us (11%)
    pallas_call x6, Pallas kernels, call(): pl.pallas_call(kernel, out_shape=shapes, in_specs=[home if i in hbm else...  72.1 us
    ppermute x1, waiting for transfers between devices, device_program(): second_o = lax.ppermute(second, 'blk', upward)  8.06 us
    ppermute x1, waiting for transfers between devices, device_program(): up = lax.ppermute(up, 'blk', upward)  7.52 us
    ppermute x1, waiting for transfers between devices, device_program(): first_o = lax.ppermute(first, 'blk', upward)  2.86 us
    ppermute x1, starting transfers between devices, device_program(): second_p = lax.ppermute(second, 'blk', chip)  2.41 us
  transfers between devices with their start and end apart: 7, of which 4 were waited for; matrix products, arithmetic and copies ran while one was open for 0% of the time, Pallas kernels for 9%

profile of v3, /device:TPU:38, one launch (start us, length us, event | category | flops | bytes accessed | tf_op | source)
XLA Modules:
  0.0 103.4 jit_solution(7301552600974038001)
XLA Ops:
  0.0 0.0 copy-start
  0.0 2.0 %collective-permute-start = (bf16[2,960,128]{2,1,0:T(8,128)(2,1)}, bf16[2,960,128]{2,1,0:T(8,128)(2,1)S(1)}, u32[]{:S(2)}, u32[]{:S(2)}) collective-permute-start(bf16[2,960,128]{2,1,0:T(8,128)(2,1)} %first.5), channel_id=1, source_target_pairs={{0,16},{16,0},{32,48},{48,32},{64,80},{80,64},{96,112},{112,96},{1... | collective-permute-start | bytes 1474568 | tf_op jit(solution)/shard_map/ppermute | solution.py:389
  2.1 2.4 %collective-permute-start.1 = (bf16[2,960,128]{2,1,0:T(8,128)(2,1)}, bf16[2,960,128]{2,1,0:T(8,128)(2,1)S(1)}, u32[]{:S(2)}, u32[]{:S(2)}) collective-permute-start(bf16[2,960,128]{2,1,0:T(8,128)(2,1)} %second.5), channel_id=1, source_target_pairs={{0,16},{16,0},{32,48},{48,32},{64,80},{80,64},{96,112},{112,96},{1... | collective-permute-start | bytes 1474568 | tf_op jit(solution)/shard_map/ppermute | solution.py:388
  4.5 1.3 %collective-permute-start.2 = (bf16[2,960,128]{2,1,0:T(8,128)(2,1)}, bf16[2,960,128]{2,1,0:T(8,128)(2,1)S(1)}, u32[]{:S(2)}, u32[]{:S(2)}) collective-permute-start(bf16[2,960,128]{2,1,0:T(8,128)(2,1)} %second.5), channel_id=1, source_target_pairs={{16,32},{48,64},{80,96},{112,128},{144,160},{176,192},{208,224},{2... | collective-permute-start | bytes 1474568 | tf_op jit(solution)/shard_map/ppermute | solution.py:386
  5.8 1.3 %collective-permute-start.3 = (bf16[2,960,128]{2,1,0:T(8,128)(2,1)}, bf16[2,960,128]{2,1,0:T(8,128)(2,1)S(1)}, u32[]{:S(2)}, u32[]{:S(2)}) collective-permute-start(bf16[2,960,128]{2,1,0:T(8,128)(2,1)} %first.5), channel_id=1, source_target_pairs={{16,32},{48,64},{80,96},{112,128},{144,160},{176,192},{208,224},{2... | collective-permute-start | bytes 1474568 | tf_op jit(solution)/shard_map/ppermute | solution.py:387
  7.1 3.9 %shard_map.46 = (f32[2,8,960]{2,1,0:T(8,128)S(1)}, f32[2,8,960]{2,1,0:T(8,128)S(1)}, bf16[2,960,256]{2,1,0:T(8,128)(2,1)S(1)}, bf16[2,960,256]{2,1,0:T(8,128)(2,1)S(1)}) custom-call(bf16[2,960,128]{2,1,0:T(8,128)(2,1)} %first.5, bf16[2,960,128]{2,1,0:T(8,128)(2,1)} %second.5), custom_call_target="tpu_custom_call" | custom-call | flops 1000000000 | bytes 1000000 | tf_op jit(solution)/shard_map/pallas_call | solution.py:361
  10.9 0.0 copy-done
  11.0 0.0 collective-permute-done.first_p
  11.0 0.0 collective-permute-done.1.second_p
  11.0 2.9 %shard_map.47 = (f32[2,8,960]{2,1,0:T(8,128)S(1)}, f32[2,8,960]{2,1,0:T(8,128)S(1)}, f32[2,8,960]{2,1,0:T(8,128)S(1)}, f32[2,8,480]{2,1,0:T(8,128)S(1)}) custom-call(bf16[2,960,128]{2,1,0:T(8,128)(2,1)} %first.5, bf16[2,960,128]{2,1,0:T(8,128)(2,1)} %second.5, bf16[2,960,128]{2,1,0:T(8,128)(2,1)S(1)} %collective-permute-done.first_p, ...), custom_call_target="tpu_custom_call" | custom-call | flops 2000000000 | bytes 2000000 | tf_op jit(solution)/shard_map/pallas_call | solution.py:361
  13.9 8.1 %collective-permute-done.2.second_o = bf16[2,960,128]{2,1,0:T(8,128)(2,1)S(1)} collective-permute-done((bf16[2,960,128]{2,1,0:T(8,128)(2,1)}, bf16[2,960,128]{2,1,0:T(8,128)(2,1)S(1)}, u32[]{:S(2)}, u32[]{:S(2)}) %collective-permute-start.2) | collective-permute-done | bytes 491552 | tf_op jit(solution)/shard_map/ppermute | solution.py:386
  22.0 2.4 %shard_map.48 = (f32[2,8,960]{2,1,0:T(8,128)S(1)}, f32[2,8,960]{2,1,0:T(8,128)S(1)}) custom-call(bf16[2,960,128]{2,1,0:T(8,128)(2,1)S(1)} %collective-permute-done.2.second_o, bf16[2,960,256]{2,1,0:T(8,128)(2,1)S(1)} %get-tuple-element.21.fs, f32[2,8,960]{2,1,0:T(8,128)S(1)} %get-tuple-element.25.fwd0), custom_call_target="tpu_custom_call" | custom-call | flops 1000000000 | bytes 1000000 | tf_op jit(solution)/shard_map/pallas_call | solution.py:361
  24.4 2.9 %collective-permute-done.3.first_o = bf16[2,960,128]{2,1,0:T(8,128)(2,1)S(1)} collective-permute-done((bf16[2,960,128]{2,1,0:T(8,128)(2,1)}, bf16[2,960,128]{2,1,0:T(8,128)(2,1)S(1)}, u32[]{:S(2)}, u32[]{:S(2)}) %collective-permute-start.3) | collective-permute-done | bytes 491552 | tf_op jit(solution)/shard_map/ppermute | solution.py:387
  27.2 61.9 %shard_map.49 = (f32[2,24,480]{2,1,0:T(8,128)S(1)}, f32[2,8,480]{2,1,0:T(8,128)S(1)}) custom-call(bf16[2,960,128]{2,1,0:T(8,128)(2,1)} %first.5, bf16[2,960,128]{2,1,0:T(8,128)(2,1)} %second.5, bf16[2,960,128]{2,1,0:T(8,128)(2,1)S(1)} %collective-permute-done.first_p, bf16[2,960,128]{2,1,0:T(8,128)(2,1)S(1)} %collective-permute-done.1.second_p, ...), custom_call_target="tpu_custom_call" | custom-call | flops 1000000000 | bytes 1000000 | tf_op jit(solution)/shard_map/pallas_call | solution.py:361
  89.2 1.3 %collective-permute-start.5 = (f32[2,24,480]{2,1,0:T(8,128)S(1)}, f32[2,24,480]{2,1,0:T(8,128)S(1)}, u32[]{:S(2)}, u32[]{:S(2)}) collective-permute-start(f32[2,24,480]{2,1,0:T(8,128)S(1)} %get-tuple-element.29.sent), channel_id=1, source_target_pairs={{32,16},{64,48},{96,80},{128,112},{160,144},{192,176},{224,208},{2... | collective-permute-start | bytes 276488 | tf_op jit(solution)/shard_map/ppermute | solution.py:404
  90.5 1.3 %collective-permute-start.4 = (f32[2,8,480]{2,1,0:T(8,128)S(1)}, f32[2,8,480]{2,1,0:T(8,128)S(1)}, u32[]{:S(2)}, u32[]{:S(2)}) collective-permute-start(f32[2,8,480]{2,1,0:T(8,128)S(1)} %get-tuple-element.30), channel_id=1, source_target_pairs={{16,32},{48,64},{80,96},{112,128},{144,160},{176,192},{208,224},{2... | collective-permute-start | bytes 92168 | tf_op jit(solution)/shard_map/ppermute | solution.py:398
  91.8 7.5 %collective-permute-done.4.up = f32[2,8,480]{2,1,0:T(8,128)S(1)} collective-permute-done((f32[2,8,480]{2,1,0:T(8,128)S(1)}, f32[2,8,480]{2,1,0:T(8,128)S(1)}, u32[]{:S(2)}, u32[]{:S(2)}) %collective-permute-start.4) | collective-permute-done | bytes 30752 | tf_op jit(solution)/shard_map/ppermute | solution.py:398
  99.3 0.0 collective-permute-done.5.down
  99.3 0.1 shard_map.50
  99.4 0.0 copy-start.1
  99.4 1.9 %collective-permute-start.6 = (f32[2,4,480]{2,1,0:T(4,128)S(1)}, f32[2,4,480]{2,1,0:T(4,128)S(1)}, u32[]{:S(2)}, u32[]{:S(2)}) collective-permute-start(f32[2,4,480]{2,1,0:T(4,128)S(1)} %get-tuple-element.32), channel_id=1, source_target_pairs={{0,16},{16,0},{32,48},{48,32},{64,80},{80,64},{96,112},{112,96},{1... | collective-permute-start | bytes 46088 | tf_op jit(solution)/shard_map/ppermute | solution.py:407
  101.4 0.0 copy-done.1
  101.4 0.1 maximum_bitcast_fusion
  101.5 0.1 reshape.6.taps
  101.6 0.1 copy.6.bias
  101.6 0.9 collective-permute-done.6.edge
  102.5 0.9 shard_map.51
  (3 shorter events, 0.0 us)
Async XLA Ops:
  0.0 10.9 %copy-start = (f32[4,4,3,3]{1,0,3,2:T(4,128)S(1)}, f32[4,4,3,3]{1,0,3,2:T(4,128)}, u32[]{:S(2)}) copy-start(f32[4,4,3,3]{1,0,3,2:T(4,128)} %param.6) | copy-start | bytes 1732
  0.0 11.0 %collective-permute-start = (bf16[2,960,128]{2,1,0:T(8,128)(2,1)}, bf16[2,960,128]{2,1,0:T(8,128)(2,1)S(1)}, u32[]{:S(2)}, u32[]{:S(2)}) collective-permute-start(bf16[2,960,128]{2,1,0:T(8,128)(2,1)} %first.5), channel_id=1, source_target_pairs={{0,16},{16,0},{32,48},{48,32},{64,80},{80,64},{96,112},{112,96},{1... | collective-permute-start | bytes 1474568 | tf_op jit(solution)/shard_map/ppermute | solution.py:389
  2.1 8.9 %collective-permute-start.1 = (bf16[2,960,128]{2,1,0:T(8,128)(2,1)}, bf16[2,960,128]{2,1,0:T(8,128)(2,1)S(1)}, u32[]{:S(2)}, u32[]{:S(2)}) collective-permute-start(bf16[2,960,128]{2,1,0:T(8,128)(2,1)} %second.5), channel_id=1, source_target_pairs={{0,16},{16,0},{32,48},{48,32},{64,80},{80,64},{96,112},{112,96},{1... | collective-permute-start | bytes 1474568 | tf_op jit(solution)/shard_map/ppermute | solution.py:388
  4.5 17.5 %collective-permute-start.2 = (bf16[2,960,128]{2,1,0:T(8,128)(2,1)}, bf16[2,960,128]{2,1,0:T(8,128)(2,1)S(1)}, u32[]{:S(2)}, u32[]{:S(2)}) collective-permute-start(bf16[2,960,128]{2,1,0:T(8,128)(2,1)} %second.5), channel_id=1, source_target_pairs={{16,32},{48,64},{80,96},{112,128},{144,160},{176,192},{208,224},{2... | collective-permute-start | bytes 1474568 | tf_op jit(solution)/shard_map/ppermute | solution.py:386
  5.8 21.5 %collective-permute-start.3 = (bf16[2,960,128]{2,1,0:T(8,128)(2,1)}, bf16[2,960,128]{2,1,0:T(8,128)(2,1)S(1)}, u32[]{:S(2)}, u32[]{:S(2)}) collective-permute-start(bf16[2,960,128]{2,1,0:T(8,128)(2,1)} %first.5), channel_id=1, source_target_pairs={{16,32},{48,64},{80,96},{112,128},{144,160},{176,192},{208,224},{2... | collective-permute-start | bytes 1474568 | tf_op jit(solution)/shard_map/ppermute | solution.py:387
  89.2 10.2 %collective-permute-start.5 = (f32[2,24,480]{2,1,0:T(8,128)S(1)}, f32[2,24,480]{2,1,0:T(8,128)S(1)}, u32[]{:S(2)}, u32[]{:S(2)}) collective-permute-start(f32[2,24,480]{2,1,0:T(8,128)S(1)} %get-tuple-element.29.sent), channel_id=1, source_target_pairs={{32,16},{64,48},{96,80},{128,112},{160,144},{192,176},{224,208},{2... | collective-permute-start | bytes 276488 | tf_op jit(solution)/shard_map/ppermute | solution.py:404
  90.5 8.8 %collective-permute-start.4 = (f32[2,8,480]{2,1,0:T(8,128)S(1)}, f32[2,8,480]{2,1,0:T(8,128)S(1)}, u32[]{:S(2)}, u32[]{:S(2)}) collective-permute-start(f32[2,8,480]{2,1,0:T(8,128)S(1)} %get-tuple-element.30), channel_id=1, source_target_pairs={{16,32},{48,64},{80,96},{112,128},{144,160},{176,192},{208,224},{2... | collective-permute-start | bytes 92168 | tf_op jit(solution)/shard_map/ppermute | solution.py:398
  99.4 1.9 %copy-start.1 = (f32[4]{0:T(128)S(1)}, f32[4]{0:T(128)}, u32[]{:S(2)}) copy-start(f32[4]{0:T(128)} %param.7) | copy-start | bytes 52
  99.4 3.1 %collective-permute-start.6 = (f32[2,4,480]{2,1,0:T(4,128)S(1)}, f32[2,4,480]{2,1,0:T(4,128)S(1)}, u32[]{:S(2)}, u32[]{:S(2)}) collective-permute-start(f32[2,4,480]{2,1,0:T(4,128)S(1)} %get-tuple-element.32), channel_id=1, source_target_pairs={{0,16},{16,0},{32,48},{48,32},{64,80},{80,64},{96,112},{112,96},{1... | collective-permute-start | bytes 46088 | tf_op jit(solution)/shard_map/ppermute | solution.py:407

commit v4 on v3

--- a/solution.py
+++ b/solution.py
@@ -3,6 +3,7 @@
 
 import jax
 import jax.numpy as jnp
+import numpy as np
 from jax import lax
 from jax.experimental import pallas as pl
 from jax.experimental.pallas import tpu as pltpu
@@ -25,11 +26,16 @@
     return lax.dot_general(a, b, dims, preferred_element_type=jnp.float32)
 
 
+def takes(pos, size):
+    upper = pos == size // 2
+    return upper | ((pos % 2 == 1) & (pos != size // 2 - 1) & (pos != size - 1))
+
+
 def side():
-    pos = lax.axis_index("blk")
+    pos, size = lax.axis_index("blk"), lax.axis_size("blk")
     even = pos % 2 == 0
-    present = jnp.where(even, pos > 0, pos < lax.axis_size("blk") - 1)
-    return even, present
+    present = jnp.where(even, pos > 0, pos < size - 1)
+    return even, takes(pos, size), present
 
 
 def moments():
@@ -181,7 +187,7 @@
 
 
 def chip_kernel(first, second, first_p, second_p, fwd0, bwd0, fs, ss, fwd, bwd, part, up, fp, sp, feats, found, sems):
-    even, _ = side()
+    even, heavy, _ = side()
     near = jnp.where(even, 2.0, -2.0)
 
     def frame(f, _):
@@ -200,7 +206,7 @@
 
     lax.fori_loop(0, FR, frame, 0)
 
-    @pl.when(jnp.logical_not(even))
+    @pl.when(jnp.logical_not(heavy))
     def _():
         for f in range(FR):
             found[f, 0, 0:4, :] = plain(fwd[f])
@@ -214,13 +220,14 @@
             for j in range(2):
                 stat = found[f, j, 0:4, :]
                 part[f, 4 * j : 4 * j + 4, :] = stat
-                up[f, 4 * j : 4 * j + 4, :] = stat[:, W:]
+                up[f, 4 * j : 4 * j + 4, :] = jnp.where(even, stat[:, :W], stat[:, W:])
 
 
 def far_second_kernel(second_o, fs, fwd0, fwd, col, so):
-    even, present = side()
-
-    @pl.when(even & present)
+    even, heavy, _ = side()
+    far = jnp.where(even, -2.0, 2.0)
+
+    @pl.when(heavy)
     def _():
         mom = moments()
 
@@ -228,45 +235,33 @@
             twice_into(so, f, second_o[f])
 
             def down(n0, w, part):
-                fwd[f, :, n0 : n0 + w] = fwd0[f, :, n0 : n0 + w] + shift_y(part, -2.0)
+                fwd[f, :, n0 : n0 + w] = fwd0[f, :, n0 : n0 + w] + shift_y(part, far)
 
             col[f] = sums(so, fs, f, down, mom)
             return 0
 
         lax.fori_loop(0, FR, frame, 0)
 
-    @pl.when(even & jnp.logical_not(present))
+
+def far_first_kernel(height, first, second, first_p, second_p, second_o, first_o, ss, bwd0, fwd, col,
+                     sent, flows, edge, fo, bwd, row, feats, found, sems):
+    even, heavy, _ = side()
+    far = jnp.where(even, -2.0, 2.0)
+
+    @pl.when(heavy)
     def _():
-        fwd[...] = fwd0[...]
-        col[...] = jnp.ones_like(col)
-
-
-def far_first_kernel(height, first, second, first_p, second_p, second_o, first_o, ss, bwd0, fwd, col,
-                     down, flows, fo, bwd, row, feats, found, sems):
-    even, present = side()
-
-    @pl.when(even)
-    def _():
-        @pl.when(present)
-        def _():
-            mom = moments()
-
-            def frame(f, _):
-                split_into(fo, f, first_o[f])
-
-                def keep(n0, w, part):
-                    bwd[f, :, n0 : n0 + w] = bwd0[f, :, n0 : n0 + w] + shift_y(part, -2.0)
-
-                row[f] = sums(fo, ss, f, keep, mom)
-                return 0
-
-            lax.fori_loop(0, FR, frame, 0)
-
-        @pl.when(jnp.logical_not(present))
-        def _():
-            bwd[...] = bwd0[...]
-            row[...] = jnp.ones_like(row)
-
+        mom = moments()
+
+        def frame(f, _):
+            split_into(fo, f, first_o[f])
+
+            def down(n0, w, part):
+                bwd[f, :, n0 : n0 + w] = bwd0[f, :, n0 : n0 + w] + shift_y(part, far)
+
+            row[f] = sums(fo, ss, f, down, mom)
+            return 0
+
+        lax.fori_loop(0, FR, frame, 0)
         for f in range(FR):
             for j, stat in enumerate((fwd, bwd, col, row)):
                 found[f, j, 0:4, :] = plain(stat[f])
@@ -274,70 +269,77 @@
         @pl.when(jnp.logical_not(inside(fwd) & inside(bwd) & inside(col) & inside(row)))
         def _():
             sources = {0: second, 1: second_p, 2: second_o, 3: first, 4: first_p, 5: first_o}
-            exact(sources, feats, found, sems, jnp.where(present, 4, 2), jnp.where(present, 3, 2), 2.0, -2.0)
-
-        for f in range(FR):
+            exact(sources, feats, found, sems, 4, 3, -far, far)
+
+        for f in range(FR):
+            maps = []
             for r in range(2):
-                maps = []
+                both = []
                 for j in range(2):
                     stat = found[f, j, 0:4, :]
                     stat = stat[:, r * W : r * W + W]
-                    maps.extend(finish(stat[1:2], stat[2:3], stat[3:4], float(r), height))
-                maps = jnp.concatenate(maps, axis=0)
-                flows[f, 4 * r : 4 * r + 4, :] = maps
-                if r == 0:
-                    down[f, 16:20, :] = maps
+                    both.extend(finish(stat[1:2], stat[2:3], stat[3:4], float(r), height))
+                maps.append(jnp.concatenate(both, axis=0))
+                flows[f, 4 * r : 4 * r + 4, :] = maps[r]
+            edge[f] = jnp.where(even, maps[1], maps[0])
+            sent[f, 16:20, :] = jnp.where(even, maps[0], maps[1])
             for j in range(2):
                 stat = found[f, 2 + j, 0:4, :]
-                down[f, 8 * j : 8 * j + 4, :] = stat[:, :W]
-                down[f, 8 * j + 4 : 8 * j + 8, :] = stat[:, W:]
-            down[f, 20:24, :] = jnp.zeros((4, W), jnp.float32)
+                sent[f, 8 * j : 8 * j + 4, :] = stat[:, :W]
+                sent[f, 8 * j + 4 : 8 * j + 8, :] = stat[:, W:]
+            sent[f, 20:24, :] = jnp.zeros((4, W), jnp.float32)
 
 
 def flow_kernel(height, part, flows, sent, up, down, rows, edge):
-    even, present = side()
+    even, heavy, present = side()
+    far = jnp.where(even, -2.0, 2.0)
 
     def stat(x, offset):
         return x[0:1], x[1:2], x[2:3], x[3:4] + offset * x[1:2]
 
-    @pl.when(even)
+    def place(f, halo):
+        rows[f, 0:4, :] = jnp.where(even, halo, 0.0)
+        rows[f, 12:16, :] = jnp.where(even, 0.0, halo)
+
+    @pl.when(heavy)
     def _():
         for f in range(FR):
             halo = []
-            for j, mine in ((0, sent[f, 12:16, :]), (1, sent[f, 4:8, :])):
-                _, total, mx, my = merge(stat(up[f, 4 * j : 4 * j + 4, :], 0.0), stat(mine, 2.0))
-                halo.extend(finish(total, mx, my, 1.0, height))
-            rows[f, 0:4, :] = jnp.where(present, jnp.concatenate(halo, axis=0), 0.0)
+            for j in range(2):
+                at = 8 * (1 - j)
+                mine = jnp.where(even, sent[f, at + 4 : at + 8, :], sent[f, at : at + 4, :])
+                _, total, mx, my = merge(stat(up[f, 4 * j : 4 * j + 4, :], 0.0), stat(mine, -far))
+                halo.extend(finish(total, mx, my, jnp.where(even, 1.0, 0.0), height))
+            place(f, jnp.concatenate(halo, axis=0))
             rows[f, 4:12, :] = flows[f]
-            rows[f, 12:16, :] = jnp.zeros((4, W), jnp.float32)
-            edge[f] = flows[f, 4:8, :]
-
-    @pl.when(jnp.logical_not(even))
+
+    @pl.when(jnp.logical_not(heavy))
     def _():
         for f in range(FR):
+            maps = []
             for r in range(2):
-                maps = []
+                both = []
                 for j in range(2):
                     mine = part[f, 4 * j : 4 * j + 4, :]
                     at = 8 * (1 - j) + 4 * r
-                    top, total, mx, my = stat(down[f, at : at + 4, :], 2.0)
+                    top, total, mx, my = stat(down[f, at : at + 4, :], far)
                     other = (jnp.where(present, top, -1e30), total, mx, my)
                     _, total, mx, my = merge(stat(mine[:, r * W : r * W + W], 0.0), other)
-                    maps.extend(finish(total, mx, my, float(r), height))
-                maps = jnp.concatenate(maps, axis=0)
-                rows[f, 4 + 4 * r : 8 + 4 * r, :] = maps
-                if r == 0:
-                    edge[f] = maps
-            rows[f, 0:4, :] = jnp.zeros((4, W), jnp.float32)
-            rows[f, 12:16, :] = jnp.where(present, down[f, 16:20, :], 0.0)
-
-
-def refine_kernel(rows, edge, taps, bias, out):
-    even, _ = side()
+                    both.extend(finish(total, mx, my, float(r), height))
+                maps.append(jnp.concatenate(both, axis=0))
+                rows[f, 4 + 4 * r : 8 + 4 * r, :] = maps[r]
+            edge[f] = jnp.where(even, maps[1], maps[0])
+            place(f, jnp.where(present, down[f, 16:20, :], 0.0))
+
+
+def refine_kernel(rows, edge_heavy, edge_light, taps, bias, out):
+    even, _, _ = side()
+    pos, size = lax.axis_index("blk"), lax.axis_size("blk")
+    from_heavy = takes(jnp.where(even, pos + 1, pos - 1), size)
     none = jnp.zeros((16, 1), jnp.float32)
     for f in range(FR):
         mine = rows[f]
-        other = edge[f]
+        other = jnp.where(from_heavy, edge_heavy[f], edge_light[f])
         full = jnp.concatenate(
             [jnp.where(even, mine[0:4], other), mine[4:12], jnp.where(even, other, mine[12:16])], axis=0
         )
@@ -380,11 +382,13 @@
     spare = [pltpu.VMEM((6, TILE, CH), jnp.bfloat16), pltpu.VMEM((FR, 4, 8, TILE), jnp.float32)]
     spare.append(pltpu.SemaphoreType.DMA((6,)))
     chip = [(i, i ^ 1) for i in range(size)]
-    upward = [(i, i + 1) for i in range(1, size - 1, 2)]
-    downward = [(j, i) for i, j in upward]
-
-    second_o = lax.ppermute(second, "blk", upward)
-    first_o = lax.ppermute(first, "blk", upward)
+    heavy = [bool(takes(np.int32(i), size)) for i in range(size)]
+    pairs = [(i, i + 1) for i in range(1, size - 1, 2)]
+    toward = [(j, i) if heavy[i] else (i, j) for i, j in pairs]
+    back = [(j, i) for i, j in toward]
+
+    second_o = lax.ppermute(second, "blk", toward)
+    first_o = lax.ppermute(first, "blk", toward)
     second_p = lax.ppermute(second, "blk", chip)
     first_p = lax.ppermute(first, "blk", chip)
     first, second = (pltpu.with_memory_space_constraint(x, pltpu.HBM) for x in (first, second))
@@ -395,21 +399,23 @@
                             first, second, hbm=(0, 1))
     fwd, bwd, part, up = call(chip_kernel, (stats, stats, stats, f32((FR, 8, W))), [wide, wide] + spare, 20,
                               2 * 10**9, first, second, first_p, second_p, fwd, bwd, fs, ss, hbm=(0, 1))
-    up = lax.ppermute(up, "blk", upward)
+    up = lax.ppermute(up, "blk", toward)
     fwd, col = call(far_second_kernel, (stats, stats), [wide], 12, 10**9, second_o, fs, fwd)
-    sent, flows = call(functools.partial(far_first_kernel, height), (f32((FR, 24, W)), f32((FR, 8, W))),
-                       [wide, kept, kept] + spare, 20, 10**9,
-                       first, second, first_p, second_p, second_o, first_o, ss, bwd, fwd, col,
-                       hbm=(0, 1), far=(2, 3, 4))
-    down = lax.ppermute(sent, "blk", downward)
+    sent, flows, edge = call(functools.partial(far_first_kernel, height),
+                             (f32((FR, 24, W)), f32((FR, 8, W)), f32((FR, 4, W))),
+                             [wide, kept, kept] + spare, 20, 10**9,
+                             first, second, first_p, second_p, second_o, first_o, ss, bwd, fwd, col,
+                             hbm=(0, 1), far=(2, 3, 4))
+    down = lax.ppermute(sent, "blk", back)
+    edge_heavy = lax.ppermute(edge, "blk", [c for c in chip if heavy[c[0]]])
     rows, edge = call(functools.partial(flow_kernel, height), (f32((FR, 16, W)), f32((FR, 4, W))), [], 4, 10**6,
                       part, flows, sent, up, down)
-    other = lax.ppermute(edge, "blk", chip)
+    edge_light = lax.ppermute(edge, "blk", [c for c in chip if not heavy[c[0]]])
     taps = conv_weight.transpose(0, 3, 2, 1)
     taps = jnp.stack([jnp.pad(taps, ((0, 0), (0, 0), (r, 1 - r), (0, 0))) for r in range(2)])
     taps = taps.reshape(8, 48)
     bias = jnp.concatenate([conv_bias, conv_bias]).reshape(8, 1)
-    return call(refine_kernel, f32((FR, 4, 2, W)), [], 4, 10**6, rows, other, taps, bias)
+    return call(refine_kernel, f32((FR, 4, 2, W)), [], 4, 10**6, rows, edge_heavy, edge_light, taps, bias)
 
 
 def solution(mesh):

time: 104 us -> 102 us (0.981)
  the two profiles are of different devices: /device:TPU:38 before, /device:TPU:14 now
where the time goes in v4:
time: 102 us; the launch traced here: 101 us
  Pallas kernels  72.1 us (71%)
  waiting for transfers between devices  16.6 us (16%)
  starting transfers between devices  12.2 us (12%)
    pallas_call x6, Pallas kernels, call(): pl.pallas_call(kernel, out_shape=shapes, in_specs=[home if i in hbm else...  72.1 us
    ppermute x1, waiting for transfers between devices, device_program(): second_o = lax.ppermute(second, 'blk', toward)  8.08 us
    ppermute x1, waiting for transfers between devices, device_program(): up = lax.ppermute(up, 'blk', toward)  5.6 us
    ppermute x1, waiting for transfers between devices, device_program(): first_o = lax.ppermute(first, 'blk', toward)  2.88 us
    ppermute x1, starting transfers between devices, device_program(): second_p = lax.ppermute(second, 'blk', chip)  2.41 us
    ppermute x1, starting transfers between devices, device_program(): first_p = lax.ppermute(first, 'blk', chip)  2.04 us
  transfers between devices with their start and end apart: 8, of which 3 were waited for; matrix products, arithmetic and copies ran while one was open for 0% of the time, Pallas kernels for 9%

profile of v4, /device:TPU:14, one launch (start us, length us, event | category | flops | bytes accessed | tf_op | source)
XLA Modules:
  0.0 101.3 jit_solution(12374554075280936755)
XLA Ops:
  0.0 0.0 copy-start
  0.0 2.0 %collective-permute-start = (bf16[2,960,128]{2,1,0:T(8,128)(2,1)}, bf16[2,960,128]{2,1,0:T(8,128)(2,1)S(1)}, u32[]{:S(2)}, u32[]{:S(2)}) collective-permute-start(bf16[2,960,128]{2,1,0:T(8,128)(2,1)} %first.5), channel_id=1, source_target_pairs={{0,16},{16,0},{32,48},{48,32},{64,80},{80,64},{96,112},{112,96},{1... | collective-permute-start | bytes 1474568 | tf_op jit(solution)/shard_map/ppermute | solution.py:393
  2.1 2.4 %collective-permute-start.1 = (bf16[2,960,128]{2,1,0:T(8,128)(2,1)}, bf16[2,960,128]{2,1,0:T(8,128)(2,1)S(1)}, u32[]{:S(2)}, u32[]{:S(2)}) collective-permute-start(bf16[2,960,128]{2,1,0:T(8,128)(2,1)} %second.5), channel_id=1, source_target_pairs={{0,16},{16,0},{32,48},{48,32},{64,80},{80,64},{96,112},{112,96},{1... | collective-permute-start | bytes 1474568 | tf_op jit(solution)/shard_map/ppermute | solution.py:392
  4.5 1.3 %collective-permute-start.2 = (bf16[2,960,128]{2,1,0:T(8,128)(2,1)}, bf16[2,960,128]{2,1,0:T(8,128)(2,1)S(1)}, u32[]{:S(2)}, u32[]{:S(2)}) collective-permute-start(bf16[2,960,128]{2,1,0:T(8,128)(2,1)} %second.5), channel_id=1, source_target_pairs={{32,16},{64,48},{96,80},{128,112},{160,144},{192,176},{224,208},{2... | collective-permute-start | bytes 1474568 | tf_op jit(solution)/shard_map/ppermute | solution.py:390
  5.8 1.3 %collective-permute-start.3 = (bf16[2,960,128]{2,1,0:T(8,128)(2,1)}, bf16[2,960,128]{2,1,0:T(8,128)(2,1)S(1)}, u32[]{:S(2)}, u32[]{:S(2)}) collective-permute-start(bf16[2,960,128]{2,1,0:T(8,128)(2,1)} %first.5), channel_id=1, source_target_pairs={{32,16},{64,48},{96,80},{128,112},{160,144},{192,176},{224,208},{2... | collective-permute-start | bytes 1474568 | tf_op jit(solution)/shard_map/ppermute | solution.py:391
  7.1 3.8 %shard_map.46 = (f32[2,8,960]{2,1,0:T(8,128)S(1)}, f32[2,8,960]{2,1,0:T(8,128)S(1)}, bf16[2,960,256]{2,1,0:T(8,128)(2,1)S(1)}, bf16[2,960,256]{2,1,0:T(8,128)(2,1)S(1)}) custom-call(bf16[2,960,128]{2,1,0:T(8,128)(2,1)} %first.5, bf16[2,960,128]{2,1,0:T(8,128)(2,1)} %second.5), custom_call_target="tpu_custom_call" | custom-call | flops 1000000000 | bytes 1000000 | tf_op jit(solution)/shard_map/pallas_call | solution.py:363
  10.9 0.0 copy-done
  11.0 0.0 collective-permute-done.first_p
  11.0 0.0 collective-permute-done.1.second_p
  11.0 2.9 %shard_map.47 = (f32[2,8,960]{2,1,0:T(8,128)S(1)}, f32[2,8,960]{2,1,0:T(8,128)S(1)}, f32[2,8,960]{2,1,0:T(8,128)S(1)}, f32[2,8,480]{2,1,0:T(8,128)S(1)}) custom-call(bf16[2,960,128]{2,1,0:T(8,128)(2,1)} %first.5, bf16[2,960,128]{2,1,0:T(8,128)(2,1)} %second.5, bf16[2,960,128]{2,1,0:T(8,128)(2,1)S(1)} %collective-permute-done.first_p, ...), custom_call_target="tpu_custom_call" | custom-call | flops 2000000000 | bytes 2000000 | tf_op jit(solution)/shard_map/pallas_call | solution.py:363
  13.9 8.1 %collective-permute-done.2.second_o = bf16[2,960,128]{2,1,0:T(8,128)(2,1)S(1)} collective-permute-done((bf16[2,960,128]{2,1,0:T(8,128)(2,1)}, bf16[2,960,128]{2,1,0:T(8,128)(2,1)S(1)}, u32[]{:S(2)}, u32[]{:S(2)}) %collective-permute-start.2) | collective-permute-done | bytes 491552 | tf_op jit(solution)/shard_map/ppermute | solution.py:390
  22.0 2.4 %shard_map.48 = (f32[2,8,960]{2,1,0:T(8,128)S(1)}, f32[2,8,960]{2,1,0:T(8,128)S(1)}) custom-call(bf16[2,960,128]{2,1,0:T(8,128)(2,1)S(1)} %collective-permute-done.2.second_o, bf16[2,960,256]{2,1,0:T(8,128)(2,1)S(1)} %get-tuple-element.22.fs, f32[2,8,960]{2,1,0:T(8,128)S(1)} %get-tuple-element.26.fwd0), custom_call_target="tpu_custom_call" | custom-call | flops 1000000000 | bytes 1000000 | tf_op jit(solution)/shard_map/pallas_call | solution.py:363
  24.4 2.9 %collective-permute-done.3.first_o = bf16[2,960,128]{2,1,0:T(8,128)(2,1)S(1)} collective-permute-done((bf16[2,960,128]{2,1,0:T(8,128)(2,1)}, bf16[2,960,128]{2,1,0:T(8,128)(2,1)S(1)}, u32[]{:S(2)}, u32[]{:S(2)}) %collective-permute-start.3) | collective-permute-done | bytes 491552 | tf_op jit(solution)/shard_map/ppermute | solution.py:391
  27.2 61.9 %shard_map.49 = (f32[2,24,480]{2,1,0:T(8,128)S(1)}, f32[2,8,480]{2,1,0:T(8,128)S(1)}, f32[2,4,480]{2,1,0:T(4,128)S(1)}) custom-call(bf16[2,960,128]{2,1,0:T(8,128)(2,1)} %first.5, bf16[2,960,128]{2,1,0:T(8,128)(2,1)} %second.5, bf16[2,960,128]{2,1,0:T(8,128)(2,1)S(1)} %collective-permute-done.first_p, ...), custom_call_target="tpu_custom_call" | custom-call | flops 1000000000 | bytes 1000000 | tf_op jit(solution)/shard_map/pallas_call | solution.py:363
  89.1 1.3 %collective-permute-start.5 = (f32[2,24,480]{2,1,0:T(8,128)S(1)}, f32[2,24,480]{2,1,0:T(8,128)S(1)}, u32[]{:S(2)}, u32[]{:S(2)}) collective-permute-start(f32[2,24,480]{2,1,0:T(8,128)S(1)} %get-tuple-element.30.sent), channel_id=1, source_target_pairs={{16,32},{48,64},{80,96},{112,128},{144,160},{176,192},{208,224},{2... | collective-permute-start | bytes 276488 | tf_op jit(solution)/shard_map/ppermute | solution.py:409
  90.4 1.3 %collective-permute-start.4 = (f32[2,8,480]{2,1,0:T(8,128)S(1)}, f32[2,8,480]{2,1,0:T(8,128)S(1)}, u32[]{:S(2)}, u32[]{:S(2)}) collective-permute-start(f32[2,8,480]{2,1,0:T(8,128)S(1)} %get-tuple-element.31), channel_id=1, source_target_pairs={{32,16},{64,48},{96,80},{128,112},{160,144},{192,176},{224,208},{2... | collective-permute-start | bytes 92168 | tf_op jit(solution)/shard_map/ppermute | solution.py:402
  91.8 1.9 %collective-permute-start.6 = (f32[2,4,480]{2,1,0:T(4,128)S(1)}, f32[2,4,480]{2,1,0:T(4,128)S(1)}, u32[]{:S(2)}, u32[]{:S(2)}) collective-permute-start(f32[2,4,480]{2,1,0:T(4,128)S(1)} %get-tuple-element.33), channel_id=1, source_target_pairs={{16,0},{48,32},{80,64},{112,96},{144,128},{176,160},{208,192},{256... | collective-permute-start | bytes 46088 | tf_op jit(solution)/shard_map/ppermute | solution.py:410
  93.7 5.6 %collective-permute-done.4.up = f32[2,8,480]{2,1,0:T(8,128)S(1)} collective-permute-done((f32[2,8,480]{2,1,0:T(8,128)S(1)}, f32[2,8,480]{2,1,0:T(8,128)S(1)}, u32[]{:S(2)}, u32[]{:S(2)}) %collective-permute-start.4) | collective-permute-done | bytes 30752 | tf_op jit(solution)/shard_map/ppermute | solution.py:402
  99.3 0.0 collective-permute-done.5.down
  99.3 0.1 shard_map.50
  99.4 0.0 copy-start.1
  99.4 0.7 collective-permute-start.7
  100.1 0.0 copy-done.1
  100.1 0.1 maximum_bitcast_fusion
  100.2 0.1 reshape.6.taps
  100.3 0.1 copy.6.bias
  100.4 0.0 collective-permute-done.6.edge_heavy
  100.4 0.0 collective-permute-done.7.edge_light
  100.4 0.9 shard_map.51
  (3 shorter events, 0.0 us)
Async XLA Ops:
  0.0 10.9 %copy-start = (f32[4,4,3,3]{1,0,3,2:T(4,128)S(1)}, f32[4,4,3,3]{1,0,3,2:T(4,128)}, u32[]{:S(2)}) copy-start(f32[4,4,3,3]{1,0,3,2:T(4,128)} %param.6) | copy-start | bytes 1732
  0.0 11.0 %collective-permute-start = (bf16[2,960,128]{2,1,0:T(8,128)(2,1)}, bf16[2,960,128]{2,1,0:T(8,128)(2,1)S(1)}, u32[]{:S(2)}, u32[]{:S(2)}) collective-permute-start(bf16[2,960,128]{2,1,0:T(8,128)(2,1)} %first.5), channel_id=1, source_target_pairs={{0,16},{16,0},{32,48},{48,32},{64,80},{80,64},{96,112},{112,96},{1... | collective-permute-start | bytes 1474568 | tf_op jit(solution)/shard_map/ppermute | solution.py:393
  2.1 8.9 %collective-permute-start.1 = (bf16[2,960,128]{2,1,0:T(8,128)(2,1)}, bf16[2,960,128]{2,1,0:T(8,128)(2,1)S(1)}, u32[]{:S(2)}, u32[]{:S(2)}) collective-permute-start(bf16[2,960,128]{2,1,0:T(8,128)(2,1)} %second.5), channel_id=1, source_target_pairs={{0,16},{16,0},{32,48},{48,32},{64,80},{80,64},{96,112},{112,96},{1... | collective-permute-start | bytes 1474568 | tf_op jit(solution)/shard_map/ppermute | solution.py:392
  4.5 17.5 %collective-permute-start.2 = (bf16[2,960,128]{2,1,0:T(8,128)(2,1)}, bf16[2,960,128]{2,1,0:T(8,128)(2,1)S(1)}, u32[]{:S(2)}, u32[]{:S(2)}) collective-permute-start(bf16[2,960,128]{2,1,0:T(8,128)(2,1)} %second.5), channel_id=1, source_target_pairs={{32,16},{64,48},{96,80},{128,112},{160,144},{192,176},{224,208},{2... | collective-permute-start | bytes 1474568 | tf_op jit(solution)/shard_map/ppermute | solution.py:390
  5.8 21.5 %collective-permute-start.3 = (bf16[2,960,128]{2,1,0:T(8,128)(2,1)}, bf16[2,960,128]{2,1,0:T(8,128)(2,1)S(1)}, u32[]{:S(2)}, u32[]{:S(2)}) collective-permute-start(bf16[2,960,128]{2,1,0:T(8,128)(2,1)} %first.5), channel_id=1, source_target_pairs={{32,16},{64,48},{96,80},{128,112},{160,144},{192,176},{224,208},{2... | collective-permute-start | bytes 1474568 | tf_op jit(solution)/shard_map/ppermute | solution.py:391
  89.1 10.2 %collective-permute-start.5 = (f32[2,24,480]{2,1,0:T(8,128)S(1)}, f32[2,24,480]{2,1,0:T(8,128)S(1)}, u32[]{:S(2)}, u32[]{:S(2)}) collective-permute-start(f32[2,24,480]{2,1,0:T(8,128)S(1)} %get-tuple-element.30.sent), channel_id=1, source_target_pairs={{16,32},{48,64},{80,96},{112,128},{144,160},{176,192},{208,224},{2... | collective-permute-start | bytes 276488 | tf_op jit(solution)/shard_map/ppermute | solution.py:409
  90.4 8.8 %collective-permute-start.4 = (f32[2,8,480]{2,1,0:T(8,128)S(1)}, f32[2,8,480]{2,1,0:T(8,128)S(1)}, u32[]{:S(2)}, u32[]{:S(2)}) collective-permute-start(f32[2,8,480]{2,1,0:T(8,128)S(1)} %get-tuple-element.31), channel_id=1, source_target_pairs={{32,16},{64,48},{96,80},{128,112},{160,144},{192,176},{224,208},{2... | collective-permute-start | bytes 92168 | tf_op jit(solution)/shard_map/ppermute | solution.py:402
  91.8 8.6 %collective-permute-start.6 = (f32[2,4,480]{2,1,0:T(4,128)S(1)}, f32[2,4,480]{2,1,0:T(4,128)S(1)}, u32[]{:S(2)}, u32[]{:S(2)}) collective-permute-start(f32[2,4,480]{2,1,0:T(4,128)S(1)} %get-tuple-element.33), channel_id=1, source_target_pairs={{16,0},{48,32},{80,64},{112,96},{144,128},{176,160},{208,192},{256... | collective-permute-start | bytes 46088 | tf_op jit(solution)/shard_map/ppermute | solution.py:410
  99.4 0.7 copy-start.1
  99.4 0.9 collective-permute-start.7

commit v5 on v4

--- a/solution.py
+++ b/solution.py
@@ -106,20 +106,22 @@
     return (mom_x / total - col) * (2.0 / W), (mom_y / total - row) * (2.0 / height)
 
 
-def own_kernel(first, second, fwd, bwd, fs, ss, fbuf, sbuf, sems):
-    copies = []
-    for f in range(FR):
-        for k, (src, dst) in enumerate(((first, fbuf), (second, sbuf))):
-            copies.append(pltpu.make_async_copy(src.at[f], dst.at[f], sems.at[2 * f + k]))
+def load_kernel(first, second, both, first0, first1, sems):
+    pairs = [(first.at[f], both.at[0, f]) for f in range(FR)] + [(second.at[f], both.at[1, f]) for f in range(FR)]
+    pairs = [(first.at[0], first0), (first.at[1], first1)] + pairs
+    copies = [pltpu.make_async_copy(src, dst, sems.at[k]) for k, (src, dst) in enumerate(pairs)]
     for c in copies:
         c.start()
-    mom = moments()
     for c in copies:
         c.wait()
 
+
+def own_kernel(both, fwd, bwd, fs, ss):
+    mom = moments()
+
     def frame(f, _):
-        split_into(fs, f, fbuf[f])
-        twice_into(ss, f, sbuf[f])
+        split_into(fs, f, both[0, f])
+        twice_into(ss, f, both[1, f])
 
         def down(n0, w, part):
             fwd[f, :, n0 : n0 + w] = part
@@ -182,17 +184,22 @@
     lax.fori_loop(0, FR, frame, 0)
 
 
+def tiles_of(both, both_p):
+    return {0: both.at[1], 1: both_p.at[1], 3: both.at[0], 4: both_p.at[0]}
+
+
 def plain(part):
     return jnp.concatenate([jnp.zeros_like(part[0:1]), part[0:3]], axis=0)
 
 
-def chip_kernel(first, second, first_p, second_p, fwd0, bwd0, fs, ss, fwd, bwd, part, up, fp, sp, feats, found, sems):
+def chip_kernel(both, both_p, fwd0, bwd0, fs, fwd, bwd, part, up, ss, fp, sp, feats, found, sems):
     even, heavy, _ = side()
     near = jnp.where(even, 2.0, -2.0)
 
     def frame(f, _):
-        split_into(fp, f, first_p[f])
-        twice_into(sp, f, second_p[f])
+        twice_into(ss, f, both[1, f])
+        split_into(fp, f, both_p[0, f])
+        twice_into(sp, f, both_p[1, f])
 
         def down_f(n0, w, part):
             fwd[f, :, n0 : n0 + w] = fwd0[f, :, n0 : n0 + w] + shift_y(part, near)
@@ -214,7 +221,7 @@
 
         @pl.when(jnp.logical_not(inside(fwd) & inside(bwd)))
         def _():
-            exact({0: second, 1: second_p, 3: first, 4: first_p}, feats, found, sems, 2, 2, near, near)
+            exact(tiles_of(both, both_p), feats, found, sems, 2, 2, near, near)
 
         for f in range(FR):
             for j in range(2):
@@ -223,7 +230,7 @@
                 up[f, 4 * j : 4 * j + 4, :] = jnp.where(even, stat[:, :W], stat[:, W:])
 
 
-def far_second_kernel(second_o, fs, fwd0, fwd, col, so):
+def far_second_kernel(second_o, fs, fwd0, taps, bias, fwd, col, so):
     even, heavy, _ = side()
     far = jnp.where(even, -2.0, 2.0)
 
@@ -243,43 +250,59 @@
         lax.fori_loop(0, FR, frame, 0)
 
 
-def far_first_kernel(height, first, second, first_p, second_p, second_o, first_o, ss, bwd0, fwd, col,
-                     sent, flows, edge, fo, bwd, row, feats, found, sems):
+def far_first(f, first_o, both, bwd0, bwd, row, fo, ss, far):
+    split_into(fo, 0, first_o[...])
+    twice_into(ss, 0, both[1, f])
+
+    def down(n0, w, part):
+        bwd[:, n0 : n0 + w] = bwd0[f, :, n0 : n0 + w] + shift_y(part, far)
+
+    row[...] = sums(fo, ss, 0, down, moments())
+
+
+def far_first0_kernel(first_o, both, bwd0, bwd, row, fo, ss):
+    even, heavy, _ = side()
+
+    @pl.when(heavy)
+    def _():
+        far_first(0, first_o, both, bwd0, bwd, row, fo, ss, jnp.where(even, -2.0, 2.0))
+
+
+def far_first1_kernel(height, both, both_p, second_o, first_o0, first_o1, bwd0, fwd, col, bwd1, row1,
+                      sent, flows, edge, fo, ss, bwd, row, feats, found, stage, sems):
     even, heavy, _ = side()
     far = jnp.where(even, -2.0, 2.0)
 
     @pl.when(heavy)
     def _():
-        mom = moments()
-
-        def frame(f, _):
-            split_into(fo, f, first_o[f])
-
-            def down(n0, w, part):
-                bwd[f, :, n0 : n0 + w] = bwd0[f, :, n0 : n0 + w] + shift_y(part, far)
-
-            row[f] = sums(fo, ss, f, down, mom)
-            return 0
-
-        lax.fori_loop(0, FR, frame, 0)
+        bwd[0] = bwd1[...]
+        row[0] = row1[...]
+        far_first(1, first_o1, both, bwd0, bwd.at[1], row.at[1], fo, ss, far)
         for f in range(FR):
             for j, stat in enumerate((fwd, bwd, col, row)):
                 found[f, j, 0:4, :] = plain(stat[f])
 
         @pl.when(jnp.logical_not(inside(fwd) & inside(bwd) & inside(col) & inside(row)))
         def _():
-            sources = {0: second, 1: second_p, 2: second_o, 3: first, 4: first_p, 5: first_o}
+            copies = [
+                pltpu.make_async_copy(src, stage.at[f], sems.at[f]) for f, src in enumerate((first_o0, first_o1))
+            ]
+            for c in copies:
+                c.start()
+            for c in copies:
+                c.wait()
+            sources = {**tiles_of(both, both_p), 2: second_o, 5: stage}
             exact(sources, feats, found, sems, 4, 3, -far, far)
 
         for f in range(FR):
             maps = []
             for r in range(2):
-                both = []
+                pieces = []
                 for j in range(2):
                     stat = found[f, j, 0:4, :]
                     stat = stat[:, r * W : r * W + W]
-                    both.extend(finish(stat[1:2], stat[2:3], stat[3:4], float(r), height))
-                maps.append(jnp.concatenate(both, axis=0))
+                    pieces.extend(finish(stat[1:2], stat[2:3], stat[3:4], float(r), height))
+                maps.append(jnp.concatenate(pieces, axis=0))
                 flows[f, 4 * r : 4 * r + 4, :] = maps[r]
             edge[f] = jnp.where(even, maps[1], maps[0])
             sent[f, 16:20, :] = jnp.where(even, maps[0], maps[1])
@@ -318,15 +341,15 @@
         for f in range(FR):
             maps = []
             for r in range(2):
-                both = []
+                pieces = []
                 for j in range(2):
                     mine = part[f, 4 * j : 4 * j + 4, :]
                     at = 8 * (1 - j) + 4 * r
                     top, total, mx, my = stat(down[f, at : at + 4, :], far)
                     other = (jnp.where(present, top, -1e30), total, mx, my)
                     _, total, mx, my = merge(stat(mine[:, r * W : r * W + W], 0.0), other)
-                    both.extend(finish(total, mx, my, float(r), height))
-                maps.append(jnp.concatenate(both, axis=0))
+                    pieces.extend(finish(total, mx, my, float(r), height))
+                maps.append(jnp.concatenate(pieces, axis=0))
                 rows[f, 4 + 4 * r : 8 + 4 * r, :] = maps[r]
             edge[f] = jnp.where(even, maps[1], maps[0])
             place(f, jnp.where(present, down[f, 16:20, :], 0.0))
@@ -355,7 +378,7 @@
             out[f, o, 1:2, :] = mixed[4 + o : 5 + o]
 
 
-def call(kernel, shapes, scratch, limit, flops, *args, hbm=(), far=(), alias={}):
+def call(kernel, shapes, scratch, limit, flops, *args, hbm=(), far=()):
     spec = pl.BlockSpec(memory_space=pltpu.VMEM)
     anywhere = pl.BlockSpec(memory_space=pl.ANY)
     home = pl.BlockSpec(memory_space=pltpu.HBM)
@@ -366,7 +389,6 @@
         in_specs=[home if i in hbm else anywhere if i in far else spec for i in range(len(args))],
         out_specs=spec if single else (spec,) * len(shapes),
         scratch_shapes=scratch,
-        input_output_aliases=alias,
         compiler_params=pltpu.CompilerParams(vmem_limit_bytes=limit << 20),
         cost_estimate=pl.CostEstimate(flops=flops, bytes_accessed=flops // 1000, transcendentals=0),
     )(*args)
@@ -387,34 +409,39 @@
     toward = [(j, i) if heavy[i] else (i, j) for i, j in pairs]
     back = [(j, i) for i, j in toward]
 
+    taps = conv_weight.transpose(0, 3, 2, 1)
+    taps = jnp.stack([jnp.pad(taps, ((0, 0), (0, 0), (r, 1 - r), (0, 0))) for r in range(2)])
+    taps = taps.reshape(8, 48)
+    bias = jnp.concatenate([conv_bias, conv_bias]).reshape(8, 1)
     second_o = lax.ppermute(second, "blk", toward)
-    first_o = lax.ppermute(first, "blk", toward)
-    second_p = lax.ppermute(second, "blk", chip)
-    first_p = lax.ppermute(first, "blk", chip)
     first, second = (pltpu.with_memory_space_constraint(x, pltpu.HBM) for x in (first, second))
-    stats = f32((FR, 8, TILE))
+    tile = jax.ShapeDtypeStruct((TILE, CH), jnp.bfloat16)
+    loaded = jax.ShapeDtypeStruct((2, FR, TILE, CH), jnp.bfloat16)
+    both, first0, first1 = call(load_kernel, (loaded, tile, tile), [pltpu.SemaphoreType.DMA((6,))], 4, 10**6,
+                                first, second, hbm=(0, 1))
+    first_o0 = lax.ppermute(first0, "blk", toward)
+    first_o1 = lax.ppermute(first1, "blk", toward)
+    both_p = lax.ppermute(both, "blk", chip)
+    stats, frame = f32((FR, 8, TILE)), f32((8, TILE))
     doubled = jax.ShapeDtypeStruct((FR, TILE, 2 * CH), jnp.bfloat16)
-    fwd, bwd, fs, ss = call(own_kernel, (stats, stats, doubled, doubled),
-                            [narrow, narrow, pltpu.SemaphoreType.DMA((4,))], 12, 10**9,
-                            first, second, hbm=(0, 1))
-    fwd, bwd, part, up = call(chip_kernel, (stats, stats, stats, f32((FR, 8, W))), [wide, wide] + spare, 20,
-                              2 * 10**9, first, second, first_p, second_p, fwd, bwd, fs, ss, hbm=(0, 1))
+    own_out = (stats, stats, doubled)
+    fwd, bwd, fs = call(own_kernel, own_out, [wide], 8, 10**9, both)
+    fwd, bwd, part, up = call(chip_kernel, (stats, stats, stats, f32((FR, 8, W))), [wide] * 3 + spare, 16,
+                              2 * 10**9, both, both_p, fwd, bwd, fs)
     up = lax.ppermute(up, "blk", toward)
-    fwd, col = call(far_second_kernel, (stats, stats), [wide], 12, 10**9, second_o, fs, fwd)
-    sent, flows, edge = call(functools.partial(far_first_kernel, height),
+    fwd, col = call(far_second_kernel, (stats, stats), [wide], 8, 10**9, second_o, fs, fwd, taps, bias)
+    single = pltpu.VMEM((1, TILE, 2 * CH), jnp.bfloat16)
+    bwd1, row1 = call(far_first0_kernel, (frame, frame), [single] * 2, 8, 5 * 10**8, first_o0, both, bwd)
+    sent, flows, edge = call(functools.partial(far_first1_kernel, height),
                              (f32((FR, 24, W)), f32((FR, 8, W)), f32((FR, 4, W))),
-                             [wide, kept, kept] + spare, 20, 10**9,
-                             first, second, first_p, second_p, second_o, first_o, ss, bwd, fwd, col,
-                             hbm=(0, 1), far=(2, 3, 4))
+                             [single, single, kept, kept] + spare[:2] + [narrow] + spare[2:], 12, 5 * 10**8,
+                             both, both_p, second_o, first_o0, first_o1, bwd, fwd, col, bwd1, row1,
+                             far=(1, 2))
     down = lax.ppermute(sent, "blk", back)
     edge_heavy = lax.ppermute(edge, "blk", [c for c in chip if heavy[c[0]]])
     rows, edge = call(functools.partial(flow_kernel, height), (f32((FR, 16, W)), f32((FR, 4, W))), [], 4, 10**6,
                       part, flows, sent, up, down)
     edge_light = lax.ppermute(edge, "blk", [c for c in chip if not heavy[c[0]]])
-    taps = conv_weight.transpose(0, 3, 2, 1)
-    taps = jnp.stack([jnp.pad(taps, ((0, 0), (0, 0), (r, 1 - r), (0, 0))) for r in range(2)])
-    taps = taps.reshape(8, 48)
-    bias = jnp.concatenate([conv_bias, conv_bias]).reshape(8, 1)
     return call(refine_kernel, f32((FR, 4, 2, W)), [], 4, 10**6, rows, edge_heavy, edge_light, taps, bias)
 
 

time: 102 us -> 102 us (level)
  Pallas kernels: 72.1 us -> 73.7 us
  starting transfers between devices: 12.2 us -> 11 us
    ppermute x1, waiting for transfers between devices: 8.08 us -> 0.01 us  [device_program(): second_o = lax.ppermute(second, 'blk', toward)]
    ppermute x3, waiting for transfers between devices: 2.88 us -> 10.3 us  [the longest x1 10.3 us: device_program(): first_o0 = lax.ppermute(first0, 'blk', toward)]
    pallas_call x6 -> x8, Pallas kernels: 72.1 us -> 73.7 us  [call(): pl.pallas_call(kernel, out_shape=shapes, in_specs=[home if i in hbm else...]
    ppermute x3, starting transfers between devices: 5.74 us -> 4.5 us  [the longest x1 1.92 us: device_program(): both_p = lax.ppermute(both, 'blk', chip)]
  transfers between devices with their start and end apart: 8 -> 8, of which waited for: 3 -> 2; matrix products, arithmetic and copies ran while one was open for 0% -> 0% of each run, Pallas kernels for 9% -> 9%
where the time goes in v5:
time: 102 us
  Pallas kernels  73.7 us (72%)
  waiting for transfers between devices  15.9 us (16%)
  starting transfers between devices  11 us (11%)
    pallas_call x8, Pallas kernels, call(): pl.pallas_call(kernel, out_shape=shapes, in_specs=[home if i in hbm else...  73.7 us
    ppermute x1, waiting for transfers between devices, device_program(): first_o0 = lax.ppermute(first0, 'blk', toward)  10.3 us
    ppermute x1, waiting for transfers between devices, device_program(): up = lax.ppermute(up, 'blk', toward)  5.62 us
  transfers between devices with their start and end apart: 8, of which 2 were waited for; matrix products, arithmetic and copies ran while one was open for 0% of the time, Pallas kernels for 9%

profile of v5, /device:TPU:14, one launch (start us, length us, event | category | flops | bytes accessed | tf_op | source)
XLA Modules:
  0.0 101.6 jit_solution(4122841291626000815)
XLA Ops:
  0.0 0.0 copy-start
  0.0 1.5 %shard_map.46 = (bf16[2,2,960,128]{3,2,1,0:T(8,128)(2,1)S(1)}, bf16[960,128]{1,0:T(8,128)(2,1)S(1)}, bf16[960,128]{1,0:T(8,128)(2,1)S(1)}) custom-call(bf16[2,960,128]{2,1,0:T(8,128)(2,1)} %first.1, bf16[2,960,128]{2,1,0:T(8,128)(2,1)} %second.1), custom_call_target="tpu_custom_call" | custom-call | flops 1000000 | bytes 1000 | tf_op jit(solution)/shard_map/pallas_call | solution.py:386
  1.5 1.9 %collective-permute-start = (bf16[2,2,960,128]{3,2,1,0:T(8,128)(2,1)S(1)}, bf16[2,2,960,128]{3,2,1,0:T(8,128)(2,1)S(1)}, u32[]{:S(2)}, u32[]{:S(2)}) collective-permute-start(bf16[2,2,960,128]{3,2,1,0:T(8,128)(2,1)S(1)} %get-tuple-element.24.both), channel_id=1, source_target_pairs={{0,16},{16,0},{32,48},{48,32},{64,80},{80,64},{96,112},{112,96},{1... | collective-permute-start | bytes 2949128 | tf_op jit(solution)/shard_map/ppermute | solution.py:424
  3.5 1.3 %collective-permute-start.1 = (bf16[2,960,128]{2,1,0:T(8,128)(2,1)}, bf16[2,960,128]{2,1,0:T(8,128)(2,1)S(1)}, u32[]{:S(2)}, u32[]{:S(2)}) collective-permute-start(bf16[2,960,128]{2,1,0:T(8,128)(2,1)} %second.1), channel_id=1, source_target_pairs={{32,16},{64,48},{96,80},{128,112},{160,144},{192,176},{224,208},{2... | collective-permute-start | bytes 1474568 | tf_op jit(solution)/shard_map/ppermute | solution.py:416
  4.8 1.3 %collective-permute-start.2 = (bf16[960,128]{1,0:T(8,128)(2,1)S(1)}, bf16[960,128]{1,0:T(8,128)(2,1)S(1)}, u32[]{:S(2)}, u32[]{:S(2)}) collective-permute-start(bf16[960,128]{1,0:T(8,128)(2,1)S(1)} %get-tuple-element.29), channel_id=1, source_target_pairs={{32,16},{64,48},{96,80},{128,112},{160,144},{192,176},{224,208},{2... | collective-permute-start | bytes 737288 | tf_op jit(solution)/shard_map/ppermute | solution.py:422
  6.1 1.3 %collective-permute-start.3 = (bf16[960,128]{1,0:T(8,128)(2,1)S(1)}, bf16[960,128]{1,0:T(8,128)(2,1)S(1)}, u32[]{:S(2)}, u32[]{:S(2)}) collective-permute-start(bf16[960,128]{1,0:T(8,128)(2,1)S(1)} %get-tuple-element.30), channel_id=1, source_target_pairs={{32,16},{64,48},{96,80},{128,112},{160,144},{192,176},{224,208},{2... | collective-permute-start | bytes 737288 | tf_op jit(solution)/shard_map/ppermute | solution.py:423
  7.4 0.0 copy-done
  7.4 0.0 copy-start.1
  7.4 0.6 copy-done.1
  8.0 0.1 maximum_bitcast_fusion
  8.1 0.1 copy.6.bias
  8.2 0.1 reshape.6.taps
  8.3 2.5 %shard_map.47 = (f32[2,8,960]{2,1,0:T(8,128)S(1)}, f32[2,8,960]{2,1,0:T(8,128)S(1)}, bf16[2,960,256]{2,1,0:T(8,128)(2,1)S(1)}) custom-call(bf16[2,2,960,128]{3,2,1,0:T(8,128)(2,1)S(1)} %get-tuple-element.24.both), custom_call_target="tpu_custom_call" | custom-call | flops 1000000000 | bytes 1000000 | tf_op jit(solution)/shard_map/pallas_call | solution.py:386
  10.8 0.0 collective-permute-done.both_p
  10.8 3.0 %shard_map.48 = (f32[2,8,960]{2,1,0:T(8,128)S(1)}, f32[2,8,960]{2,1,0:T(8,128)S(1)}, f32[2,8,960]{2,1,0:T(8,128)S(1)}, f32[2,8,480]{2,1,0:T(8,128)S(1)}) custom-call(bf16[2,2,960,128]{3,2,1,0:T(8,128)(2,1)S(1)} %get-tuple-element.24.both, bf16[2,2,960,128]{3,2,1,0:T(8,128)(2,1)S(1)} %collective-permute-done.both_p, f32[2,8,960]{2,1,0:T(8,128)S(1)} %get-tuple-element.25.fwd0, ...), custom_call_target="tpu_custom_call" | custom-call | flops 2000000000 | bytes 2000000 | tf_op jit(solution)/shard_map/pallas_call | solution.py:386
  13.8 10.3 %collective-permute-done.2.first_o.first_o0 = bf16[960,128]{1,0:T(8,128)(2,1)S(1)} collective-permute-done((bf16[960,128]{1,0:T(8,128)(2,1)S(1)}, bf16[960,128]{1,0:T(8,128)(2,1)S(1)}, u32[]{:S(2)}, u32[]{:S(2)}) %collective-permute-start.2) | collective-permute-done | bytes 245792 | tf_op jit(solution)/shard_map/ppermute | solution.py:422
  24.1 1.2 %shard_map.50 = (f32[8,960]{1,0:T(8,128)S(1)}, f32[8,960]{1,0:T(8,128)S(1)}) custom-call(bf16[960,128]{1,0:T(8,128)(2,1)S(1)} %collective-permute-done.2.first_o.first_o0, bf16[2,2,960,128]{3,2,1,0:T(8,128)(2,1)S(1)} %get-tuple-element.24.both, f32[2,8,960]{2,1,0:T(8,128)S(1)} %get-tuple-element.31.bwd0), custom_call_target="tpu_custom_call" | custom-call | flops 500000000 | bytes 500000 | tf_op jit(solution)/shard_map/pallas_call | solution.py:386
  25.3 0.0 collective-permute-done.1.second_o
  25.3 2.4 %shard_map.49 = (f32[2,8,960]{2,1,0:T(8,128)S(1)}, f32[2,8,960]{2,1,0:T(8,128)S(1)}) custom-call(bf16[2,960,128]{2,1,0:T(8,128)(2,1)S(1)} %collective-permute-done.1.second_o, bf16[2,960,256]{2,1,0:T(8,128)(2,1)S(1)} %get-tuple-element.27.fs, f32[2,8,960]{2,1,0:T(8,128)S(1)} %get-tuple-element.32.fwd0, f32[8,48]{1,0:T(8,128)S(1)} %reshape.6.taps, ...), custom_call_target="tpu_custom_call" | custom-call | flops 1000000000 | bytes 1000000 | tf_op jit(solution)/shard_map/pallas_call | solution.py:386
  27.7 0.0 collective-permute-done.3.first_o1
  27.7 62.0 %shard_map.51 = (f32[2,24,480]{2,1,0:T(8,128)S(1)}, f32[2,8,480]{2,1,0:T(8,128)S(1)}, f32[2,4,480]{2,1,0:T(4,128)S(1)}) custom-call(bf16[2,2,960,128]{3,2,1,0:T(8,128)(2,1)S(1)} %get-tuple-element.24.both, bf16[2,2,960,128]{3,2,1,0:T(8,128)(2,1)S(1)} %collective-permute-done.both_p, bf16[2,960,128]{2,1,0:T(8,128)(2,1)S(1)} %collective-permute-done.1.second_o, ...), custom_call_target="tpu_custom_call" | custom-call | flops 500000000 | bytes 500000 | tf_op jit(solution)/shard_map/pallas_call | solution.py:386
  89.7 1.3 %collective-permute-start.5 = (f32[2,24,480]{2,1,0:T(8,128)S(1)}, f32[2,24,480]{2,1,0:T(8,128)S(1)}, u32[]{:S(2)}, u32[]{:S(2)}) collective-permute-start(f32[2,24,480]{2,1,0:T(8,128)S(1)} %get-tuple-element.38.sent), channel_id=1, source_target_pairs={{16,32},{48,64},{80,96},{112,128},{144,160},{176,192},{208,224},{2... | collective-permute-start | bytes 276488 | tf_op jit(solution)/shard_map/ppermute | solution.py:440
  91.0 1.3 %collective-permute-start.4 = (f32[2,8,480]{2,1,0:T(8,128)S(1)}, f32[2,8,480]{2,1,0:T(8,128)S(1)}, u32[]{:S(2)}, u32[]{:S(2)}) collective-permute-start(f32[2,8,480]{2,1,0:T(8,128)S(1)} %get-tuple-element.39), channel_id=1, source_target_pairs={{32,16},{64,48},{96,80},{128,112},{160,144},{192,176},{224,208},{2... | collective-permute-start | bytes 92168 | tf_op jit(solution)/shard_map/ppermute | solution.py:431
  92.3 1.9 %collective-permute-start.6 = (f32[2,4,480]{2,1,0:T(4,128)S(1)}, f32[2,4,480]{2,1,0:T(4,128)S(1)}, u32[]{:S(2)}, u32[]{:S(2)}) collective-permute-start(f32[2,4,480]{2,1,0:T(4,128)S(1)} %get-tuple-element.41), channel_id=1, source_target_pairs={{16,0},{48,32},{80,64},{112,96},{144,128},{176,160},{208,192},{256... | collective-permute-start | bytes 46088 | tf_op jit(solution)/shard_map/ppermute | solution.py:441
  94.2 5.6 %collective-permute-done.4.up = f32[2,8,480]{2,1,0:T(8,128)S(1)} collective-permute-done((f32[2,8,480]{2,1,0:T(8,128)S(1)}, f32[2,8,480]{2,1,0:T(8,128)S(1)}, u32[]{:S(2)}, u32[]{:S(2)}) %collective-permute-start.4) | collective-permute-done | bytes 30752 | tf_op jit(solution)/shard_map/ppermute | solution.py:431
  99.8 0.0 collective-permute-done.5.down
  99.8 0.1 shard_map.52
  100.0 0.7 collective-permute-start.7
  100.6 0.0 collective-permute-done.6.edge_heavy
  100.6 0.0 collective-permute-done.7.edge_light
  100.7 0.9 shard_map.53
  (3 shorter events, 0.0 us)
Async XLA Ops:
  0.0 7.4 %copy-start = (f32[4,4,3,3]{1,0,3,2:T(4,128)S(1)}, f32[4,4,3,3]{1,0,3,2:T(4,128)}, u32[]{:S(2)}) copy-start(f32[4,4,3,3]{1,0,3,2:T(4,128)} %param.6) | copy-start | bytes 1732
  1.5 9.3 %collective-permute-start = (bf16[2,2,960,128]{3,2,1,0:T(8,128)(2,1)S(1)}, bf16[2,2,960,128]{3,2,1,0:T(8,128)(2,1)S(1)}, u32[]{:S(2)}, u32[]{:S(2)}) collective-permute-start(bf16[2,2,960,128]{3,2,1,0:T(8,128)(2,1)S(1)} %get-tuple-element.24.both), channel_id=1, source_target_pairs={{0,16},{16,0},{32,48},{48,32},{64,80},{80,64},{96,112},{112,96},{1... | collective-permute-start | bytes 2949128 | tf_op jit(solution)/shard_map/ppermute | solution.py:424
  3.5 21.9 %collective-permute-start.1 = (bf16[2,960,128]{2,1,0:T(8,128)(2,1)}, bf16[2,960,128]{2,1,0:T(8,128)(2,1)S(1)}, u32[]{:S(2)}, u32[]{:S(2)}) collective-permute-start(bf16[2,960,128]{2,1,0:T(8,128)(2,1)} %second.1), channel_id=1, source_target_pairs={{32,16},{64,48},{96,80},{128,112},{160,144},{192,176},{224,208},{2... | collective-permute-start | bytes 1474568 | tf_op jit(solution)/shard_map/ppermute | solution.py:416
  4.8 19.3 %collective-permute-start.2 = (bf16[960,128]{1,0:T(8,128)(2,1)S(1)}, bf16[960,128]{1,0:T(8,128)(2,1)S(1)}, u32[]{:S(2)}, u32[]{:S(2)}) collective-permute-start(bf16[960,128]{1,0:T(8,128)(2,1)S(1)} %get-tuple-element.29), channel_id=1, source_target_pairs={{32,16},{64,48},{96,80},{128,112},{160,144},{192,176},{224,208},{2... | collective-permute-start | bytes 737288 | tf_op jit(solution)/shard_map/ppermute | solution.py:422
  6.1 21.7 %collective-permute-start.3 = (bf16[960,128]{1,0:T(8,128)(2,1)S(1)}, bf16[960,128]{1,0:T(8,128)(2,1)S(1)}, u32[]{:S(2)}, u32[]{:S(2)}) collective-permute-start(bf16[960,128]{1,0:T(8,128)(2,1)S(1)} %get-tuple-element.30), channel_id=1, source_target_pairs={{32,16},{64,48},{96,80},{128,112},{160,144},{192,176},{224,208},{2... | collective-permute-start | bytes 737288 | tf_op jit(solution)/shard_map/ppermute | solution.py:423
  7.4 0.7 copy-start.1
  89.7 10.2 %collective-permute-start.5 = (f32[2,24,480]{2,1,0:T(8,128)S(1)}, f32[2,24,480]{2,1,0:T(8,128)S(1)}, u32[]{:S(2)}, u32[]{:S(2)}) collective-permute-start(f32[2,24,480]{2,1,0:T(8,128)S(1)} %get-tuple-element.38.sent), channel_id=1, source_target_pairs={{16,32},{48,64},{80,96},{112,128},{144,160},{176,192},{208,224},{2... | collective-permute-start | bytes 276488 | tf_op jit(solution)/shard_map/ppermute | solution.py:440
  91.0 8.8 %collective-permute-start.4 = (f32[2,8,480]{2,1,0:T(8,128)S(1)}, f32[2,8,480]{2,1,0:T(8,128)S(1)}, u32[]{:S(2)}, u32[]{:S(2)}) collective-permute-start(f32[2,8,480]{2,1,0:T(8,128)S(1)} %get-tuple-element.39), channel_id=1, source_target_pairs={{32,16},{64,48},{96,80},{128,112},{160,144},{192,176},{224,208},{2... | collective-permute-start | bytes 92168 | tf_op jit(solution)/shard_map/ppermute | solution.py:431
  92.3 8.3 %collective-permute-start.6 = (f32[2,4,480]{2,1,0:T(4,128)S(1)}, f32[2,4,480]{2,1,0:T(4,128)S(1)}, u32[]{:S(2)}, u32[]{:S(2)}) collective-permute-start(f32[2,4,480]{2,1,0:T(4,128)S(1)} %get-tuple-element.41), channel_id=1, source_target_pairs={{16,0},{48,32},{80,64},{112,96},{144,128},{176,160},{208,192},{256... | collective-permute-start | bytes 46088 | tf_op jit(solution)/shard_map/ppermute | solution.py:441
  100.0 0.7 collective-permute-start.7

commit v6 on v5

--- a/solution.py
+++ b/solution.py
@@ -108,12 +108,13 @@
 
 def load_kernel(first, second, both, first0, first1, sems):
     pairs = [(first.at[f], both.at[0, f]) for f in range(FR)] + [(second.at[f], both.at[1, f]) for f in range(FR)]
-    pairs = [(first.at[0], first0), (first.at[1], first1)] + pairs
     copies = [pltpu.make_async_copy(src, dst, sems.at[k]) for k, (src, dst) in enumerate(pairs)]
     for c in copies:
         c.start()
     for c in copies:
         c.wait()
+    first0[...] = both[0, 0]
+    first1[...] = both[0, 1]
 
 
 def own_kernel(both, fwd, bwd, fs, ss):
@@ -268,10 +269,20 @@
         far_first(0, first_o, both, bwd0, bwd, row, fo, ss, jnp.where(even, -2.0, 2.0))
 
 
-def far_first1_kernel(height, both, both_p, second_o, first_o0, first_o1, bwd0, fwd, col, bwd1, row1,
+def far_first1_kernel(height, both, both_p, second_o, first_o0, first_o1, bwd0, fwd, col, bwd1, row1, part,
                       sent, flows, edge, fo, ss, bwd, row, feats, found, stage, sems):
-    even, heavy, _ = side()
+    even, heavy, present = side()
     far = jnp.where(even, -2.0, 2.0)
+
+    @pl.when(jnp.logical_not(present))
+    def _():
+        for f in range(FR):
+            pieces = []
+            for j in range(2):
+                stat = part[f, 4 * j : 4 * j + 4, :]
+                stat = jnp.where(even, stat[:, W:], stat[:, :W])
+                pieces.extend(finish(stat[1:2], stat[2:3], stat[3:4], jnp.where(even, 1.0, 0.0), height))
+            edge[f] = jnp.concatenate(pieces, axis=0)
 
     @pl.when(heavy)
     def _():
@@ -358,7 +369,8 @@
 def refine_kernel(rows, edge_heavy, edge_light, taps, bias, out):
     even, _, _ = side()
     pos, size = lax.axis_index("blk"), lax.axis_size("blk")
-    from_heavy = takes(jnp.where(even, pos + 1, pos - 1), size)
+    partner = jnp.where(even, pos + 1, pos - 1)
+    from_heavy = takes(partner, size) | (partner == 0) | (partner == size - 1)
     none = jnp.zeros((16, 1), jnp.float32)
     for f in range(FR):
         mine = rows[f]
@@ -408,6 +420,7 @@
     pairs = [(i, i + 1) for i in range(1, size - 1, 2)]
     toward = [(j, i) if heavy[i] else (i, j) for i, j in pairs]
     back = [(j, i) for i, j in toward]
+    early = [heavy[i] or i in (0, size - 1) for i in range(size)]
 
     taps = conv_weight.transpose(0, 3, 2, 1)
     taps = jnp.stack([jnp.pad(taps, ((0, 0), (0, 0), (r, 1 - r), (0, 0))) for r in range(2)])
@@ -417,7 +430,7 @@
     first, second = (pltpu.with_memory_space_constraint(x, pltpu.HBM) for x in (first, second))
     tile = jax.ShapeDtypeStruct((TILE, CH), jnp.bfloat16)
     loaded = jax.ShapeDtypeStruct((2, FR, TILE, CH), jnp.bfloat16)
-    both, first0, first1 = call(load_kernel, (loaded, tile, tile), [pltpu.SemaphoreType.DMA((6,))], 4, 10**6,
+    both, first0, first1 = call(load_kernel, (loaded, tile, tile), [pltpu.SemaphoreType.DMA((4,))], 4, 10**6,
                                 first, second, hbm=(0, 1))
     first_o0 = lax.ppermute(first0, "blk", toward)
     first_o1 = lax.ppermute(first1, "blk", toward)
@@ -435,13 +448,13 @@
     sent, flows, edge = call(functools.partial(far_first1_kernel, height),
                              (f32((FR, 24, W)), f32((FR, 8, W)), f32((FR, 4, W))),
                              [single, single, kept, kept] + spare[:2] + [narrow] + spare[2:], 12, 5 * 10**8,
-                             both, both_p, second_o, first_o0, first_o1, bwd, fwd, col, bwd1, row1,
+                             both, both_p, second_o, first_o0, first_o1, bwd, fwd, col, bwd1, row1, part,
                              far=(1, 2))
     down = lax.ppermute(sent, "blk", back)
-    edge_heavy = lax.ppermute(edge, "blk", [c for c in chip if heavy[c[0]]])
+    edge_heavy = lax.ppermute(edge, "blk", [c for c in chip if early[c[0]]])
     rows, edge = call(functools.partial(flow_kernel, height), (f32((FR, 16, W)), f32((FR, 4, W))), [], 4, 10**6,
                       part, flows, sent, up, down)
-    edge_light = lax.ppermute(edge, "blk", [c for c in chip if not heavy[c[0]]])
+    edge_light = lax.ppermute(edge, "blk", [c for c in chip if not early[c[0]]])
     return call(refine_kernel, f32((FR, 4, 2, W)), [], 4, 10**6, rows, edge_heavy, edge_light, taps, bias)
 
 

time: 102 us -> 102 us (level)
  the two profiles are of different devices: /device:TPU:14 before, /device:TPU:6 now
where the time goes in v6:
time: 102 us; the launch traced here: 101 us
  Pallas kernels  73.5 us (72%)
  waiting for transfers between devices  15.9 us (16%)
  starting transfers between devices  11 us (11%)
    pallas_call x8, Pallas kernels, call(): pl.pallas_call(kernel, out_shape=shapes, in_specs=[home if i in hbm else...  73.5 us
    ppermute x1, waiting for transfers between devices, device_program(): first_o0 = lax.ppermute(first0, 'blk', toward)  10.3 us
    ppermute x1, waiting for transfers between devices, device_program(): up = lax.ppermute(up, 'blk', toward)  5.62 us
  transfers between devices with their start and end apart: 8, of which 2 were waited for; matrix products, arithmetic and copies ran while one was open for 0% of the time, Pallas kernels for 9%

profile of v6, /device:TPU:6, one launch (start us, length us, event | category | flops | bytes accessed | tf_op | source)
XLA Modules:
  0.0 101.5 jit_solution(9309029480565882358)
XLA Ops:
  0.0 0.0 copy-start
  0.0 1.4 %shard_map.46 = (bf16[2,2,960,128]{3,2,1,0:T(8,128)(2,1)S(1)}, bf16[960,128]{1,0:T(8,128)(2,1)S(1)}, bf16[960,128]{1,0:T(8,128)(2,1)S(1)}) custom-call(bf16[2,960,128]{2,1,0:T(8,128)(2,1)} %first.1, bf16[2,960,128]{2,1,0:T(8,128)(2,1)} %second.1), custom_call_target="tpu_custom_call" | custom-call | flops 1000000 | bytes 1000 | tf_op jit(solution)/shard_map/pallas_call | solution.py:398
  1.4 1.9 %collective-permute-start = (bf16[2,2,960,128]{3,2,1,0:T(8,128)(2,1)S(1)}, bf16[2,2,960,128]{3,2,1,0:T(8,128)(2,1)S(1)}, u32[]{:S(2)}, u32[]{:S(2)}) collective-permute-start(bf16[2,2,960,128]{3,2,1,0:T(8,128)(2,1)S(1)} %get-tuple-element.24.both), channel_id=1, source_target_pairs={{0,16},{16,0},{32,48},{48,32},{64,80},{80,64},{96,112},{112,96},{1... | collective-permute-start | bytes 2949128 | tf_op jit(solution)/shard_map/ppermute | solution.py:437
  3.3 1.3 %collective-permute-start.1 = (bf16[2,960,128]{2,1,0:T(8,128)(2,1)}, bf16[2,960,128]{2,1,0:T(8,128)(2,1)S(1)}, u32[]{:S(2)}, u32[]{:S(2)}) collective-permute-start(bf16[2,960,128]{2,1,0:T(8,128)(2,1)} %second.1), channel_id=1, source_target_pairs={{32,16},{64,48},{96,80},{128,112},{160,144},{192,176},{224,208},{2... | collective-permute-start | bytes 1474568 | tf_op jit(solution)/shard_map/ppermute | solution.py:429
  4.6 1.3 %collective-permute-start.2 = (bf16[960,128]{1,0:T(8,128)(2,1)S(1)}, bf16[960,128]{1,0:T(8,128)(2,1)S(1)}, u32[]{:S(2)}, u32[]{:S(2)}) collective-permute-start(bf16[960,128]{1,0:T(8,128)(2,1)S(1)} %get-tuple-element.29), channel_id=1, source_target_pairs={{32,16},{64,48},{96,80},{128,112},{160,144},{192,176},{224,208},{2... | collective-permute-start | bytes 737288 | tf_op jit(solution)/shard_map/ppermute | solution.py:435
  5.9 1.3 %collective-permute-start.3 = (bf16[960,128]{1,0:T(8,128)(2,1)S(1)}, bf16[960,128]{1,0:T(8,128)(2,1)S(1)}, u32[]{:S(2)}, u32[]{:S(2)}) collective-permute-start(bf16[960,128]{1,0:T(8,128)(2,1)S(1)} %get-tuple-element.30), channel_id=1, source_target_pairs={{32,16},{64,48},{96,80},{128,112},{160,144},{192,176},{224,208},{2... | collective-permute-start | bytes 737288 | tf_op jit(solution)/shard_map/ppermute | solution.py:436
  7.2 0.0 copy-done
  7.2 0.0 copy-start.1
  7.3 0.6 copy-done.1
  7.9 0.1 maximum_bitcast_fusion
  8.0 0.1 copy.6.bias
  8.1 0.1 reshape.6.taps
  8.2 2.5 %shard_map.47 = (f32[2,8,960]{2,1,0:T(8,128)S(1)}, f32[2,8,960]{2,1,0:T(8,128)S(1)}, bf16[2,960,256]{2,1,0:T(8,128)(2,1)S(1)}) custom-call(bf16[2,2,960,128]{3,2,1,0:T(8,128)(2,1)S(1)} %get-tuple-element.24.both), custom_call_target="tpu_custom_call" | custom-call | flops 1000000000 | bytes 1000000 | tf_op jit(solution)/shard_map/pallas_call | solution.py:398
  10.7 0.0 collective-permute-done.both_p
  10.7 3.0 %shard_map.48 = (f32[2,8,960]{2,1,0:T(8,128)S(1)}, f32[2,8,960]{2,1,0:T(8,128)S(1)}, f32[2,8,960]{2,1,0:T(8,128)S(1)}, f32[2,8,480]{2,1,0:T(8,128)S(1)}) custom-call(bf16[2,2,960,128]{3,2,1,0:T(8,128)(2,1)S(1)} %get-tuple-element.24.both, bf16[2,2,960,128]{3,2,1,0:T(8,128)(2,1)S(1)} %collective-permute-done.both_p, f32[2,8,960]{2,1,0:T(8,128)S(1)} %get-tuple-element.25.fwd0, ...), custom_call_target="tpu_custom_call" | custom-call | flops 2000000000 | bytes 2000000 | tf_op jit(solution)/shard_map/pallas_call | solution.py:398
  13.7 10.3 %collective-permute-done.2.first_o.first_o0 = bf16[960,128]{1,0:T(8,128)(2,1)S(1)} collective-permute-done((bf16[960,128]{1,0:T(8,128)(2,1)S(1)}, bf16[960,128]{1,0:T(8,128)(2,1)S(1)}, u32[]{:S(2)}, u32[]{:S(2)}) %collective-permute-start.2) | collective-permute-done | bytes 245792 | tf_op jit(solution)/shard_map/ppermute | solution.py:435
  23.9 1.2 %shard_map.50 = (f32[8,960]{1,0:T(8,128)S(1)}, f32[8,960]{1,0:T(8,128)S(1)}) custom-call(bf16[960,128]{1,0:T(8,128)(2,1)S(1)} %collective-permute-done.2.first_o.first_o0, bf16[2,2,960,128]{3,2,1,0:T(8,128)(2,1)S(1)} %get-tuple-element.24.both, f32[2,8,960]{2,1,0:T(8,128)S(1)} %get-tuple-element.31.bwd0), custom_call_target="tpu_custom_call" | custom-call | flops 500000000 | bytes 500000 | tf_op jit(solution)/shard_map/pallas_call | solution.py:398
  25.2 0.0 collective-permute-done.1.second_o
  25.2 2.4 %shard_map.49 = (f32[2,8,960]{2,1,0:T(8,128)S(1)}, f32[2,8,960]{2,1,0:T(8,128)S(1)}) custom-call(bf16[2,960,128]{2,1,0:T(8,128)(2,1)S(1)} %collective-permute-done.1.second_o, bf16[2,960,256]{2,1,0:T(8,128)(2,1)S(1)} %get-tuple-element.27.fs, f32[2,8,960]{2,1,0:T(8,128)S(1)} %get-tuple-element.32.fwd0, f32[8,48]{1,0:T(8,128)S(1)} %reshape.6.taps, ...), custom_call_target="tpu_custom_call" | custom-call | flops 1000000000 | bytes 1000000 | tf_op jit(solution)/shard_map/pallas_call | solution.py:398
  27.6 0.0 collective-permute-done.3.first_o1
  27.6 62.0 %shard_map.51 = (f32[2,24,480]{2,1,0:T(8,128)S(1)}, f32[2,8,480]{2,1,0:T(8,128)S(1)}, f32[2,4,480]{2,1,0:T(4,128)S(1)}) custom-call(bf16[2,2,960,128]{3,2,1,0:T(8,128)(2,1)S(1)} %get-tuple-element.24.both, bf16[2,2,960,128]{3,2,1,0:T(8,128)(2,1)S(1)} %collective-permute-done.both_p, bf16[2,960,128]{2,1,0:T(8,128)(2,1)S(1)} %collective-permute-done.1.second_o, ...), custom_call_target="tpu_custom_call" | custom-call | flops 500000000 | bytes 500000 | tf_op jit(solution)/shard_map/pallas_call | solution.py:398
  89.6 1.3 %collective-permute-start.5 = (f32[2,24,480]{2,1,0:T(8,128)S(1)}, f32[2,24,480]{2,1,0:T(8,128)S(1)}, u32[]{:S(2)}, u32[]{:S(2)}) collective-permute-start(f32[2,24,480]{2,1,0:T(8,128)S(1)} %get-tuple-element.38.sent), channel_id=1, source_target_pairs={{16,32},{48,64},{80,96},{112,128},{144,160},{176,192},{208,224},{2... | collective-permute-start | bytes 276488 | tf_op jit(solution)/shard_map/ppermute | solution.py:453
  90.9 1.3 %collective-permute-start.4 = (f32[2,8,480]{2,1,0:T(8,128)S(1)}, f32[2,8,480]{2,1,0:T(8,128)S(1)}, u32[]{:S(2)}, u32[]{:S(2)}) collective-permute-start(f32[2,8,480]{2,1,0:T(8,128)S(1)} %get-tuple-element.39), channel_id=1, source_target_pairs={{32,16},{64,48},{96,80},{128,112},{160,144},{192,176},{224,208},{2... | collective-permute-start | bytes 92168 | tf_op jit(solution)/shard_map/ppermute | solution.py:444
  92.2 1.9 %collective-permute-start.6 = (f32[2,4,480]{2,1,0:T(4,128)S(1)}, f32[2,4,480]{2,1,0:T(4,128)S(1)}, u32[]{:S(2)}, u32[]{:S(2)}) collective-permute-start(f32[2,4,480]{2,1,0:T(4,128)S(1)} %get-tuple-element.41), channel_id=1, source_target_pairs={{0,16},{16,0},{48,32},{80,64},{112,96},{144,128},{176,160},{208,19... | collective-permute-start | bytes 46088 | tf_op jit(solution)/shard_map/ppermute | solution.py:454
  94.1 5.6 %collective-permute-done.4.up = f32[2,8,480]{2,1,0:T(8,128)S(1)} collective-permute-done((f32[2,8,480]{2,1,0:T(8,128)S(1)}, f32[2,8,480]{2,1,0:T(8,128)S(1)}, u32[]{:S(2)}, u32[]{:S(2)}) %collective-permute-start.4) | collective-permute-done | bytes 30752 | tf_op jit(solution)/shard_map/ppermute | solution.py:444
  99.7 0.0 collective-permute-done.5.down
  99.7 0.1 shard_map.52
  99.8 0.7 collective-permute-start.7
  100.5 0.0 collective-permute-done.6.edge_heavy
  100.5 0.0 collective-permute-done.7.edge_light
  100.5 0.9 shard_map.53
  (3 shorter events, 0.0 us)
Async XLA Ops:
  0.0 7.2 %copy-start = (f32[4,4,3,3]{1,0,3,2:T(4,128)S(1)}, f32[4,4,3,3]{1,0,3,2:T(4,128)}, u32[]{:S(2)}) copy-start(f32[4,4,3,3]{1,0,3,2:T(4,128)} %param.6) | copy-start | bytes 1732
  1.4 9.3 %collective-permute-start = (bf16[2,2,960,128]{3,2,1,0:T(8,128)(2,1)S(1)}, bf16[2,2,960,128]{3,2,1,0:T(8,128)(2,1)S(1)}, u32[]{:S(2)}, u32[]{:S(2)}) collective-permute-start(bf16[2,2,960,128]{3,2,1,0:T(8,128)(2,1)S(1)} %get-tuple-element.24.both), channel_id=1, source_target_pairs={{0,16},{16,0},{32,48},{48,32},{64,80},{80,64},{96,112},{112,96},{1... | collective-permute-start | bytes 2949128 | tf_op jit(solution)/shard_map/ppermute | solution.py:437
  3.3 21.9 %collective-permute-start.1 = (bf16[2,960,128]{2,1,0:T(8,128)(2,1)}, bf16[2,960,128]{2,1,0:T(8,128)(2,1)S(1)}, u32[]{:S(2)}, u32[]{:S(2)}) collective-permute-start(bf16[2,960,128]{2,1,0:T(8,128)(2,1)} %second.1), channel_id=1, source_target_pairs={{32,16},{64,48},{96,80},{128,112},{160,144},{192,176},{224,208},{2... | collective-permute-start | bytes 1474568 | tf_op jit(solution)/shard_map/ppermute | solution.py:429
  4.6 19.3 %collective-permute-start.2 = (bf16[960,128]{1,0:T(8,128)(2,1)S(1)}, bf16[960,128]{1,0:T(8,128)(2,1)S(1)}, u32[]{:S(2)}, u32[]{:S(2)}) collective-permute-start(bf16[960,128]{1,0:T(8,128)(2,1)S(1)} %get-tuple-element.29), channel_id=1, source_target_pairs={{32,16},{64,48},{96,80},{128,112},{160,144},{192,176},{224,208},{2... | collective-permute-start | bytes 737288 | tf_op jit(solution)/shard_map/ppermute | solution.py:435
  5.9 21.7 %collective-permute-start.3 = (bf16[960,128]{1,0:T(8,128)(2,1)S(1)}, bf16[960,128]{1,0:T(8,128)(2,1)S(1)}, u32[]{:S(2)}, u32[]{:S(2)}) collective-permute-start(bf16[960,128]{1,0:T(8,128)(2,1)S(1)} %get-tuple-element.30), channel_id=1, source_target_pairs={{32,16},{64,48},{96,80},{128,112},{160,144},{192,176},{224,208},{2... | collective-permute-start | bytes 737288 | tf_op jit(solution)/shard_map/ppermute | solution.py:436
  7.2 0.7 copy-start.1
  89.6 10.2 %collective-permute-start.5 = (f32[2,24,480]{2,1,0:T(8,128)S(1)}, f32[2,24,480]{2,1,0:T(8,128)S(1)}, u32[]{:S(2)}, u32[]{:S(2)}) collective-permute-start(f32[2,24,480]{2,1,0:T(8,128)S(1)} %get-tuple-element.38.sent), channel_id=1, source_target_pairs={{16,32},{48,64},{80,96},{112,128},{144,160},{176,192},{208,224},{2... | collective-permute-start | bytes 276488 | tf_op jit(solution)/shard_map/ppermute | solution.py:453
  90.9 8.8 %collective-permute-start.4 = (f32[2,8,480]{2,1,0:T(8,128)S(1)}, f32[2,8,480]{2,1,0:T(8,128)S(1)}, u32[]{:S(2)}, u32[]{:S(2)}) collective-permute-start(f32[2,8,480]{2,1,0:T(8,128)S(1)} %get-tuple-element.39), channel_id=1, source_target_pairs={{32,16},{64,48},{96,80},{128,112},{160,144},{192,176},{224,208},{2... | collective-permute-start | bytes 92168 | tf_op jit(solution)/shard_map/ppermute | solution.py:444
  92.2 8.3 %collective-permute-start.6 = (f32[2,4,480]{2,1,0:T(4,128)S(1)}, f32[2,4,480]{2,1,0:T(4,128)S(1)}, u32[]{:S(2)}, u32[]{:S(2)}) collective-permute-start(f32[2,4,480]{2,1,0:T(4,128)S(1)} %get-tuple-element.41), channel_id=1, source_target_pairs={{0,16},{16,0},{48,32},{80,64},{112,96},{144,128},{176,160},{208,19... | collective-permute-start | bytes 46088 | tf_op jit(solution)/shard_map/ppermute | solution.py:454
  99.8 0.7 collective-permute-start.7

commit v7 on v6

--- a/solution.py
+++ b/solution.py
@@ -106,15 +106,13 @@
     return (mom_x / total - col) * (2.0 / W), (mom_y / total - row) * (2.0 / height)
 
 
-def load_kernel(first, second, both, first0, first1, sems):
+def load_kernel(first, second, both, sems):
     pairs = [(first.at[f], both.at[0, f]) for f in range(FR)] + [(second.at[f], both.at[1, f]) for f in range(FR)]
     copies = [pltpu.make_async_copy(src, dst, sems.at[k]) for k, (src, dst) in enumerate(pairs)]
     for c in copies:
         c.start()
     for c in copies:
         c.wait()
-    first0[...] = both[0, 0]
-    first1[...] = both[0, 1]
 
 
 def own_kernel(both, fwd, bwd, fs, ss):
@@ -251,26 +249,8 @@
         lax.fori_loop(0, FR, frame, 0)
 
 
-def far_first(f, first_o, both, bwd0, bwd, row, fo, ss, far):
-    split_into(fo, 0, first_o[...])
-    twice_into(ss, 0, both[1, f])
-
-    def down(n0, w, part):
-        bwd[:, n0 : n0 + w] = bwd0[f, :, n0 : n0 + w] + shift_y(part, far)
-
-    row[...] = sums(fo, ss, 0, down, moments())
-
-
-def far_first0_kernel(first_o, both, bwd0, bwd, row, fo, ss):
-    even, heavy, _ = side()
-
-    @pl.when(heavy)
-    def _():
-        far_first(0, first_o, both, bwd0, bwd, row, fo, ss, jnp.where(even, -2.0, 2.0))
-
-
-def far_first1_kernel(height, both, both_p, second_o, first_o0, first_o1, bwd0, fwd, col, bwd1, row1, part,
-                      sent, flows, edge, fo, ss, bwd, row, feats, found, stage, sems):
+def far_first_kernel(height, both, both_p, second_o, first_o, bwd0, fwd, col, part,
+                     sent, flows, edge, fo, ss, bwd, row, feats, found, sems):
     even, heavy, present = side()
     far = jnp.where(even, -2.0, 2.0)
 
@@ -286,23 +266,26 @@
 
     @pl.when(heavy)
     def _():
-        bwd[0] = bwd1[...]
-        row[0] = row1[...]
-        far_first(1, first_o1, both, bwd0, bwd.at[1], row.at[1], fo, ss, far)
+        mom = moments()
+
+        def frame(f, _):
+            split_into(fo, f, first_o[f])
+            twice_into(ss, f, both[1, f])
+
+            def down(n0, w, part):
+                bwd[f, :, n0 : n0 + w] = bwd0[f, :, n0 : n0 + w] + shift_y(part, far)
+
+            row[f] = sums(fo, ss, f, down, mom)
+            return 0
+
+        lax.fori_loop(0, FR, frame, 0)
         for f in range(FR):
             for j, stat in enumerate((fwd, bwd, col, row)):
                 found[f, j, 0:4, :] = plain(stat[f])
 
         @pl.when(jnp.logical_not(inside(fwd) & inside(bwd) & inside(col) & inside(row)))
         def _():
-            copies = [
-                pltpu.make_async_copy(src, stage.at[f], sems.at[f]) for f, src in enumerate((first_o0, first_o1))
-            ]
-            for c in copies:
-                c.start()
-            for c in copies:
-                c.wait()
-            sources = {**tiles_of(both, both_p), 2: second_o, 5: stage}
+            sources = {**tiles_of(both, both_p), 2: second_o, 5: first_o}
             exact(sources, feats, found, sems, 4, 3, -far, far)
 
         for f in range(FR):
@@ -411,7 +394,6 @@
     height = 2 * size
     f32 = functools.partial(jax.ShapeDtypeStruct, dtype=jnp.float32)
     wide = pltpu.VMEM((FR, TILE, 2 * CH), jnp.bfloat16)
-    narrow = pltpu.VMEM((FR, TILE, CH), jnp.bfloat16)
     kept = pltpu.VMEM((FR, 8, TILE), jnp.float32)
     spare = [pltpu.VMEM((6, TILE, CH), jnp.bfloat16), pltpu.VMEM((FR, 4, 8, TILE), jnp.float32)]
     spare.append(pltpu.SemaphoreType.DMA((6,)))
@@ -427,15 +409,12 @@
     taps = taps.reshape(8, 48)
     bias = jnp.concatenate([conv_bias, conv_bias]).reshape(8, 1)
     second_o = lax.ppermute(second, "blk", toward)
+    first_o = lax.ppermute(first, "blk", toward)
     first, second = (pltpu.with_memory_space_constraint(x, pltpu.HBM) for x in (first, second))
-    tile = jax.ShapeDtypeStruct((TILE, CH), jnp.bfloat16)
     loaded = jax.ShapeDtypeStruct((2, FR, TILE, CH), jnp.bfloat16)
-    both, first0, first1 = call(load_kernel, (loaded, tile, tile), [pltpu.SemaphoreType.DMA((4,))], 4, 10**6,
-                                first, second, hbm=(0, 1))
-    first_o0 = lax.ppermute(first0, "blk", toward)
-    first_o1 = lax.ppermute(first1, "blk", toward)
+    both = call(load_kernel, loaded, [pltpu.SemaphoreType.DMA((4,))], 4, 10**6, first, second, hbm=(0, 1))
     both_p = lax.ppermute(both, "blk", chip)
-    stats, frame = f32((FR, 8, TILE)), f32((8, TILE))
+    stats = f32((FR, 8, TILE))
     doubled = jax.ShapeDtypeStruct((FR, TILE, 2 * CH), jnp.bfloat16)
     own_out = (stats, stats, doubled)
     fwd, bwd, fs = call(own_kernel, own_out, [wide], 8, 10**9, both)
@@ -443,13 +422,10 @@
                               2 * 10**9, both, both_p, fwd, bwd, fs)
     up = lax.ppermute(up, "blk", toward)
     fwd, col = call(far_second_kernel, (stats, stats), [wide], 8, 10**9, second_o, fs, fwd, taps, bias)
-    single = pltpu.VMEM((1, TILE, 2 * CH), jnp.bfloat16)
-    bwd1, row1 = call(far_first0_kernel, (frame, frame), [single] * 2, 8, 5 * 10**8, first_o0, both, bwd)
-    sent, flows, edge = call(functools.partial(far_first1_kernel, height),
+    sent, flows, edge = call(functools.partial(far_first_kernel, height),
                              (f32((FR, 24, W)), f32((FR, 8, W)), f32((FR, 4, W))),
-                             [single, single, kept, kept] + spare[:2] + [narrow] + spare[2:], 12, 5 * 10**8,
-                             both, both_p, second_o, first_o0, first_o1, bwd, fwd, col, bwd1, row1, part,
-                             far=(1, 2))
+                             [wide, wide, kept, kept] + spare, 14, 10**9,
+                             both, both_p, second_o, first_o, bwd, fwd, col, part, far=(1, 2))
     down = lax.ppermute(sent, "blk", back)
     edge_heavy = lax.ppermute(edge, "blk", [c for c in chip if early[c[0]]])
     rows, edge = call(functools.partial(flow_kernel, height), (f32((FR, 16, W)), f32((FR, 4, W))), [], 4, 10**6,

time: 102 us -> 101 us (level)
  the two profiles are of different devices: /device:TPU:6 before, /device:TPU:46 now
where the time goes in v7:
time: 101 us
  Pallas kernels  72.9 us (72%)
  waiting for transfers between devices  17.2 us (17%)
  starting transfers between devices  9.67 us (10%)
    pallas_call x7, Pallas kernels, call(): pl.pallas_call(kernel, out_shape=shapes, in_specs=[home if i in hbm else...  72.9 us
    ppermute x1, waiting for transfers between devices, device_program(): second_o = lax.ppermute(second, 'blk', toward)  8.75 us
    ppermute x1, waiting for transfers between devices, device_program(): up = lax.ppermute(up, 'blk', toward)  5.62 us
    ppermute x1, waiting for transfers between devices, device_program(): first_o = lax.ppermute(first, 'blk', toward)  2.86 us
  transfers between devices with their start and end apart: 7, of which 3 were waited for; matrix products, arithmetic and copies ran while one was open for 0% of the time, Pallas kernels for 8%

profile of v7, /device:TPU:46, one launch (start us, length us, event | category | flops | bytes accessed | tf_op | source)
XLA Modules:
  0.0 100.9 jit_solution(15557189571746135556)
XLA Ops:
  0.0 0.0 copy-start
  0.0 0.0 copy-start.1
  0.0 1.4 %shard_map.46.both = bf16[2,2,960,128]{3,2,1,0:T(8,128)(2,1)S(1)} custom-call(bf16[2,960,128]{2,1,0:T(8,128)(2,1)} %first.1, bf16[2,960,128]{2,1,0:T(8,128)(2,1)} %second.1), custom_call_target="tpu_custom_call" | custom-call | flops 1000000 | bytes 1000 | tf_op jit(solution)/shard_map/pallas_call | solution.py:381
  1.4 1.9 %collective-permute-start = (bf16[2,2,960,128]{3,2,1,0:T(8,128)(2,1)S(1)}, bf16[2,2,960,128]{3,2,1,0:T(8,128)(2,1)S(1)}, u32[]{:S(2)}, u32[]{:S(2)}) collective-permute-start(bf16[2,2,960,128]{3,2,1,0:T(8,128)(2,1)S(1)} %shard_map.46.both), channel_id=1, source_target_pairs={{0,16},{16,0},{32,48},{48,32},{64,80},{80,64},{96,112},{112,96},{1... | collective-permute-start | bytes 2949128 | tf_op jit(solution)/shard_map/ppermute | solution.py:416
  3.3 0.0 copy-done
  3.3 1.3 %collective-permute-start.1 = (bf16[2,960,128]{2,1,0:T(8,128)(2,1)S(1)}, bf16[2,960,128]{2,1,0:T(8,128)(2,1)S(1)}, u32[]{:S(2)}, u32[]{:S(2)}) collective-permute-start(bf16[2,960,128]{2,1,0:T(8,128)(2,1)S(1)} %copy-done), channel_id=1, source_target_pairs={{32,16},{64,48},{96,80},{128,112},{160,144},{192,176},{224,208},{2... | collective-permute-start | bytes 1474568 | tf_op jit(solution)/shard_map/ppermute | solution.py:411
  4.6 1.3 %collective-permute-start.2 = (bf16[2,960,128]{2,1,0:T(8,128)(2,1)}, bf16[2,960,128]{2,1,0:T(8,128)(2,1)S(1)}, u32[]{:S(2)}, u32[]{:S(2)}) collective-permute-start(bf16[2,960,128]{2,1,0:T(8,128)(2,1)} %first.1), channel_id=1, source_target_pairs={{32,16},{64,48},{96,80},{128,112},{160,144},{192,176},{224,208},{2... | collective-permute-start | bytes 1474568 | tf_op jit(solution)/shard_map/ppermute | solution.py:412
  5.9 0.0 copy-done.1
  6.0 0.0 copy-start.2
  6.0 0.1 reshape.6.taps
  6.1 0.6 copy-done.2
  6.7 0.1 maximum_bitcast_fusion
  6.7 0.1 copy.6.bias
  6.8 2.5 %shard_map.47 = (f32[2,8,960]{2,1,0:T(8,128)S(1)}, f32[2,8,960]{2,1,0:T(8,128)S(1)}, bf16[2,960,256]{2,1,0:T(8,128)(2,1)S(1)}) custom-call(bf16[2,2,960,128]{3,2,1,0:T(8,128)(2,1)S(1)} %shard_map.46.both), custom_call_target="tpu_custom_call" | custom-call | flops 1000000000 | bytes 1000000 | tf_op jit(solution)/shard_map/pallas_call | solution.py:381
  9.3 0.0 collective-permute-done.both_p
  9.3 3.0 %shard_map.48 = (f32[2,8,960]{2,1,0:T(8,128)S(1)}, f32[2,8,960]{2,1,0:T(8,128)S(1)}, f32[2,8,960]{2,1,0:T(8,128)S(1)}, f32[2,8,480]{2,1,0:T(8,128)S(1)}) custom-call(bf16[2,2,960,128]{3,2,1,0:T(8,128)(2,1)S(1)} %shard_map.46.both, bf16[2,2,960,128]{3,2,1,0:T(8,128)(2,1)S(1)} %collective-permute-done.both_p, f32[2,8,960]{2,1,0:T(8,128)S(1)} %get-tuple-element.19.fwd0, ...), custom_call_target="tpu_custom_call" | custom-call | flops 2000000000 | bytes 2000000 | tf_op jit(solution)/shard_map/pallas_call | solution.py:381
  12.4 8.8 %collective-permute-done.1.second_o = bf16[2,960,128]{2,1,0:T(8,128)(2,1)S(1)} collective-permute-done((bf16[2,960,128]{2,1,0:T(8,128)(2,1)S(1)}, bf16[2,960,128]{2,1,0:T(8,128)(2,1)S(1)}, u32[]{:S(2)}, u32[]{:S(2)}) %collective-permute-start.1) | collective-permute-done | bytes 491552 | tf_op jit(solution)/shard_map/ppermute | solution.py:411
  21.1 2.4 %shard_map.49 = (f32[2,8,960]{2,1,0:T(8,128)S(1)}, f32[2,8,960]{2,1,0:T(8,128)S(1)}) custom-call(bf16[2,960,128]{2,1,0:T(8,128)(2,1)S(1)} %collective-permute-done.1.second_o, bf16[2,960,256]{2,1,0:T(8,128)(2,1)S(1)} %get-tuple-element.21.fs, f32[2,8,960]{2,1,0:T(8,128)S(1)} %get-tuple-element.24.fwd0, f32[8,48]{1,0:T(8,128)S(1)} %reshape.6.taps, ...), custom_call_target="tpu_custom_call" | custom-call | flops 1000000000 | bytes 1000000 | tf_op jit(solution)/shard_map/pallas_call | solution.py:381
  23.5 2.9 %collective-permute-done.2.first_o = bf16[2,960,128]{2,1,0:T(8,128)(2,1)S(1)} collective-permute-done((bf16[2,960,128]{2,1,0:T(8,128)(2,1)}, bf16[2,960,128]{2,1,0:T(8,128)(2,1)S(1)}, u32[]{:S(2)}, u32[]{:S(2)}) %collective-permute-start.2) | collective-permute-done | bytes 491552 | tf_op jit(solution)/shard_map/ppermute | solution.py:412
  26.4 62.6 %shard_map.50 = (f32[2,24,480]{2,1,0:T(8,128)S(1)}, f32[2,8,480]{2,1,0:T(8,128)S(1)}, f32[2,4,480]{2,1,0:T(4,128)S(1)}) custom-call(bf16[2,2,960,128]{3,2,1,0:T(8,128)(2,1)S(1)} %shard_map.46.both, bf16[2,2,960,128]{3,2,1,0:T(8,128)(2,1)S(1)} %collective-permute-done.both_p, bf16[2,960,128]{2,1,0:T(8,128)(2,1)S(1)} %collective-permute-done.1.second_o, ...), custom_call_target="tpu_custom_call" | custom-call | flops 1000000000 | bytes 1000000 | tf_op jit(solution)/shard_map/pallas_call | solution.py:381
  89.0 1.3 %collective-permute-start.4 = (f32[2,24,480]{2,1,0:T(8,128)S(1)}, f32[2,24,480]{2,1,0:T(8,128)S(1)}, u32[]{:S(2)}, u32[]{:S(2)}) collective-permute-start(f32[2,24,480]{2,1,0:T(8,128)S(1)} %get-tuple-element.28.sent), channel_id=1, source_target_pairs={{16,32},{48,64},{80,96},{112,128},{144,160},{176,192},{208,224},{2... | collective-permute-start | bytes 276488 | tf_op jit(solution)/shard_map/ppermute | solution.py:429
  90.3 1.3 %collective-permute-start.3 = (f32[2,8,480]{2,1,0:T(8,128)S(1)}, f32[2,8,480]{2,1,0:T(8,128)S(1)}, u32[]{:S(2)}, u32[]{:S(2)}) collective-permute-start(f32[2,8,480]{2,1,0:T(8,128)S(1)} %get-tuple-element.29), channel_id=1, source_target_pairs={{32,16},{64,48},{96,80},{128,112},{160,144},{192,176},{224,208},{2... | collective-permute-start | bytes 92168 | tf_op jit(solution)/shard_map/ppermute | solution.py:423
  91.6 1.9 %collective-permute-start.5 = (f32[2,4,480]{2,1,0:T(4,128)S(1)}, f32[2,4,480]{2,1,0:T(4,128)S(1)}, u32[]{:S(2)}, u32[]{:S(2)}) collective-permute-start(f32[2,4,480]{2,1,0:T(4,128)S(1)} %get-tuple-element.31), channel_id=1, source_target_pairs={{0,16},{16,0},{48,32},{80,64},{112,96},{144,128},{176,160},{208,19... | collective-permute-start | bytes 46088 | tf_op jit(solution)/shard_map/ppermute | solution.py:430
  93.5 5.6 %collective-permute-done.3.up = f32[2,8,480]{2,1,0:T(8,128)S(1)} collective-permute-done((f32[2,8,480]{2,1,0:T(8,128)S(1)}, f32[2,8,480]{2,1,0:T(8,128)S(1)}, u32[]{:S(2)}, u32[]{:S(2)}) %collective-permute-start.3) | collective-permute-done | bytes 30752 | tf_op jit(solution)/shard_map/ppermute | solution.py:423
  99.1 0.0 collective-permute-done.4.down
  99.1 0.1 shard_map.51
  99.2 0.7 collective-permute-start.6
  99.9 0.0 collective-permute-done.5.edge_heavy
  99.9 0.0 collective-permute-done.6.edge_light
  99.9 0.9 shard_map.52
  (3 shorter events, 0.0 us)
Async XLA Ops:
  0.0 3.3 %copy-start = (bf16[2,960,128]{2,1,0:T(8,128)(2,1)S(1)}, bf16[2,960,128]{2,1,0:T(8,128)(2,1)}, u32[]{:S(2)}) copy-start(bf16[2,960,128]{2,1,0:T(8,128)(2,1)} %second.1) | copy-start | bytes 1474564
  0.0 5.9 %copy-start.1 = (f32[4,4,3,3]{1,0,3,2:T(4,128)S(1)}, f32[4,4,3,3]{1,0,3,2:T(4,128)}, u32[]{:S(2)}) copy-start(f32[4,4,3,3]{1,0,3,2:T(4,128)} %param.6) | copy-start | bytes 1732
  1.4 7.9 %collective-permute-start = (bf16[2,2,960,128]{3,2,1,0:T(8,128)(2,1)S(1)}, bf16[2,2,960,128]{3,2,1,0:T(8,128)(2,1)S(1)}, u32[]{:S(2)}, u32[]{:S(2)}) collective-permute-start(bf16[2,2,960,128]{3,2,1,0:T(8,128)(2,1)S(1)} %shard_map.46.both), channel_id=1, source_target_pairs={{0,16},{16,0},{32,48},{48,32},{64,80},{80,64},{96,112},{112,96},{1... | collective-permute-start | bytes 2949128 | tf_op jit(solution)/shard_map/ppermute | solution.py:416
  3.3 17.8 %collective-permute-start.1 = (bf16[2,960,128]{2,1,0:T(8,128)(2,1)S(1)}, bf16[2,960,128]{2,1,0:T(8,128)(2,1)S(1)}, u32[]{:S(2)}, u32[]{:S(2)}) collective-permute-start(bf16[2,960,128]{2,1,0:T(8,128)(2,1)S(1)} %copy-done), channel_id=1, source_target_pairs={{32,16},{64,48},{96,80},{128,112},{160,144},{192,176},{224,208},{2... | collective-permute-start | bytes 1474568 | tf_op jit(solution)/shard_map/ppermute | solution.py:411
  4.6 21.7 %collective-permute-start.2 = (bf16[2,960,128]{2,1,0:T(8,128)(2,1)}, bf16[2,960,128]{2,1,0:T(8,128)(2,1)S(1)}, u32[]{:S(2)}, u32[]{:S(2)}) collective-permute-start(bf16[2,960,128]{2,1,0:T(8,128)(2,1)} %first.1), channel_id=1, source_target_pairs={{32,16},{64,48},{96,80},{128,112},{160,144},{192,176},{224,208},{2... | collective-permute-start | bytes 1474568 | tf_op jit(solution)/shard_map/ppermute | solution.py:412
  6.0 0.7 copy-start.2
  89.0 10.2 %collective-permute-start.4 = (f32[2,24,480]{2,1,0:T(8,128)S(1)}, f32[2,24,480]{2,1,0:T(8,128)S(1)}, u32[]{:S(2)}, u32[]{:S(2)}) collective-permute-start(f32[2,24,480]{2,1,0:T(8,128)S(1)} %get-tuple-element.28.sent), channel_id=1, source_target_pairs={{16,32},{48,64},{80,96},{112,128},{144,160},{176,192},{208,224},{2... | collective-permute-start | bytes 276488 | tf_op jit(solution)/shard_map/ppermute | solution.py:429
  90.3 8.8 %collective-permute-start.3 = (f32[2,8,480]{2,1,0:T(8,128)S(1)}, f32[2,8,480]{2,1,0:T(8,128)S(1)}, u32[]{:S(2)}, u32[]{:S(2)}) collective-permute-start(f32[2,8,480]{2,1,0:T(8,128)S(1)} %get-tuple-element.29), channel_id=1, source_target_pairs={{32,16},{64,48},{96,80},{128,112},{160,144},{192,176},{224,208},{2... | collective-permute-start | bytes 92168 | tf_op jit(solution)/shard_map/ppermute | solution.py:423
  91.6 8.3 %collective-permute-start.5 = (f32[2,4,480]{2,1,0:T(4,128)S(1)}, f32[2,4,480]{2,1,0:T(4,128)S(1)}, u32[]{:S(2)}, u32[]{:S(2)}) collective-permute-start(f32[2,4,480]{2,1,0:T(4,128)S(1)} %get-tuple-element.31), channel_id=1, source_target_pairs={{0,16},{16,0},{48,32},{80,64},{112,96},{144,128},{176,160},{208,19... | collective-permute-start | bytes 46088 | tf_op jit(solution)/shard_map/ppermute | solution.py:430
  99.2 0.7 collective-permute-start.6
